TPU v7x, 32 devices: a whole 2x2x4 slice. The times are simulated.
32 devices in a mesh: group: 4 (over z), depth: 2 (over x), image: 4 (over y, core).
Axes of the slice: x: 2, y: 2, z: 4, core: 2. Of those that a mesh axis runs over, the one named last changes fastest.
Arguments:
- density: float32 [16, 192, 512], P('depth', 'group', 'image'), may hold values from 0.5 to 1.5
- velocity: float32 [3, 16, 192, 512], P(None, 'depth', 'group', 'image'), may hold values from -1.2 to 1.2
- pressure: float32 [16, 192, 512], P('depth', 'group', 'image'), may hold values from 0.5 to 1.5
- palette: float32 [4, 256], replicated, may hold values from 0.2 to 2
- palette_index: int32 [8, 256], replicated, may hold values from 0 to 255
Outputs:
- fluid_state: float32 [5, 16, 192, 512], P(None, 'depth', 'group', 'image')
- picture: float32 [8, 3, 192, 512], P('depth', None, 'group', 'image')
All inputs are finite; a program needn't handle non-finite values.
Results may differ from a plain program's by a relative error of at most 0.0003.
Values sent between devices are 32-bit elements; how exact they have to be, the bound alone decides.
No kernel may reach another device: no remote copies, remote signals or barrier semaphores. Data moves between devices by JAX's collectives and lax.ppermute only.
A program may use at most 128 MiB of HBM per device.

v0:
```python
import jax
import jax.numpy as jnp
from jax import lax
from jax.sharding import PartitionSpec as P

HEAT_RATIO = 1.4
COURANT = 0.8


def extended(array, sides, width, wrap):
    for axis, dim in sides:
        size, length = (lax.axis_size(axis), array.shape[dim])
        up = [(i, (i + 1) % size) for i in range(size if wrap else size - 1)]
        down = [(j, i) for i, j in up]
        last = lax.slice_in_dim(array, length - width, length, axis=dim)
        first = lax.slice_in_dim(array, 0, width, axis=dim)
        before = lax.ppermute(last, axis, up)
        after = lax.ppermute(first, axis, down)
        array = jnp.concatenate([before, array, after], axis=dim)
    return array


def passed_along(block, axis, distance):
    devices = range(lax.axis_size(axis))
    route = [(i - distance, i) for i in devices if i - distance in devices]
    return lax.ppermute(block, axis, route)


def leading(values, direction):
    return lax.slice_in_dim(values, 0, values.shape[direction] - 1, axis=direction)


def trailing(values, direction):
    return lax.slice_in_dim(values, 1, values.shape[direction], axis=direction)


def conserved(density, velocity, pressure):
    momentum = density[None] * velocity
    kinetic = 0.5 * density * jnp.sum(velocity * velocity, axis=0)
    return jnp.concatenate(
        [density[None], momentum, (pressure / (HEAT_RATIO - 1.0) + kinetic)[None]], axis=0
    )


def primitives(fluid_state):
    density = fluid_state[0]
    velocities = fluid_state[1:4] / density[None]
    kinetic = 0.5 * jnp.sum(fluid_state[1:4] * velocities, axis=0)
    pressures = (HEAT_RATIO - 1.0) * (fluid_state[4] - kinetic)
    return (density, velocities, pressures)


def euler_flux(fluid_state, component):
    density, velocities, pressures = primitives(fluid_state)
    normal = velocities[component - 1]
    rows = [
        fluid_state[0] * normal,
        fluid_state[1] * normal,
        fluid_state[2] * normal,
        fluid_state[3] * normal,
        (fluid_state[4] + pressures) * normal,
    ]
    rows[component] = rows[component] + pressures
    signal = jnp.abs(normal) + jnp.sqrt(HEAT_RATIO * pressures / density)
    return (jnp.stack(rows), signal)


def tendency(padded):
    summed = None
    for direction, component in ((1, 3), (2, 1), (3, 2)):
        strip_cells = padded
        for across in (1, 2, 3):
            if across != direction:
                strip_cells = lax.slice_in_dim(
                    strip_cells, 1, strip_cells.shape[across] - 1, axis=across
                )
        fluxes, signal = euler_flux(strip_cells, component)
        fastest_face = jnp.maximum(leading(signal, direction - 1), trailing(signal, direction - 1))
        face_flux = 0.5 * (
            leading(fluxes, direction) + trailing(fluxes, direction)
        ) - 0.5 * fastest_face[None] * (
            trailing(strip_cells, direction) - leading(strip_cells, direction)
        )
        change = trailing(face_flux, direction) - leading(face_flux, direction)
        summed = change if summed is None else summed + change
    return -summed


def wave_bound(fluid_state):
    density, velocities, pressures = primitives(fluid_state)
    return jnp.max(
        jnp.sum(jnp.abs(velocities), axis=0) + 3.0 * jnp.sqrt(HEAT_RATIO * pressures / density)
    )


def mirror_sign():
    return jnp.array([1.0, -1.0, 1.0, 1.0, 1.0], jnp.float32)[:, None, None, None]


def colour_table(palette, palette_index):
    count_tf = palette_index.shape[0]
    count_bins = palette_index.shape[1]
    onehot = (
        jnp.arange(palette.shape[1], dtype=jnp.int32)[:, None] == palette_index.reshape(-1)[None, :]
    ).astype(jnp.float32)
    table = jnp.dot(palette, onehot, precision=lax.Precision.HIGHEST)
    return (
        table.reshape(4, count_tf, count_bins).transpose(1, 0, 2).reshape(count_tf * 4, count_bins)
    )


def sheet_shares(
    screen_shades, unrolled_mass_per_volume, thermal_grid_quantity, ray_increment_distance
):
    count_bins = screen_shades.shape[1]
    position = jnp.clip(unrolled_mass_per_volume - 0.5, 0.0, 1.0) * (count_bins - 1)
    hat_weights = jnp.maximum(
        0.0, 1.0 - jnp.abs(position[None, :] - jnp.arange(count_bins, dtype=jnp.float32)[:, None])
    )
    shade_mapping_index = jnp.dot(
        screen_shades, hat_weights, precision=lax.Precision.HIGHEST
    ).reshape(screen_shades.shape[0] // 4, 4, unrolled_mass_per_volume.shape[0])
    extinct = shade_mapping_index[:, 3] * unrolled_mass_per_volume[None] * ray_increment_distance
    absorbance_entries = 1.0 - jnp.exp(-extinct)
    radiance_source = (
        shade_mapping_index[:, :3] * (absorbance_entries * thermal_grid_quantity[None])[:, None]
    )
    return (extinct, radiance_source)


def march_slab(screen_shades, density_field, heat_field, ray_increment_distance):
    count_tf = screen_shades.shape[0] // 4
    planes = density_field.shape[0]
    cell_count = density_field.shape[1] * density_field.shape[2]

    def march_plane(carried, slab):
        optical, colour = carried
        extinct, radiance_source = sheet_shares(
            screen_shades, slab[0], slab[1], ray_increment_distance
        )
        return ((optical + extinct, colour + jnp.exp(-optical)[:, None] * radiance_source), None)

    initial = (
        jnp.zeros((count_tf, cell_count), jnp.float32),
        jnp.zeros((count_tf, 3, cell_count), jnp.float32),
    )
    (optical, colour), unused = lax.scan(
        march_plane,
        initial,
        (density_field.reshape(planes, cell_count), heat_field.reshape(planes, cell_count)),
    )
    return (optical, colour)


def widen(values, row_index, fluid_rows):
    sided = extended(values, (("group", 2),), 1, False)
    lower = jnp.where(row_index == 0, values[:, :, :1] * mirror_sign(), sided[:, :, :1])
    upper = jnp.where(
        row_index == fluid_rows - 1, values[:, :, -1:] * mirror_sign(), sided[:, :, -1:]
    )
    walled = jnp.concatenate([lower, values, upper], axis=2)
    return extended(walled, (("depth", 1), ("image", 3)), 1, True)


def shards(density, velocity, pressure, palette, palette_index):
    group_count = lax.axis_size("group")
    fluid_rows = group_count - 1
    depth_count = lax.axis_size("depth")
    row_index = lax.axis_index("group")
    is_fluid = row_index < fluid_rows
    is_render = row_index == fluid_rows
    shard_state = conserved(density, velocity, pressure)
    fastest = lax.pmax(wave_bound(shard_state), ("group", "depth", "image"))
    time_step = COURANT / fastest
    shard_rows = shard_state.shape[2]
    brick_rows = shard_rows * group_count // fluid_rows
    step_rows = brick_rows - shard_rows
    following = passed_along(shard_state, "group", -1)
    joined = jnp.concatenate([shard_state, following], axis=2)
    initial_state = lax.dynamic_slice_in_dim(joined, row_index * step_rows, brick_rows, axis=2)

    def change(values):
        padded = widen(values, row_index, fluid_rows)
        return lax.cond(is_fluid, tendency, lambda unused: jnp.zeros_like(values), padded)

    section_one = initial_state + time_step * change(initial_state)
    section_two = 0.75 * initial_state + 0.25 * (section_one + time_step * change(section_one))
    section_three = initial_state / 3.0 + 2.0 / 3.0 * (
        section_two + time_step * change(section_two)
    )
    previous = passed_along(section_three, "group", 1)
    joined_out = jnp.concatenate([previous, section_three], axis=2)
    fluid_state = lax.dynamic_slice_in_dim(
        joined_out, brick_rows - row_index * step_rows, shard_rows, axis=2
    )
    field_density, velocities, pressures = primitives(section_three)
    safe_density = jnp.where(is_fluid, field_density, 1.0)
    safe_heat = jnp.where(is_fluid, pressures / field_density, 1.0)
    ray_increment_distance = 2.0 / (section_three.shape[1] * depth_count)
    screen_shades = colour_table(palette, palette_index)
    count_tf = palette_index.shape[0]
    width_y = section_three.shape[3]
    picture_rows = fluid_rows * brick_rows
    all_density, all_heat = (
        lax.all_gather(safe_density, "group", axis=1, tiled=True),
        lax.all_gather(safe_heat, "group", axis=1, tiled=True),
    )
    block_density = all_density[:, :picture_rows]
    block_heat = all_heat[:, :picture_rows]
    rows_here = block_density.shape[1]

    def render():
        optical, colour = march_slab(
            screen_shades, block_density, block_heat, ray_increment_distance
        )
        return (
            optical.reshape(count_tf, rows_here, width_y),
            colour.reshape(count_tf, 3, rows_here, width_y),
        )

    def skip():
        return (
            jnp.zeros((count_tf, rows_here, width_y), jnp.float32),
            jnp.zeros((count_tf, 3, rows_here, width_y), jnp.float32),
        )

    optical, colour = lax.cond(is_render, render, skip)
    per_dev = count_tf // depth_count
    colour_parts = (
        colour.reshape(depth_count, per_dev, 3, group_count, shard_rows, width_y)
        .transpose(3, 0, 1, 2, 4, 5)
        .reshape(group_count * depth_count, per_dev, 3, shard_rows, width_y)
    )
    optical_parts = (
        optical.reshape(depth_count, per_dev, group_count, shard_rows, width_y)
        .transpose(2, 0, 1, 3, 4)
        .reshape(group_count * depth_count, per_dev, shard_rows, width_y)
    )
    got_colour, got_optical = (
        lax.all_to_all(colour_parts, ("group", "depth"), split_axis=0, concat_axis=0, tiled=True),
        lax.all_to_all(optical_parts, ("group", "depth"), split_axis=0, concat_axis=0, tiled=True),
    )
    got_colour = got_colour[fluid_rows * depth_count :]
    got_optical = got_optical[fluid_rows * depth_count :]
    before = jnp.cumsum(got_optical, axis=0) - got_optical
    picture = jnp.sum(jnp.exp(-before)[:, :, None] * got_colour, axis=0)
    return (fluid_state, picture)


def solution(mesh):
    return jax.shard_map(
        shards,
        mesh=mesh,
        in_specs=(
            P("depth", "group", "image"),
            P(None, "depth", "group", "image"),
            P("depth", "group", "image"),
            P(),
            P(),
        ),
        out_specs=(P(None, "depth", "group", "image"), P("depth", None, "group", "image")),
        check_vma=False,
    )
```

profile of v0, /device:TPU:17, one launch (start us, length us, event | category | flops | bytes accessed | tf_op | source)
XLA Modules:
  0.0 877.5 jit_solution(6687542848462764435)
XLA Ops:
  9.6 2.1 collective-permute-start
  11.7 22.4 %collective-permute-done = f32[5,8,48,128]{3,2,1,0:T(8,128)S(1)} collective-permute-done((f32[5,8,48,128]{3,2,1,0:T(8,128)S(1)}, f32[5,8,48,128]{3,2,1,0:T(8,128)S(1)}, u32[]{:S(2)}, u32[]{:S(2)}) %collective-permute-start) | collective-permute-done | bytes 983072 | tf_op jit(solution)/shard_map/ppermute | solution.py:26
  34.4 1.9 collective-permute-start.1
  36.3 3.4 collective-permute-start.2
  42.8 2.9 collective-permute-done.4
  45.8 3.4 collective-permute-done.3
  51.2 3.1 copy.149
  54.3 3.2 collective-permute-start.6
  60.3 37.4 %pmax.7 = f32[]{:T(128)} all-reduce(f32[]{:T(128)} %get-tuple-element.210), channel_id=1, replica_groups=mesh['group'=4,'depth'=2,'image'=4] {'group','depth','image'}, use_global_device_ids=true, to_apply=%region_4.0 | all-reduce | flops 1 | bytes 8 | tf_op jit(solution)/shard_map/pmax | solution.py:173
  99.9 2.7 copy.120
  102.6 6.3 pad_maximum_fusion
  108.9 12.3 %conditional.4 = (f32[5,8,64,128]{3,2,1,0:T(8,128)S(1)}) conditional(s32[]{:T(128)} %convert_element_type.4, () %tuple.46, f32[5,10,66,130]{3,2,1,0:T(8,128)} %pad_maximum_fusion), branch_computations={%region_5.6_spmd, %region_6.10_spmd} | conditional | flops 13370877 | bytes 73016488 | solution.py:184
  110.2 2.1 multiply_reduce_fusion
  124.0 1.9 collective-permute-start.7
  125.9 3.4 collective-permute-start.8
  132.2 2.9 collective-permute-done.10
  135.1 3.2 collective-permute-done.9
  138.5 2.3 fusion.112
  140.9 2.5 copy.151
  143.3 3.5 collective-permute-start.12
  146.8 2.5 copy.150
  150.7 2.0 copy.129
  152.6 1.9 copy.128
  154.5 6.5 pad_maximum_fusion.1
  161.0 12.1 %conditional.5 = (f32[5,8,64,128]{3,2,1,0:T(8,128)S(1)}) conditional(s32[]{:T(128)} %convert_element_type.4, () %tuple.47, f32[5,10,66,130]{3,2,1,0:T(8,128)} %pad_maximum_fusion.1), branch_computations={%region_10.11_spmd, %region_11.15_spmd} | conditional | flops 13370877 | bytes 73016488 | solution.py:184
  162.2 2.1 multiply_reduce_fusion.3
  174.2 2.2 multiply_add_fusion.1
  178.4 3.8 collective-permute-start.14
  184.6 2.9 collective-permute-done.16
  187.5 4.1 collective-permute-done.15
  191.8 2.3 fusion.111
  194.2 2.5 copy.153
  196.6 2.6 collective-permute-start.18
  199.2 2.5 copy.152
  202.0 2.0 copy.137
  204.0 1.9 copy.136
  205.9 6.5 pad_maximum_fusion.2
  212.4 13.1 %conditional.6 = (f32[5,8,64,128]{3,2,1,0:T(8,128)}) conditional(s32[]{:T(128)} %convert_element_type.4, () %tuple.48, f32[5,10,66,130]{3,2,1,0:T(8,128)} %pad_maximum_fusion.2), branch_computations={%region_15.16_spmd, %region_16.20_spmd} | conditional | flops 13370877 | bytes 73016488 | solution.py:184
  213.5 2.1 multiply_reduce_fusion.6
  231.1 25.5 %all-gather.3.cloned.1.call-done = f32[8,256,128]{2,0,1:T(8,128)} async-done(((f32[8,64,128]{2,0,1:T(8,128)}), f32[8,256,128]{2,0,1:T(8,128)}) %all-gather.3.cloned.1.call-update) | async-done | bytes 1048592 | tf_op jit(solution)/shard_map/all_gather | solution.py:205
  256.5 29.5 %all-gather.5.cloned.1.call-done = f32[8,256,128]{2,0,1:T(8,128)} async-done(((f32[8,64,128]{2,0,1:T(8,128)}), f32[8,256,128]{2,0,1:T(8,128)}) %all-gather.5.cloned.1.call-update) | async-done | bytes 1048592 | tf_op jit(solution)/shard_map/all_gather | solution.py:206
  286.1 2.8 conditional.7
  291.2 470.9 %all-to-all-start = ((f32[8,4,48,128]{3,2,1,0:T(8,128)}), f32[8,4,48,128]{3,2,1,0:T(8,128)S(1)}, u32[]{:S(2)}, u32[]{:S(2)}) async-start(f32[8,4,48,128]{3,2,1,0:T(8,128)} %bitcast.60), calls=%async_computation | async-start | bytes 1572864 | tf_op jit(solution)/shard_map/all_to_all | solution.py:241
  762.0 3.3 copy.144
  765.4 13.9 %all-to-all-done = f32[8,4,48,128]{3,2,1,0:T(8,128)S(1)} async-done(((f32[8,4,48,128]{3,2,1,0:T(8,128)}), f32[8,4,48,128]{3,2,1,0:T(8,128)S(1)}, u32[]{:S(2)}, u32[]{:S(2)}) %all-to-all-start) | async-done | bytes 786464 | tf_op jit(solution)/shard_map/all_to_all | solution.py:241
  779.3 6.8 all-to-all-start.1
  786.1 3.1 collective-permute-start.19
  789.2 78.1 %collective-permute-done.19 = f32[5,8,64,128]{3,2,1,0:T(8,128)S(1)} collective-permute-done((f32[5,8,64,128]{3,2,1,0:T(8,128)S(1)}, f32[5,8,64,128]{3,2,1,0:T(8,128)S(1)}, u32[]{:S(2)}, u32[]{:S(2)}) %collective-permute-start.19) | collective-permute-done | bytes 1310752 | tf_op jit(solution)/shard_map/ppermute | solution.py:26
  (180 shorter events, 69.2 us)
Async XLA Ops:
  7.2 223.1 %copy-start = (f32[4,256]{1,0:T(4,128)S(1)}, f32[4,256]{1,0:T(4,128)}, u32[]{:S(2)}) copy-start(f32[4,256]{1,0:T(4,128)} %param.24) | copy-start | bytes 12292
  7.2 1.6 copy-start.11
  7.2 1.6 copy-start.13
  7.2 249.3 %all-gather.3.cloned.1.call-start = ((), (), s32[]{:S(2)}) async-start(), calls=%async_computation.2 | async-start | bytes 1310720 | tf_op jit(solution)/shard_map/all_gather | solution.py:205
  9.6 24.5 %collective-permute-start = (f32[5,8,48,128]{3,2,1,0:T(8,128)S(1)}, f32[5,8,48,128]{3,2,1,0:T(8,128)S(1)}, u32[]{:S(2)}, u32[]{:S(2)}) collective-permute-start(f32[5,8,48,128]{3,2,1,0:T(8,128)S(1)} %pad_maximum_fusion.6), channel_id=1, source_target_pairs={{8,0},{16,8},{24,16},{9,1},{17,9},{25,17},{10,2},{18,10},{26,18},{... | collective-permute-start | bytes 2949128 | tf_op jit(solution)/shard_map/ppermute | solution.py:26
  11.7 29.4 %copy-start.15 = (f32[5]{0:T(128)S(1)}, f32[5]{0:T(128)}, u32[]{:S(2)}) copy-start(f32[5]{0:T(128)} %constant.158.clone) | copy-start | bytes 64
  34.4 5.3 collective-permute-start.1
  36.3 4.8 collective-permute-start.2
  41.3 7.9 copy-start.12
  41.3 4.5 collective-permute-start.4
  42.6 6.5 collective-permute-start.3
  54.3 44.0 %collective-permute-start.6 = (f32[5,10,66,1]{2,1,3,0:T(8,128)}, f32[5,10,66,1]{2,1,3,0:T(8,128)}, u32[]{:S(2)}, u32[]{:S(2)}) collective-permute-start(f32[5,10,66,1]{2,1,3,0:T(8,128)} %copy.149), channel_id=1, source_target_pairs={{1,0},{2,1},{3,2},{0,3},{5,4},{6,5},{7,6},{4,7},{9,8},{10,9},{11,1... | collective-permute-start | bytes 39608 | tf_op jit(solution)/shard_map/ppermute | solution.py:18
  59.1 40.7 %collective-permute-start.5 = (f32[5,10,66,1]{2,1,3,0:T(8,128)}, f32[5,10,66,1]{2,1,3,0:T(8,128)}, u32[]{:S(2)}, u32[]{:S(2)}) collective-permute-start(f32[5,10,66,1]{2,1,3,0:T(8,128)} %copy.148), channel_id=1, source_target_pairs={{0,1},{1,2},{2,3},{3,0},{4,5},{5,6},{6,7},{7,4},{8,9},{9,10},{10,1... | collective-permute-start | bytes 39608 | tf_op jit(solution)/shard_map/ppermute | solution.py:17
  110.2 2.6 copy-start.4
  121.2 1.2 copy-start.9
  124.0 5.3 collective-permute-start.7
  125.9 4.6 collective-permute-start.8
  130.7 4.5 collective-permute-start.10
  131.7 6.6 collective-permute-start.9
  143.3 7.3 collective-permute-start.12
  149.3 3.4 collective-permute-start.11
  162.2 2.6 copy-start.2
  173.1 1.1 copy-start.10
  176.4 5.8 collective-permute-start.13
  178.4 4.5 collective-permute-start.14
  183.1 4.5 collective-permute-start.16
  184.6 7.1 collective-permute-start.15
  196.6 5.4 collective-permute-start.18
  201.7 2.3 collective-permute-start.17
  213.5 2.6 copy-start.3
  227.3 1.1 copy-start.7
  228.4 1.9 copy-start.14
  229.3 56.8 %all-gather.5.cloned.1.call-start = ((), (), s32[]{:S(2)}) async-start(), calls=%async_computation.3 | async-start | bytes 1310720 | tf_op jit(solution)/shard_map/all_gather | solution.py:206
  291.2 488.1 %all-to-all-start = ((f32[8,4,48,128]{3,2,1,0:T(8,128)}), f32[8,4,48,128]{3,2,1,0:T(8,128)S(1)}, u32[]{:S(2)}, u32[]{:S(2)}) async-start(f32[8,4,48,128]{3,2,1,0:T(8,128)} %bitcast.60), calls=%async_computation | async-start | bytes 1572864 | tf_op jit(solution)/shard_map/all_to_all | solution.py:241
  779.3 6.8 copy-start.8
  779.3 89.2 %all-to-all-start.1 = ((f32[8,4,3,48,128]{4,3,2,1,0:T(8,128)}), f32[8,4,3,48,128]{4,3,2,1,0:T(8,128)}, u32[]{:S(2)}, u32[]{:S(2)}) async-start(f32[8,4,3,48,128]{4,3,2,1,0:T(8,128)} %bitcast.297), calls=%async_computation.1 | async-start | bytes 4718592 | tf_op jit(solution)/shard_map/all_to_all | solution.py:240
  786.1 81.2 %collective-permute-start.19 = (f32[5,8,64,128]{3,2,1,0:T(8,128)S(1)}, f32[5,8,64,128]{3,2,1,0:T(8,128)S(1)}, u32[]{:S(2)}, u32[]{:S(2)}) collective-permute-start(f32[5,8,64,128]{3,2,1,0:T(8,128)S(1)} %copy-done.8), channel_id=1, source_target_pairs={{0,8},{8,16},{16,24},{1,9},{9,17},{17,25},{2,10},{10,18},{18,26},{... | collective-permute-start | bytes 3932168 | tf_op jit(solution)/shard_map/ppermute | solution.py:26
  867.3 3.1 copy-start.1
Sparse Core Ops, SparseCore 0:
  229.4 27.0 all-gather.2
  258.7 27.3 all-gather.4
where the time goes:
time: 884 us; the launch traced here: 877 us
  starting transfers between devices  516 us (58%)
  waiting for transfers between devices  192 us (22%)
  other arithmetic  62.9 us (7%)
  local copies, waits for them, and re-layouts  51.9 us (6%)
  blocking collectives  37.4 us (4%)
  between operations  15.3 us (2%)
    all_to_all x1, starting transfers between devices, shards(): lax.all_to_all(optical_parts, ('group', 'depth'), split_axis=0, concat_ax...  471 us
    ppermute x2, waiting for transfers between devices, passed_along(): return lax.ppermute(block, axis, route)  101 us
    pmax x1, blocking collectives, shards(): fastest = lax.pmax(wave_bound(shard_state), ('group', 'depth', 'image'))  37.4 us
    all_gather x1, waiting for transfers between devices, shards(): lax.all_gather(safe_heat, 'group', axis=1, tiled=True)  29.5 us
    all_gather x1, waiting for transfers between devices, shards(): lax.all_gather(safe_density, 'group', axis=1, tiled=True)  25.5 us
    ppermute x9, starting transfers between devices, extended(): after = lax.ppermute(first, axis, down)  23.6 us
    concatenate x6, other arithmetic, extended(): array = jnp.concatenate([before, array, after], axis=dim)  19.9 us
    unnamed x29, local copies, waits for them, and re-layouts  17.8 us
  transfers between devices with their start and end apart: 24, of which 14 were waited for; matrix products, arithmetic and copies ran while one was open for 2% of the time, Pallas kernels for 0%

commit v1 on v0

v1 whole, which is shorter than its diff:
```python
import jax
import jax.numpy as jnp
from jax import lax
from jax.experimental import pallas as pl
from jax.experimental.pallas import tpu as pltpu
from jax.sharding import PartitionSpec as P

HEAT_RATIO = 1.4
COURANT = 0.8


def extended(array, sides, width, wrap):
    for axis, dim in sides:
        size, length = (lax.axis_size(axis), array.shape[dim])
        up = [(i, (i + 1) % size) for i in range(size if wrap else size - 1)]
        down = [(j, i) for i, j in up]
        last = lax.slice_in_dim(array, length - width, length, axis=dim)
        first = lax.slice_in_dim(array, 0, width, axis=dim)
        before = lax.ppermute(last, axis, up)
        after = lax.ppermute(first, axis, down)
        array = jnp.concatenate([before, array, after], axis=dim)
    return array


def leading(values, direction):
    return lax.slice_in_dim(values, 0, values.shape[direction] - 1, axis=direction)


def trailing(values, direction):
    return lax.slice_in_dim(values, 1, values.shape[direction], axis=direction)


def conserved(density, velocity, pressure):
    momentum = density[None] * velocity
    kinetic = 0.5 * density * jnp.sum(velocity * velocity, axis=0)
    return jnp.concatenate(
        [density[None], momentum, (pressure / (HEAT_RATIO - 1.0) + kinetic)[None]], axis=0
    )


def primitives(fluid_state):
    density = fluid_state[0]
    velocities = fluid_state[1:4] / density[None]
    kinetic = 0.5 * jnp.sum(fluid_state[1:4] * velocities, axis=0)
    pressures = (HEAT_RATIO - 1.0) * (fluid_state[4] - kinetic)
    return (density, velocities, pressures)


def euler_flux(fluid_state, component):
    density, velocities, pressures = primitives(fluid_state)
    normal = velocities[component - 1]
    rows = [
        fluid_state[0] * normal,
        fluid_state[1] * normal,
        fluid_state[2] * normal,
        fluid_state[3] * normal,
        (fluid_state[4] + pressures) * normal,
    ]
    rows[component] = rows[component] + pressures
    signal = jnp.abs(normal) + jnp.sqrt(HEAT_RATIO * pressures / density)
    return (jnp.stack(rows), signal)


def tendency(padded):
    summed = None
    for direction, component in ((1, 3), (2, 1), (3, 2)):
        strip_cells = padded
        for across in (1, 2, 3):
            if across != direction:
                strip_cells = lax.slice_in_dim(
                    strip_cells, 1, strip_cells.shape[across] - 1, axis=across
                )
        fluxes, signal = euler_flux(strip_cells, component)
        fastest_face = jnp.maximum(leading(signal, direction - 1), trailing(signal, direction - 1))
        face_flux = 0.5 * (
            leading(fluxes, direction) + trailing(fluxes, direction)
        ) - 0.5 * fastest_face[None] * (
            trailing(strip_cells, direction) - leading(strip_cells, direction)
        )
        change = trailing(face_flux, direction) - leading(face_flux, direction)
        summed = change if summed is None else summed + change
    return -summed


def wave_bound(fluid_state):
    density, velocities, pressures = primitives(fluid_state)
    return jnp.max(
        jnp.sum(jnp.abs(velocities), axis=0) + 3.0 * jnp.sqrt(HEAT_RATIO * pressures / density)
    )


def lanes(values, index):
    return jnp.take_along_axis(values, index, axis=1)

def render_kernel(scale, rho_ref, heat_ref, palette_ref, index_ref, out_ref, table, ke, ko, we, wo):
    planes, rows, width = rho_ref.shape
    count_tf, bins = index_ref.shape
    half = bins // 2
    lane = lax.broadcasted_iota(jnp.int32, (count_tf, half), 1)
    low, high = index_ref[:, :half], index_ref[:, half:]
    for parity in range(2):
        at = lane * 2 + parity
        inside = jnp.where(at < half, at, at - half)
        colour = jnp.where(at < half, lanes(low, inside), lanes(high, inside))
        wrapped = jnp.where(colour < half, colour, colour - half)
        for c in range(4):
            first = jnp.broadcast_to(palette_ref[c:c+1, :half], (count_tf, half))
            second = jnp.broadcast_to(palette_ref[c:c+1, half:], (count_tf, half))
            table[c, parity] = jnp.where(colour < half, lanes(first, wrapped), lanes(second, wrapped))
    def prepare(z, _):
        position = jnp.clip(rho_ref[z] - 0.5, 0.0, 1.0) * (bins - 1)
        cell = jnp.minimum(position.astype(jnp.int32), bins - 2)
        even = (cell + 1) >> 1
        odd = cell >> 1
        ke[z] = even
        ko[z] = odd
        we[z] = 1.0 - jnp.abs(position - (2 * even).astype(jnp.float32))
        wo[z] = 1.0 - jnp.abs(position - (2 * odd + 1).astype(jnp.float32))
        return 0
    lax.fori_loop(0, planes, prepare, 0)
    tables = [[table[c, p] for p in range(2)] for c in range(4)]
    def ray(x, _):
        trans = jnp.ones((count_tf, width), jnp.float32)
        light = [jnp.zeros((count_tf, width), jnp.float32) for _ in range(3)]
        for z in range(planes):
            def wide(ref):
                return jnp.broadcast_to(ref[z, pl.ds(x, 1), :], (count_tf, width))
            ie, io, fe, fo = wide(ke), wide(ko), wide(we), wide(wo)
            looked = [lanes(tables[c][0], ie) * fe + lanes(tables[c][1], io) * fo for c in range(4)]
            passed = jnp.exp(looked[3] * (wide(rho_ref) * -scale))
            weight = trans * (1.0 - passed) * wide(heat_ref)
            light = [light[c] + looked[c] * weight for c in range(3)]
            trans = trans * passed
        for c, values in enumerate(light + [trans]):
            out_ref[pl.ds(c * rows + x, count_tf, stride=4 * rows), :] = values
        return 0
    lax.fori_loop(0, rows, ray, 0)

def render(rho, heat, palette, index, scale):
    planes, rows, width = rho.shape
    count_tf, bins = index.shape
    out = pl.pallas_call(
        lambda *refs: render_kernel(scale, *refs),
        out_shape=jax.ShapeDtypeStruct((count_tf * 4 * rows, width), jnp.float32),
        in_specs=[pl.BlockSpec(memory_space=pltpu.VMEM)] * 4,
        out_specs=pl.BlockSpec(memory_space=pltpu.VMEM),
        scratch_shapes=[pltpu.VMEM((4, 2, count_tf, bins // 2), jnp.float32)]
        + [pltpu.VMEM((planes, rows, width), jnp.int32)] * 2
        + [pltpu.VMEM((planes, rows, width), jnp.float32)] * 2,
        name="render",
    )(rho, heat, palette, index)
    return out.reshape(count_tf, 4, rows, width)


def largest(value, axes):
    for axis in axes:
        size = lax.axis_size(axis)
        step = 1
        while step < size:
            route = [(i, (i + step) % size) for i in range(size)]
            value = jnp.maximum(value, lax.ppermute(value, axis, route))
            step *= 2
    return value


def mirror_sign():
    return jnp.array([1.0, -1.0, 1.0, 1.0, 1.0], jnp.float32)[:, None, None, None]


def widen(values):
    row_index, rows = lax.axis_index("group"), lax.axis_size("group")
    sided = extended(values, (("group", 2),), 1, False)
    lower = jnp.where(row_index == 0, values[:, :, :1] * mirror_sign(), sided[:, :, :1])
    upper = jnp.where(row_index == rows - 1, values[:, :, -1:] * mirror_sign(), sided[:, :, -1:])
    walled = jnp.concatenate([lower, values, upper], axis=2)
    return extended(walled, (("depth", 1), ("image", 3)), 1, True)


def composed(shares):
    light, passed = None, None
    for d in range(shares.shape[0]):
        slab = shares[d]
        light = slab[:, :3] if d == 0 else light + passed * slab[:, :3]
        passed = slab[:, 3:] if d == 0 else passed * slab[:, 3:]
    return light


def exchanged(shares):
    depth = lax.axis_size("depth")
    count_tf = shares.shape[0]
    per_dev = count_tf // depth
    parts = shares.reshape((depth, per_dev) + shares.shape[1:])
    if depth == 2:
        me = lax.axis_index("depth")
        mine = jnp.where(me == 0, parts[0], parts[1])
        other = lax.ppermute(jnp.where(me == 0, parts[1], parts[0]), "depth", [(0, 1), (1, 0)])
        front = jnp.where(me == 0, mine, other)
        back = jnp.where(me == 0, other, mine)
        return front[:, :3] + front[:, 3:] * back[:, :3]
    return composed(lax.all_to_all(parts, "depth", 0, 0, tiled=True))


def shards(density, velocity, pressure, palette, palette_index):
    initial_state = conserved(density, velocity, pressure)
    fastest = largest(wave_bound(initial_state)[None], ("image", "depth", "group"))[0]
    time_step = COURANT / fastest

    def change(values):
        return tendency(widen(values))

    section_one = initial_state + time_step * change(initial_state)
    section_two = 0.75 * initial_state + 0.25 * (section_one + time_step * change(section_one))
    fluid_state = initial_state / 3.0 + 2.0 / 3.0 * (
        section_two + time_step * change(section_two)
    )
    field_density, velocities, pressures = primitives(fluid_state)
    planes = density.shape[0] * lax.axis_size("depth")
    shares = render(field_density, pressures / field_density, palette, palette_index, 2.0 / planes)
    return (fluid_state, exchanged(shares))


def solution(mesh):
    return jax.shard_map(
        shards,
        mesh=mesh,
        in_specs=(
            P("depth", "group", "image"),
            P(None, "depth", "group", "image"),
            P("depth", "group", "image"),
            P(),
            P(),
        ),
        out_specs=(P(None, "depth", "group", "image"), P("depth", None, "group", "image")),
        check_vma=False,
    )
```

time: 884 us -> 167 us (0.19)
  the two profiles are of different devices: /device:TPU:17 before, /device:TPU:0 now
where the time goes in v1:
time: 167 us; the launch traced here: 166 us
  other arithmetic  40.2 us (24%)
  starting transfers between devices  40 us (24%)
  waiting for transfers between devices  37.4 us (22%)
  local copies, waits for them, and re-layouts  29.7 us (18%)
  Pallas kernels  12.9 us (8%)
  between operations  5.52 us (3%)
    sub x9, other arithmetic, tendency(): 0.5 * (leading(fluxes, direction) + trailing(fluxes, direction))  14.3 us
    ppermute x9, starting transfers between devices, extended(): after = lax.ppermute(first, axis, down)  14.3 us
    ppermute x9, waiting for transfers between devices, extended(): after = lax.ppermute(first, axis, down)  13.1 us
    pallas_call x1, Pallas kernels, render(): pl.pallas_call(lambda *refs: render_kernel(scale, *refs), out_shape=jax.S...  12.9 us
    slice x6, local copies, waits for them, and re-layouts, extended(): first = lax.slice_in_dim(array, 0, width, axis=dim)  12.3 us
    ppermute x5, starting transfers between devices, largest(): value = jnp.maximum(value, lax.ppermute(value, axis, route))  12.2 us
    ppermute x9, starting transfers between devices, extended(): before = lax.ppermute(last, axis, up)  12.1 us
    ppermute x1, waiting for transfers between devices, exchanged(): lax.ppermute(jnp.where(me == 0, parts[1], parts[0]), 'depth', [(0, 1), (1...  10.1 us
  transfers between devices with their start and end apart: 24, of which 15 were waited for; matrix products, arithmetic and copies ran while one was open for 12% of the time, Pallas kernels for 0%

profile of v1, /device:TPU:0, one launch (start us, length us, event | category | flops | bytes accessed | tf_op | source)
XLA Modules:
  0.0 165.7 jit_solution(16490021494295004483)
XLA Ops:
  0.7 1.5 multiply_reduce_fusion.9
  3.0 5.0 %collective-permute-start.5 = (f32[5,8,1,128]{3,2,1,0:T(1,128)S(1)}, f32[5,8,1,128]{3,2,1,0:T(1,128)S(1)}, u32[]{:S(2)}, u32[]{:S(2)}) collective-permute-start(f32[5,8,1,128]{3,2,1,0:T(1,128)S(1)} %get-tuple-element.49), channel_id=1, source_target_pairs={{0,8},{8,16},{16,24},{1,9},{9,17},{17,25},{2,10},{10,18},{18,26},{... | collective-permute-start | bytes 61448 | tf_op jit(solution)/shard_map/ppermute | solution.py:19
  9.4 3.0 %collective-permute-done = f32[1]{0:T(128)} collective-permute-done((f32[1]{0:T(128)}, f32[1]{0:T(128)}, u32[]{:S(2)}, u32[]{:S(2)}) %collective-permute-start) | collective-permute-done | bytes 36 | tf_op jit(solution)/shard_map/ppermute | solution.py:161
  13.6 2.9 %collective-permute-start.1 = (f32[1]{0:T(128)}, f32[1]{0:T(128)}, u32[]{:S(2)}, u32[]{:S(2)}) collective-permute-start(f32[1]{0:T(128)} %max.42), channel_id=1, source_target_pairs={{0,2},{1,3},{2,0},{3,1},{4,6},{5,7},{6,4},{7,5},{8,10},{9,11},{10,... | collective-permute-start | bytes 20 | tf_op jit(solution)/shard_map/ppermute | solution.py:161
  18.0 2.9 %collective-permute-start.2 = (f32[1]{0:T(128)}, f32[1]{0:T(128)}, u32[]{:S(2)}, u32[]{:S(2)}) collective-permute-start(f32[1]{0:T(128)} %max.43), channel_id=1, source_target_pairs={{0,4},{4,0},{1,5},{5,1},{2,6},{6,2},{3,7},{7,3},{8,12},{12,8},{9,1... | collective-permute-start | bytes 20 | tf_op jit(solution)/shard_map/ppermute | solution.py:161
  22.3 4.0 %collective-permute-start.3 = (f32[1]{0:T(128)}, f32[1]{0:T(128)}, u32[]{:S(2)}, u32[]{:S(2)}) collective-permute-start(f32[1]{0:T(128)} %max.44), channel_id=1, source_target_pairs={{0,8},{8,16},{16,24},{24,0},{1,9},{9,17},{17,25},{25,1},{2,10},{10... | collective-permute-start | bytes 20 | tf_op jit(solution)/shard_map/ppermute | solution.py:161
  26.3 2.4 %collective-permute-done.3 = f32[1]{0:T(128)} collective-permute-done((f32[1]{0:T(128)}, f32[1]{0:T(128)}, u32[]{:S(2)}, u32[]{:S(2)}) %collective-permute-start.3) | collective-permute-done | bytes 36 | tf_op jit(solution)/shard_map/ppermute | solution.py:161
  29.3 2.4 %collective-permute-start.4 = (f32[1]{0:T(128)}, f32[1]{0:T(128)}, u32[]{:S(2)}, u32[]{:S(2)}) collective-permute-start(f32[1]{0:T(128)} %max.45), channel_id=1, source_target_pairs={{0,16},{8,24},{16,0},{24,8},{1,17},{9,25},{17,1},{25,9},{2,18},{10... | collective-permute-start | bytes 20 | tf_op jit(solution)/shard_map/ppermute | solution.py:161
  31.7 2.3 %collective-permute-done.4 = f32[1]{0:T(128)} collective-permute-done((f32[1]{0:T(128)}, f32[1]{0:T(128)}, u32[]{:S(2)}, u32[]{:S(2)}) %collective-permute-start.4) | collective-permute-done | bytes 36 | tf_op jit(solution)/shard_map/ppermute | solution.py:161
  35.0 1.6 collective-permute-start.8
  37.5 1.5 fusion.31
  40.2 1.5 collective-permute-done.7
  41.8 2.0 %fusion.165 = (f32[5,10,50,1]{3,2,1,0:T(8,128)}, f32[5,10,50,1]{3,2,1,0:T(8,128)}) fusion(f32[5,10,50,128]{3,2,1,0:T(8,128)S(1)} %pad_maximum_fusion.23), kind=kLoop, calls=%fused_computation.363 | loop fusion | bytes 40000 | tf_op jit(solution)/shard_map/slice | solution.py:18
  43.9 2.5 %copy.13 = f32[5,10,50,1]{2,3,1,0:T(1,128)} copy(f32[5,10,50,1]{3,2,1,0:T(8,128)} %get-tuple-element.32) | data formatting | bytes 20000 | tf_op jit(solution)/shard_map/slice | solution.py:17
  46.4 2.5 %copy.14 = f32[5,10,50,1]{2,3,1,0:T(1,128)} copy(f32[5,10,50,1]{3,2,1,0:T(8,128)} %get-tuple-element.31) | data formatting | bytes 20000 | tf_op jit(solution)/shard_map/slice | solution.py:18
  48.9 1.7 %collective-permute-start.10 = (f32[5,10,50,1]{2,3,1,0:T(1,128)}, f32[5,10,50,1]{2,3,1,0:T(1,128)}, u32[]{:S(2)}, u32[]{:S(2)}) collective-permute-start(f32[5,10,50,1]{2,3,1,0:T(1,128)} %copy.14), channel_id=1, source_target_pairs={{1,0},{2,1},{3,2},{0,3},{5,4},{6,5},{7,6},{4,7},{9,8},{10,9},{11,1... | collective-permute-start | bytes 30008 | tf_op jit(solution)/shard_map/ppermute | solution.py:20
  52.3 1.4 copy.15
  53.7 2.5 %copy.16 = f32[5,10,50,1]{3,2,1,0:T(8,128)} copy(f32[5,10,50,1]{2,3,1,0:T(1,128)} %collective-permute-done.10) | data formatting | bytes 20000 | tf_op jit(solution)/shard_map/ppermute | solution.py:20
  56.1 4.7 %pad_maximum_fusion = f32[5,10,50,130]{3,2,1,0:T(8,128)S(1)} fusion(f32[5,10,50,1]{3,2,1,0:T(8,128)} %copy.16, f32[5,1,50,128]{3,2,1,0:T(8,128)} %copy-done.18, f32[5,8,1,128]{3,2,1,0:T(1,128)} %copy-done.25, f32[1,8,48,128]{3,2,1,0:T(8,128)S(1)} %get-tuple-element.55, f32[3,8,48,128]{3,2,1,0:T(8,128)S(1)} %get-tuple-element.53, ...), kind=kLoop, calls=%fused_computation | loop fusion | flops 2600000 | bytes 2600000 | tf_op jit(solution)/shard_map/concatenate | solution.py:21
  63.3 2.5 %fusion.9 = f32[5,8,48,129]{3,2,1,0:T(8,128)S(1)} fusion(f32[1,8,48,128]{3,2,1,0:T(8,128)S(1)} %bitcast.239, f32[3,8,48,128]{3,2,1,0:T(8,128)S(1)} %get-tuple-element.53, f32[5,10,50,1]{3,2,1,0:T(8,128)S(1)} %copy.15, f32[5,1,50,128]{3,2,1,0:T(8,128)S(1)} %copy-done.20, f32[5,1,50,128]{3,2,1,0:T(8,128)S(1)} %copy-done.23, ...), kind=kLoop, calls=%fused_computation.16 | loop fusion | flops 4705920 | bytes 4470304 | tf_op jit(solution)/shard_map/sub | solution.py:75
  66.4 1.9 %collective-permute-start.11 = (f32[5,8,1,128]{3,2,1,0:T(1,128)S(1)}, f32[5,8,1,128]{3,2,1,0:T(1,128)S(1)}, u32[]{:S(2)}, u32[]{:S(2)}) collective-permute-start(f32[5,8,1,128]{3,2,1,0:T(1,128)S(1)} %get-tuple-element.47), channel_id=1, source_target_pairs={{0,8},{8,16},{16,24},{1,9},{9,17},{17,25},{2,10},{10,18},{18,26},{... | collective-permute-start | bytes 61448 | tf_op jit(solution)/shard_map/ppermute | solution.py:19
  68.3 1.5 collective-permute-start.12
  69.8 4.2 %collective-permute-done.12 = f32[5,8,1,128]{3,2,1,0:T(1,128)S(1)} collective-permute-done((f32[5,8,1,128]{3,2,1,0:T(1,128)S(1)}, f32[5,8,1,128]{3,2,1,0:T(1,128)S(1)}, u32[]{:S(2)}, u32[]{:S(2)}) %collective-permute-start.12) | collective-permute-done | bytes 20512 | tf_op jit(solution)/shard_map/ppermute | solution.py:20
  74.3 1.6 collective-permute-start.14
  76.9 1.5 fusion.29
  78.3 2.2 %collective-permute-done.14 = f32[5,1,50,128]{3,2,1,0:T(8,128)S(1)} collective-permute-done((f32[5,1,50,128]{3,2,1,0:T(8,128)S(1)}, f32[5,1,50,128]{3,2,1,0:T(8,128)S(1)}, u32[]{:S(2)}, u32[]{:S(2)}) %collective-permute-start.14) | collective-permute-done | bytes 128032 | tf_op jit(solution)/shard_map/ppermute | solution.py:20
  80.5 1.5 collective-permute-done.13
  82.2 2.0 %fusion.164 = (f32[5,10,50,1]{3,2,1,0:T(8,128)}, f32[5,10,50,1]{3,2,1,0:T(8,128)}) fusion(f32[5,10,50,128]{3,2,1,0:T(8,128)S(1)} %pad_maximum_fusion.24), kind=kLoop, calls=%fused_computation.362 | loop fusion | bytes 40000 | tf_op jit(solution)/shard_map/slice | solution.py:18
  84.3 1.9 %copy.19 = f32[5,10,50,1]{2,3,1,0:T(1,128)S(1)} copy(f32[5,10,50,1]{3,2,1,0:T(8,128)} %get-tuple-element.30) | data formatting | bytes 20000 | tf_op jit(solution)/shard_map/slice | solution.py:17
  86.2 1.9 %copy.20 = f32[5,10,50,1]{2,3,1,0:T(1,128)S(1)} copy(f32[5,10,50,1]{3,2,1,0:T(8,128)} %get-tuple-element.29) | data formatting | bytes 20000 | tf_op jit(solution)/shard_map/slice | solution.py:18
  88.1 1.8 %collective-permute-start.16 = (f32[5,10,50,1]{2,3,1,0:T(1,128)S(1)}, f32[5,10,50,1]{2,3,1,0:T(1,128)S(1)}, u32[]{:S(2)}, u32[]{:S(2)}) collective-permute-start(f32[5,10,50,1]{2,3,1,0:T(1,128)S(1)} %copy.20), channel_id=1, source_target_pairs={{1,0},{2,1},{3,2},{0,3},{5,4},{6,5},{7,6},{4,7},{9,8},{10,9},{11,1... | collective-permute-start | bytes 30008 | tf_op jit(solution)/shard_map/ppermute | solution.py:20
  92.5 1.7 %copy.22 = f32[5,10,50,1]{3,2,1,0:T(8,128)} copy(f32[5,10,50,1]{2,3,1,0:T(1,128)S(1)} %collective-permute-done.16) | data formatting | bytes 20000 | tf_op jit(solution)/shard_map/ppermute | solution.py:20
  95.7 1.4 pad_maximum_fusion.1
  98.8 2.3 %fusion.23 = f32[5,8,48,129]{3,2,1,0:T(8,128)S(1)} fusion(f32[5,10,50,1]{3,2,1,0:T(8,128)S(1)} %copy.21, f32[5,1,50,128]{3,2,1,0:T(8,128)S(1)} %collective-permute-done.14, f32[5,1,50,128]{3,2,1,0:T(8,128)S(1)} %collective-permute-done.13, f32[5,8,1,128]{3,2,1,0:T(1,128)S(1)} %get-tuple-element.42, f32[5,8,48,128]{3,2,1,0:T(8,128)S(1)} %fusion.64, ...), kind=kLoop, calls=%fused_computation.42 | loop fusion | flops 3715200 | bytes 4470304 | tf_op jit(solution)/shard_map/sub | solution.py:75
  101.9 3.5 %collective-permute-start.17 = (f32[5,8,1,128]{3,2,1,0:T(1,128)S(1)}, f32[5,8,1,128]{3,2,1,0:T(1,128)S(1)}, u32[]{:S(2)}, u32[]{:S(2)}) collective-permute-start(f32[5,8,1,128]{3,2,1,0:T(1,128)S(1)} %get-tuple-element.45), channel_id=1, source_target_pairs={{0,8},{8,16},{16,24},{1,9},{9,17},{17,25},{2,10},{10,18},{18,26},{... | collective-permute-start | bytes 61448 | tf_op jit(solution)/shard_map/ppermute | solution.py:19
  106.8 4.2 %collective-permute-done.18 = f32[5,8,1,128]{3,2,1,0:T(1,128)S(1)} collective-permute-done((f32[5,8,1,128]{3,2,1,0:T(1,128)S(1)}, f32[5,8,1,128]{3,2,1,0:T(1,128)S(1)}, u32[]{:S(2)}, u32[]{:S(2)}) %collective-permute-start.18) | collective-permute-done | bytes 20512 | tf_op jit(solution)/shard_map/ppermute | solution.py:20
  111.3 1.6 collective-permute-start.20
  113.9 1.5 fusion.27
  116.7 1.5 collective-permute-done.19
  118.4 2.0 %fusion.163 = (f32[5,10,50,1]{3,2,1,0:T(8,128)}, f32[5,10,50,1]{3,2,1,0:T(8,128)}) fusion(f32[5,10,50,128]{3,2,1,0:T(8,128)S(1)} %pad_maximum_fusion.25), kind=kLoop, calls=%fused_computation.361 | loop fusion | bytes 40000 | tf_op jit(solution)/shard_map/slice | solution.py:18
  120.4 1.9 %copy.25 = f32[5,10,50,1]{2,3,1,0:T(1,128)S(1)} copy(f32[5,10,50,1]{3,2,1,0:T(8,128)} %get-tuple-element.28) | data formatting | bytes 20000 | tf_op jit(solution)/shard_map/slice | solution.py:17
  122.3 1.9 %copy.26 = f32[5,10,50,1]{2,3,1,0:T(1,128)S(1)} copy(f32[5,10,50,1]{3,2,1,0:T(8,128)} %get-tuple-element.27) | data formatting | bytes 20000 | tf_op jit(solution)/shard_map/slice | solution.py:18
  124.2 2.0 %collective-permute-start.22 = (f32[5,10,50,1]{2,3,1,0:T(1,128)S(1)}, f32[5,10,50,1]{2,3,1,0:T(1,128)S(1)}, u32[]{:S(2)}, u32[]{:S(2)}) collective-permute-start(f32[5,10,50,1]{2,3,1,0:T(1,128)S(1)} %copy.26), channel_id=1, source_target_pairs={{1,0},{2,1},{3,2},{0,3},{5,4},{6,5},{7,6},{4,7},{9,8},{10,9},{11,1... | collective-permute-start | bytes 30008 | tf_op jit(solution)/shard_map/ppermute | solution.py:20
  128.8 1.7 %copy.28 = f32[5,10,50,1]{3,2,1,0:T(8,128)} copy(f32[5,10,50,1]{2,3,1,0:T(1,128)S(1)} %collective-permute-done.22) | data formatting | bytes 20000 | tf_op jit(solution)/shard_map/ppermute | solution.py:20
  135.2 2.3 %fusion.19 = f32[5,8,48,129]{3,2,1,0:T(8,128)S(1)} fusion(f32[5,10,50,1]{3,2,1,0:T(8,128)S(1)} %copy.27, f32[5,1,50,128]{3,2,1,0:T(8,128)S(1)} %collective-permute-done.20, f32[5,1,50,128]{3,2,1,0:T(8,128)S(1)} %collective-permute-done.19, f32[5,8,1,128]{3,2,1,0:T(1,128)S(1)} %get-tuple-element.40, f32[5,8,48,128]{3,2,1,0:T(8,128)S(1)} %fusion.59, ...), kind=kLoop, calls=%fused_computation.27 | loop fusion | flops 3715200 | bytes 4470304 | tf_op jit(solution)/shard_map/sub | solution.py:75
  139.2 12.9 %render.1 = f32[1536,128]{1,0:T(8,128)} custom-call(f32[8,48,128]{2,1,0:T(8,128)} %copy-done.24, f32[8,48,128]{2,1,0:T(8,128)} %fusion.161.refs_1_, f32[4,256]{1,0:T(4,128)} %refs_2_.1, s32[8,256]{1,0:T(8,128)} %refs_3_.1), custom_call_target="tpu_custom_call" | custom-call | tf_op jit(solution)/shard_map/render/pallas_call | solution.py:142
  153.2 1.6 collective-permute-start.23
  154.8 10.1 %collective-permute-done.23 = f32[4,4,48,128]{3,2,1,0:T(8,128)S(1)} collective-permute-done((f32[4,4,48,128]{3,2,1,0:T(8,128)S(1)}, f32[4,4,48,128]{3,2,1,0:T(8,128)S(1)}, u32[]{:S(2)}, u32[]{:S(2)}) %collective-permute-start.23) | collective-permute-done | bytes 393248 | tf_op jit(solution)/shard_map/ppermute | solution.py:196
  (197 shorter events, 33.9 us)
Async XLA Ops:
  0.6 1.5 copy-start.5
  0.6 1.5 copy-start.28
  2.1 63.6 %copy-start.2 = (f32[3,8,48,128]{3,2,1,0:T(8,128)}, f32[3,8,48,128]{3,2,1,0:T(8,128)S(1)}, u32[]{:S(2)}) copy-start(f32[3,8,48,128]{3,2,1,0:T(8,128)S(1)} %get-tuple-element.53) | copy-start | bytes 1769476
  2.2 32.5 %copy-start.29 = (f32[5]{0:T(128)S(1)}, f32[5]{0:T(128)}, u32[]{:S(2)}) copy-start(f32[5]{0:T(128)} %constant.67.clone) | copy-start | bytes 64
  2.9 62.9 %copy-start.8 = (f32[1,8,48,128]{3,2,1,0:T(8,128)}, f32[1,8,48,128]{3,2,1,0:T(8,128)S(1)}, u32[]{:S(2)}) copy-start(f32[1,8,48,128]{3,2,1,0:T(8,128)S(1)} %get-tuple-element.55) | copy-start | bytes 589828
  3.0 31.6 %collective-permute-start.5 = (f32[5,8,1,128]{3,2,1,0:T(1,128)S(1)}, f32[5,8,1,128]{3,2,1,0:T(1,128)S(1)}, u32[]{:S(2)}, u32[]{:S(2)}) collective-permute-start(f32[5,8,1,128]{3,2,1,0:T(1,128)S(1)} %get-tuple-element.49), channel_id=1, source_target_pairs={{0,8},{8,16},{16,24},{1,9},{9,17},{17,25},{2,10},{10,18},{18,26},{... | collective-permute-start | bytes 61448 | tf_op jit(solution)/shard_map/ppermute | solution.py:19
  8.0 26.7 %collective-permute-start.6 = (f32[5,8,1,128]{3,2,1,0:T(1,128)S(1)}, f32[5,8,1,128]{3,2,1,0:T(1,128)S(1)}, u32[]{:S(2)}, u32[]{:S(2)}) collective-permute-start(f32[5,8,1,128]{3,2,1,0:T(1,128)S(1)} %get-tuple-element.50), channel_id=1, source_target_pairs={{8,0},{16,8},{24,16},{9,1},{17,9},{25,17},{10,2},{18,10},{26,18},{... | collective-permute-start | bytes 61448 | tf_op jit(solution)/shard_map/ppermute | solution.py:20
  9.3 3.1 %collective-permute-start = (f32[1]{0:T(128)}, f32[1]{0:T(128)}, u32[]{:S(2)}, u32[]{:S(2)}) collective-permute-start(f32[1]{0:T(128)} %bitcast.2), channel_id=1, source_target_pairs={{0,1},{1,2},{2,3},{3,0},{4,5},{5,6},{6,7},{7,4},{8,9},{9,10},{10,1... | collective-permute-start | bytes 20 | tf_op jit(solution)/shard_map/ppermute | solution.py:161
  13.6 3.7 %collective-permute-start.1 = (f32[1]{0:T(128)}, f32[1]{0:T(128)}, u32[]{:S(2)}, u32[]{:S(2)}) collective-permute-start(f32[1]{0:T(128)} %max.42), channel_id=1, source_target_pairs={{0,2},{1,3},{2,0},{3,1},{4,6},{5,7},{6,4},{7,5},{8,10},{9,11},{10,... | collective-permute-start | bytes 20 | tf_op jit(solution)/shard_map/ppermute | solution.py:161
  18.0 3.7 %collective-permute-start.2 = (f32[1]{0:T(128)}, f32[1]{0:T(128)}, u32[]{:S(2)}, u32[]{:S(2)}) collective-permute-start(f32[1]{0:T(128)} %max.43), channel_id=1, source_target_pairs={{0,4},{4,0},{1,5},{5,1},{2,6},{6,2},{3,7},{7,3},{8,12},{12,8},{9,1... | collective-permute-start | bytes 20 | tf_op jit(solution)/shard_map/ppermute | solution.py:161
  22.3 6.4 %collective-permute-start.3 = (f32[1]{0:T(128)}, f32[1]{0:T(128)}, u32[]{:S(2)}, u32[]{:S(2)}) collective-permute-start(f32[1]{0:T(128)} %max.44), channel_id=1, source_target_pairs={{0,8},{8,16},{16,24},{24,0},{1,9},{9,17},{17,25},{25,1},{2,10},{10... | collective-permute-start | bytes 20 | tf_op jit(solution)/shard_map/ppermute | solution.py:161
  29.3 4.6 %collective-permute-start.4 = (f32[1]{0:T(128)}, f32[1]{0:T(128)}, u32[]{:S(2)}, u32[]{:S(2)}) collective-permute-start(f32[1]{0:T(128)} %max.45), channel_id=1, source_target_pairs={{0,16},{8,24},{16,0},{24,8},{1,17},{9,25},{17,1},{25,9},{2,18},{10... | collective-permute-start | bytes 20 | tf_op jit(solution)/shard_map/ppermute | solution.py:161
  34.8 6.9 %copy-start.25 = (f32[5,8,1,128]{3,2,1,0:T(1,128)}, f32[5,8,1,128]{3,2,1,0:T(1,128)S(1)}, u32[]{:S(2)}) copy-start(f32[5,8,1,128]{3,2,1,0:T(1,128)S(1)} %get-tuple-element.44) | copy-start | bytes 61444
  35.0 5.2 %collective-permute-start.8 = (f32[5,1,50,128]{3,2,1,0:T(8,128)S(1)}, f32[5,1,50,128]{3,2,1,0:T(8,128)S(1)}, u32[]{:S(2)}, u32[]{:S(2)}) collective-permute-start(f32[5,1,50,128]{3,2,1,0:T(8,128)S(1)} %get-tuple-element.38), channel_id=1, source_target_pairs={{4,0},{0,4},{5,1},{1,5},{6,2},{2,6},{7,3},{3,7},{12,8},{8,12},{13,... | collective-permute-start | bytes 384008 | tf_op jit(solution)/shard_map/ppermute | solution.py:20
  36.5 5.1 %collective-permute-start.7 = (f32[5,1,50,128]{3,2,1,0:T(8,128)S(1)}, f32[5,1,50,128]{3,2,1,0:T(8,128)S(1)}, u32[]{:S(2)}, u32[]{:S(2)}) collective-permute-start(f32[5,1,50,128]{3,2,1,0:T(8,128)S(1)} %get-tuple-element.37), channel_id=1, source_target_pairs={{0,4},{4,0},{1,5},{5,1},{2,6},{6,2},{3,7},{7,3},{8,12},{12,8},{9,1... | collective-permute-start | bytes 384008 | tf_op jit(solution)/shard_map/ppermute | solution.py:19
  40.2 3.7 %copy-start.18 = (f32[5,1,50,128]{3,2,1,0:T(8,128)}, f32[5,1,50,128]{3,2,1,0:T(8,128)S(1)}, u32[]{:S(2)}) copy-start(f32[5,1,50,128]{3,2,1,0:T(8,128)S(1)} %collective-permute-done.8) | copy-start | bytes 384004
  41.7 2.1 %copy-start.21 = (f32[5,1,50,128]{3,2,1,0:T(8,128)}, f32[5,1,50,128]{3,2,1,0:T(8,128)S(1)}, u32[]{:S(2)}) copy-start(f32[5,1,50,128]{3,2,1,0:T(8,128)S(1)} %collective-permute-done.7) | copy-start | bytes 384004
  46.4 5.9 %collective-permute-start.9 = (f32[5,10,50,1]{2,3,1,0:T(1,128)}, f32[5,10,50,1]{2,3,1,0:T(1,128)}, u32[]{:S(2)}, u32[]{:S(2)}) collective-permute-start(f32[5,10,50,1]{2,3,1,0:T(1,128)} %copy.13), channel_id=1, source_target_pairs={{0,1},{1,2},{2,3},{3,0},{4,5},{5,6},{6,7},{7,4},{8,9},{9,10},{10,1... | collective-permute-start | bytes 30008 | tf_op jit(solution)/shard_map/ppermute | solution.py:19
  48.9 4.8 %collective-permute-start.10 = (f32[5,10,50,1]{2,3,1,0:T(1,128)}, f32[5,10,50,1]{2,3,1,0:T(1,128)}, u32[]{:S(2)}, u32[]{:S(2)}) collective-permute-start(f32[5,10,50,1]{2,3,1,0:T(1,128)} %copy.14), channel_id=1, source_target_pairs={{1,0},{2,1},{3,2},{0,3},{5,4},{6,5},{7,6},{4,7},{9,8},{10,9},{11,1... | collective-permute-start | bytes 30008 | tf_op jit(solution)/shard_map/ppermute | solution.py:20
  61.9 1.4 copy-start.11
  61.9 1.4 copy-start.23
  63.3 2.5 %copy-start.16 = (f32[5,8,49,128]{3,2,1,0:T(8,128)S(1)}, f32[5,8,49,128]{3,2,1,0:T(8,128)}, u32[]{:S(2)}) copy-start(f32[5,8,49,128]{3,2,1,0:T(8,128)} %fusion.31) | copy-start | bytes 3010564
  66.4 3.4 %collective-permute-start.11 = (f32[5,8,1,128]{3,2,1,0:T(1,128)S(1)}, f32[5,8,1,128]{3,2,1,0:T(1,128)S(1)}, u32[]{:S(2)}, u32[]{:S(2)}) collective-permute-start(f32[5,8,1,128]{3,2,1,0:T(1,128)S(1)} %get-tuple-element.47), channel_id=1, source_target_pairs={{0,8},{8,16},{16,24},{1,9},{9,17},{17,25},{2,10},{10,18},{18,26},{... | collective-permute-start | bytes 61448 | tf_op jit(solution)/shard_map/ppermute | solution.py:19
  68.3 5.7 %collective-permute-start.12 = (f32[5,8,1,128]{3,2,1,0:T(1,128)S(1)}, f32[5,8,1,128]{3,2,1,0:T(1,128)S(1)}, u32[]{:S(2)}, u32[]{:S(2)}) collective-permute-start(f32[5,8,1,128]{3,2,1,0:T(1,128)S(1)} %get-tuple-element.48), channel_id=1, source_target_pairs={{8,0},{16,8},{24,16},{9,1},{17,9},{25,17},{10,2},{18,10},{26,18},{... | collective-permute-start | bytes 61448 | tf_op jit(solution)/shard_map/ppermute | solution.py:20
  74.3 6.3 %collective-permute-start.14 = (f32[5,1,50,128]{3,2,1,0:T(8,128)S(1)}, f32[5,1,50,128]{3,2,1,0:T(8,128)S(1)}, u32[]{:S(2)}, u32[]{:S(2)}) collective-permute-start(f32[5,1,50,128]{3,2,1,0:T(8,128)S(1)} %get-tuple-element.36), channel_id=1, source_target_pairs={{4,0},{0,4},{5,1},{1,5},{6,2},{2,6},{7,3},{3,7},{12,8},{8,12},{13,... | collective-permute-start | bytes 384008 | tf_op jit(solution)/shard_map/ppermute | solution.py:20
  75.8 6.2 %collective-permute-start.13 = (f32[5,1,50,128]{3,2,1,0:T(8,128)S(1)}, f32[5,1,50,128]{3,2,1,0:T(8,128)S(1)}, u32[]{:S(2)}, u32[]{:S(2)}) collective-permute-start(f32[5,1,50,128]{3,2,1,0:T(8,128)S(1)} %get-tuple-element.35), channel_id=1, source_target_pairs={{0,4},{4,0},{1,5},{5,1},{2,6},{6,2},{3,7},{7,3},{8,12},{12,8},{9,1... | collective-permute-start | bytes 384008 | tf_op jit(solution)/shard_map/ppermute | solution.py:19
  86.1 5.7 %collective-permute-start.15 = (f32[5,10,50,1]{2,3,1,0:T(1,128)S(1)}, f32[5,10,50,1]{2,3,1,0:T(1,128)S(1)}, u32[]{:S(2)}, u32[]{:S(2)}) collective-permute-start(f32[5,10,50,1]{2,3,1,0:T(1,128)S(1)} %copy.19), channel_id=1, source_target_pairs={{0,1},{1,2},{2,3},{3,0},{4,5},{5,6},{6,7},{7,4},{8,9},{9,10},{10,1... | collective-permute-start | bytes 30008 | tf_op jit(solution)/shard_map/ppermute | solution.py:19
  88.1 4.4 %collective-permute-start.16 = (f32[5,10,50,1]{2,3,1,0:T(1,128)S(1)}, f32[5,10,50,1]{2,3,1,0:T(1,128)S(1)}, u32[]{:S(2)}, u32[]{:S(2)}) collective-permute-start(f32[5,10,50,1]{2,3,1,0:T(1,128)S(1)} %copy.20), channel_id=1, source_target_pairs={{1,0},{2,1},{3,2},{0,3},{5,4},{6,5},{7,6},{4,7},{9,8},{10,9},{11,1... | collective-permute-start | bytes 30008 | tf_op jit(solution)/shard_map/ppermute | solution.py:20
  94.2 1.5 copy-start
  98.8 2.3 %copy-start.3 = (f32[3,8,48,128]{3,2,1,0:T(8,128)S(1)}, f32[3,8,48,128]{3,2,1,0:T(8,128)}, u32[]{:S(2)}) copy-start(f32[3,8,48,128]{3,2,1,0:T(8,128)} %copy-done.2) | copy-start | bytes 1769476
  98.8 2.3 %copy-start.6 = (f32[8,48,128]{2,1,0:T(8,128)S(1)}, f32[8,48,128]{2,1,0:T(8,128)}, u32[]{:S(2)}) copy-start(f32[8,48,128]{2,1,0:T(8,128)} %param.11) | copy-start | bytes 589828
  98.8 2.3 %copy-start.9 = (f32[1,8,48,128]{3,2,1,0:T(8,128)S(1)}, f32[1,8,48,128]{3,2,1,0:T(8,128)}, u32[]{:S(2)}) copy-start(f32[1,8,48,128]{3,2,1,0:T(8,128)} %copy-done.8) | copy-start | bytes 589828
  98.8 2.3 %copy-start.13 = (f32[5,9,48,128]{3,2,1,0:T(8,128)S(1)}, f32[5,9,48,128]{3,2,1,0:T(8,128)}, u32[]{:S(2)}) copy-start(f32[5,9,48,128]{3,2,1,0:T(8,128)} %fusion.41) | copy-start | bytes 3317764
  98.8 2.3 %copy-start.15 = (f32[5,8,49,128]{3,2,1,0:T(8,128)S(1)}, f32[5,8,49,128]{3,2,1,0:T(8,128)}, u32[]{:S(2)}) copy-start(f32[5,8,49,128]{3,2,1,0:T(8,128)} %fusion.29) | copy-start | bytes 3010564
  101.9 5.0 %collective-permute-start.17 = (f32[5,8,1,128]{3,2,1,0:T(1,128)S(1)}, f32[5,8,1,128]{3,2,1,0:T(1,128)S(1)}, u32[]{:S(2)}, u32[]{:S(2)}) collective-permute-start(f32[5,8,1,128]{3,2,1,0:T(1,128)S(1)} %get-tuple-element.45), channel_id=1, source_target_pairs={{0,8},{8,16},{16,24},{1,9},{9,17},{17,25},{2,10},{10,18},{18,26},{... | collective-permute-start | bytes 61448 | tf_op jit(solution)/shard_map/ppermute | solution.py:19
  105.4 5.7 %collective-permute-start.18 = (f32[5,8,1,128]{3,2,1,0:T(1,128)S(1)}, f32[5,8,1,128]{3,2,1,0:T(1,128)S(1)}, u32[]{:S(2)}, u32[]{:S(2)}) collective-permute-start(f32[5,8,1,128]{3,2,1,0:T(1,128)S(1)} %get-tuple-element.46), channel_id=1, source_target_pairs={{8,0},{16,8},{24,16},{9,1},{17,9},{25,17},{10,2},{18,10},{26,18},{... | collective-permute-start | bytes 61448 | tf_op jit(solution)/shard_map/ppermute | solution.py:20
  111.3 5.4 %collective-permute-start.20 = (f32[5,1,50,128]{3,2,1,0:T(8,128)S(1)}, f32[5,1,50,128]{3,2,1,0:T(8,128)S(1)}, u32[]{:S(2)}, u32[]{:S(2)}) collective-permute-start(f32[5,1,50,128]{3,2,1,0:T(8,128)S(1)} %get-tuple-element.34), channel_id=1, source_target_pairs={{4,0},{0,4},{5,1},{1,5},{6,2},{2,6},{7,3},{3,7},{12,8},{8,12},{13,... | collective-permute-start | bytes 384008 | tf_op jit(solution)/shard_map/ppermute | solution.py:20
  112.9 5.4 %collective-permute-start.19 = (f32[5,1,50,128]{3,2,1,0:T(8,128)S(1)}, f32[5,1,50,128]{3,2,1,0:T(8,128)S(1)}, u32[]{:S(2)}, u32[]{:S(2)}) collective-permute-start(f32[5,1,50,128]{3,2,1,0:T(8,128)S(1)} %get-tuple-element.33), channel_id=1, source_target_pairs={{0,4},{4,0},{1,5},{5,1},{2,6},{6,2},{3,7},{7,3},{8,12},{12,8},{9,1... | collective-permute-start | bytes 384008 | tf_op jit(solution)/shard_map/ppermute | solution.py:19
  122.3 5.9 %collective-permute-start.21 = (f32[5,10,50,1]{2,3,1,0:T(1,128)S(1)}, f32[5,10,50,1]{2,3,1,0:T(1,128)S(1)}, u32[]{:S(2)}, u32[]{:S(2)}) collective-permute-start(f32[5,10,50,1]{2,3,1,0:T(1,128)S(1)} %copy.25), channel_id=1, source_target_pairs={{0,1},{1,2},{2,3},{3,0},{4,5},{5,6},{6,7},{7,4},{8,9},{9,10},{10,1... | collective-permute-start | bytes 30008 | tf_op jit(solution)/shard_map/ppermute | solution.py:19
  124.2 4.6 %collective-permute-start.22 = (f32[5,10,50,1]{2,3,1,0:T(1,128)S(1)}, f32[5,10,50,1]{2,3,1,0:T(1,128)S(1)}, u32[]{:S(2)}, u32[]{:S(2)}) collective-permute-start(f32[5,10,50,1]{2,3,1,0:T(1,128)S(1)} %copy.26), channel_id=1, source_target_pairs={{1,0},{2,1},{3,2},{0,3},{5,4},{6,5},{7,6},{4,7},{9,8},{10,9},{11,1... | collective-permute-start | bytes 30008 | tf_op jit(solution)/shard_map/ppermute | solution.py:20
  130.5 1.5 copy-start.1
  135.1 2.3 %copy-start.4 = (f32[3,8,48,128]{3,2,1,0:T(8,128)S(1)}, f32[3,8,48,128]{3,2,1,0:T(8,128)}, u32[]{:S(2)}) copy-start(f32[3,8,48,128]{3,2,1,0:T(8,128)} %copy-done.2) | copy-start | bytes 1769476
  135.1 2.3 %copy-start.7 = (f32[8,48,128]{2,1,0:T(8,128)S(1)}, f32[8,48,128]{2,1,0:T(8,128)}, u32[]{:S(2)}) copy-start(f32[8,48,128]{2,1,0:T(8,128)} %param.11) | copy-start | bytes 589828
  135.1 2.3 %copy-start.10 = (f32[1,8,48,128]{3,2,1,0:T(8,128)S(1)}, f32[1,8,48,128]{3,2,1,0:T(8,128)}, u32[]{:S(2)}) copy-start(f32[1,8,48,128]{3,2,1,0:T(8,128)} %copy-done.8) | copy-start | bytes 589828
  135.2 2.3 %copy-start.12 = (f32[5,9,48,128]{3,2,1,0:T(8,128)S(1)}, f32[5,9,48,128]{3,2,1,0:T(8,128)}, u32[]{:S(2)}) copy-start(f32[5,9,48,128]{3,2,1,0:T(8,128)} %fusion.37) | copy-start | bytes 3317764
  135.2 2.3 %copy-start.14 = (f32[5,8,49,128]{3,2,1,0:T(8,128)S(1)}, f32[5,8,49,128]{3,2,1,0:T(8,128)}, u32[]{:S(2)}) copy-start(f32[5,8,49,128]{3,2,1,0:T(8,128)} %fusion.27) | copy-start | bytes 3010564
  138.2 13.9 %copy-start.17 = (f32[5,8,48,128]{3,2,1,0:T(8,128)}, f32[5,8,48,128]{3,2,1,0:T(8,128)S(1)}, u32[]{:S(2)}) copy-start(f32[5,8,48,128]{3,2,1,0:T(8,128)S(1)} %fusion.52) | copy-start | bytes 2949124
  153.2 11.7 %collective-permute-start.23 = (f32[4,4,48,128]{3,2,1,0:T(8,128)S(1)}, f32[4,4,48,128]{3,2,1,0:T(8,128)S(1)}, u32[]{:S(2)}, u32[]{:S(2)}) collective-permute-start(f32[4,4,48,128]{3,2,1,0:T(8,128)S(1)} %bitcast.247), channel_id=1, source_target_pairs={{0,4},{4,0},{1,5},{5,1},{2,6},{6,2},{3,7},{7,3},{8,12},{12,8},{9,1... | collective-permute-start | bytes 1179656 | tf_op jit(solution)/shard_map/ppermute | solution.py:196
  (6 other events, 6.5 us)

commit v2 on v1

v2 whole, which is shorter than its diff:
```python
import functools

import jax
import jax.numpy as jnp
from jax import lax
from jax.experimental import pallas as pl
from jax.experimental.pallas import tpu as pltpu
from jax.sharding import PartitionSpec as P

HEAT_RATIO = 1.4
COURANT = 0.8
REACH = 3
WINDOW = 3 * REACH
SUB = 8
VMEM = pl.BlockSpec(memory_space=pltpu.VMEM)


def ahead(values, distance=1):
    return pltpu.roll(values, values.shape[-1] - distance, axis=values.ndim - 1)


def behind(values, distance=1):
    return pltpu.roll(values, distance, axis=values.ndim - 1)


def turned(values, shift):
    return pltpu.roll(values, shift % values.shape[-1], axis=values.ndim - 1)


def padded_rows(rows):
    return -(-(rows + 2 * REACH) // SUB) * SUB


def primitives(rho, mx, my, mz, energy):
    inverse = 1.0 / rho
    ux, uy, uz = mx * inverse, my * inverse, mz * inverse
    pressure = (HEAT_RATIO - 1.0) * (energy - 0.5 * (mx * ux + my * uy + mz * uz))
    sound = jnp.sqrt(HEAT_RATIO * pressure * inverse)
    return ux, uy, uz, pressure, sound


def fluxes(state, normal, pressure, component):
    rho, mx, my, mz, energy = state
    rows = [state[component], mx * normal, my * normal, mz * normal, (energy + pressure) * normal]
    rows[component] = rows[component] + pressure
    return rows


def face(flux_a, flux_b, state_a, state_b, signal_a, signal_b):
    fastest = jnp.maximum(signal_a, signal_b)
    return [
        (fa + fb) - fastest * (ub - ua)
        for fa, fb, ua, ub in zip(flux_a, flux_b, state_a, state_b)
    ]


def opening_kernel(rho_ref, vel_ref, pre_ref, state_ref, zpay_ref, low_ref, high_ref, top_ref):
    planes, rows, width = rho_ref.shape
    edge = list(range(REACH)) + list(range(planes - REACH, planes))
    fastest = None
    for z in range(planes):
        rho, p = rho_ref[z], pre_ref[z]
        v = [vel_ref[i, z] for i in range(3)]
        signal = jnp.abs(v[0]) + jnp.abs(v[1]) + jnp.abs(v[2]) + 3.0 * jnp.sqrt(HEAT_RATIO * p / rho)
        signal = jnp.max(signal.reshape(rows // SUB, SUB, width), axis=0)
        fastest = signal if fastest is None else jnp.maximum(fastest, signal)
        kinetic = 0.5 * rho * (v[0] * v[0] + v[1] * v[1] + v[2] * v[2])
        fields = [rho, rho * v[0], rho * v[1], rho * v[2], p / (HEAT_RATIO - 1.0) + kinetic]
        for f in range(5):
            state_ref[f, z] = fields[f]
            if z in edge:
                zpay_ref[f, edge.index(z)] = fields[f]
            at = (f * planes + z) * REACH
            low_ref[at : at + REACH, :] = fields[f][:REACH]
            high_ref[at : at + REACH, :] = fields[f][rows - REACH :]
    top_ref[...] = fastest


def opening(density, velocity, pressure):
    planes, rows, width = density.shape
    f32 = jnp.float32
    return pl.pallas_call(
        opening_kernel,
        out_shape=[
            jax.ShapeDtypeStruct((5, planes, rows, width), f32),
            jax.ShapeDtypeStruct((5, 2 * REACH, rows, width), f32),
            jax.ShapeDtypeStruct((5 * planes * REACH, width), f32),
            jax.ShapeDtypeStruct((5 * planes * REACH, width), f32),
            jax.ShapeDtypeStruct((SUB, width), f32),
        ],
        in_specs=[VMEM] * 3,
        out_specs=[VMEM] * 5,
        name="opening",
    )(density, velocity, pressure)


def window_kernel(state_ref, low_ref, high_ref, wide_ref, right_ref, left_ref):
    planes, rows, width = state_ref.shape[1:]
    total = wide_ref.shape[2]
    group, groups = lax.axis_index("group"), lax.axis_size("group")
    lane = lax.broadcasted_iota(jnp.int32, (SUB, width), 1)
    for f in range(5):
        sign = -1.0 if f == 1 else 1.0
        for z in range(planes):
            at = (f * planes + z) * REACH
            wide_ref[f, z, REACH : REACH + rows, :] = state_ref[f, z]
            mirrored = [state_ref[f, z, r : r + 1, :] * sign for r in range(REACH - 1, -1, -1)]
            below = jnp.where(group == 0, jnp.concatenate(mirrored, axis=0), low_ref[at : at + REACH, :])
            wide_ref[f, z, :REACH, :] = below
            mirrored = [state_ref[f, z, rows - 1 - r : rows - r, :] * sign for r in range(REACH)]
            above = jnp.where(
                group == groups - 1, jnp.concatenate(mirrored, axis=0), high_ref[at : at + REACH, :]
            )
            wide_ref[f, z, REACH + rows : 2 * REACH + rows, :] = above

    def fields(f, carry):
        for t in range(total // SUB):
            cut = slice(SUB * t, SUB * (t + 1))
            right = jnp.zeros((SUB, width), jnp.float32)
            left = right
            for z in range(planes):
                start = WINDOW * (z + REACH)
                inside = (lane >= start) & (lane < start + WINDOW)
                values = wide_ref[f, z, cut, :]
                right = jnp.where(inside, turned(values, start - (width - 2 * REACH)), right)
                left = jnp.where(inside, turned(values, start - (width - REACH)), left)
            right_ref[f, cut, :] = right
            left_ref[f, cut, :] = left
        return carry

    lax.fori_loop(0, 5, fields, 0)


def windows(state, low, high):
    planes, rows, width = state.shape[1:]
    total = padded_rows(rows)
    f32 = jnp.float32
    return pl.pallas_call(
        window_kernel,
        out_shape=[
            jax.ShapeDtypeStruct((5, planes, total, width), f32),
            jax.ShapeDtypeStruct((5, total, width), f32),
            jax.ShapeDtypeStruct((5, total, width), f32),
        ],
        in_specs=[VMEM] * 3,
        out_specs=[VMEM] * 3,
        name="windows",
    )(state, low, high)


def strip_kernel(wide_ref, right_ref, left_ref, from_right, from_left, strips_ref, pay_ref):
    planes, total, width = wide_ref.shape[1:]
    rows = total - 2 * REACH - (total - 2 * REACH) % SUB
    lane = lax.broadcasted_iota(jnp.int32, (SUB, width), 1)
    column = lane % WINDOW
    span = WINDOW * REACH
    first, last = WINDOW * REACH, WINDOW * planes
    far = WINDOW * (REACH + planes)
    for f in range(5):
        for t in range(total // SUB):
            cut = slice(SUB * t, SUB * (t + 1))
            right = jnp.where(column >= 2 * REACH, from_right[f, cut, :], right_ref[f, cut, :])
            left = jnp.where(column < REACH, from_left[f, cut, :], left_ref[f, cut, :])
            strips_ref[0, f, cut, :] = left
            strips_ref[1, f, cut, :] = right
            sent = jnp.where(lane < span, turned(right, -last), left)
            pay_ref[f, cut, :] = jnp.where(lane >= far, turned(right, far - first), sent)
        low, high = REACH - 1, REACH + rows
        for side, (near, next_one) in enumerate(((0, 1), (planes - 1, planes - 2))):
            at = total + SUB * side
            pay_ref[f, at : at + 2, :] = wide_ref[f, near, low - 1 : low + 1, :]
            pay_ref[f, at + 2 : at + 3, :] = wide_ref[f, next_one, low : low + 1, :]
            pay_ref[f, at + 3 : at + 5, :] = wide_ref[f, near, high : high + 2, :]
            pay_ref[f, at + 5 : at + 6, :] = wide_ref[f, next_one, high : high + 1, :]
            pay_ref[f, at + 6 : at + 8, :] = jnp.zeros((2, width), jnp.float32)


def strips_of(wide, right, left, from_right, from_left):
    planes, total, width = wide.shape[1:]
    f32 = jnp.float32
    return pl.pallas_call(
        strip_kernel,
        out_shape=[
            jax.ShapeDtypeStruct((2, 5, total, width), f32),
            jax.ShapeDtypeStruct((5, total + 2 * SUB, width), f32),
        ],
        in_specs=[VMEM] * 5,
        out_specs=[VMEM] * 2,
        name="strips",
    )(wide, right, left, from_right, from_left)


def blend(section, base, here, change):
    if section == 0:
        return here + change
    if section == 1:
        return 0.75 * base + 0.25 * (here + change)
    return base * (1.0 / 3.0) + (2.0 / 3.0) * (here + change)


def section_kernel(shared, *refs):
    if shared:
        wide_ref, zone_ref, pay_ref, strips_ref, top_ref = refs[:5]
        zone_refs, pay_refs = (zone_ref, zone_ref), (pay_ref, pay_ref)
        rest = refs[5:]
    else:
        wide_ref, strips_ref, top_ref = refs[0], refs[5], refs[6]
        zone_refs, pay_refs = refs[1:3], refs[3:5]
        rest = refs[7:]
    out_ref, heat_ref, main, strip, fx, fz, fy, gz, gx, acc = rest
    planes, total, width = wide_ref.shape[1:]
    rows = out_ref.shape[2]
    tiles = total // SUB
    lane = lax.broadcasted_iota(jnp.int32, (SUB, width), 1)
    far = WINDOW * (REACH + planes)
    for f in range(5):
        for z in range(planes):
            main[0, f, z + REACH, :total, :] = wide_ref[f, z]
        for z in range(REACH):
            main[0, f, z, REACH : REACH + rows, :] = zone_refs[0][f, REACH + z]
            main[0, f, planes + REACH + z, REACH : REACH + rows, :] = zone_refs[1][f, z]
        low, high = REACH - 1, REACH + rows
        for pay, near, next_one, at in (
            (pay_refs[1], planes + REACH, planes + REACH + 1, total),
            (pay_refs[0], REACH - 1, REACH - 2, total + SUB),
        ):
            main[0, f, near, low - 1 : low + 1, :] = pay[f, at : at + 2, :]
            main[0, f, next_one, low : low + 1, :] = pay[f, at + 2 : at + 3, :]
            main[0, f, near, high : high + 2, :] = pay[f, at + 3 : at + 5, :]
            main[0, f, next_one, high : high + 1, :] = pay[f, at + 5 : at + 6, :]
        for t in range(tiles):
            cut = slice(SUB * t, SUB * (t + 1))
            before, after = pay_refs[0][f, cut, :], pay_refs[1][f, cut, :]
            span = WINDOW * REACH
            left = jnp.where(lane < span, turned(before, -WINDOW * planes), strips_ref[0, f, cut, :])
            strip[0, 0, f, cut, :] = jnp.where(lane >= far, turned(after, far - span), left)
            right = jnp.where(lane < span, before, strips_ref[1, f, cut, :])
            strip[0, 1, f, cut, :] = jnp.where(lane >= far, after, right)
    half = jnp.broadcast_to(0.5 * COURANT / jnp.max(top_ref[...], keepdims=True), (SUB, width))

    def along_y(state, uy, pressure, signal):
        flux = fluxes(state, uy, pressure, 2)
        other = [ahead(v) for v in state]
        flux_other = fluxes(other, ahead(uy), ahead(pressure), 2)
        g = face(flux, flux_other, state, other, signal, ahead(signal))
        return [behind(v) - v for v in g]

    def x_faces(load):
        for t in range(tiles):
            here, there = slice(SUB * t, SUB * (t + 1)), slice(SUB * t + 1, SUB * (t + 1) + 1)
            a, b = load(here), load(there)
            g = face(a[1], b[1], a[0], b[0], a[2], b[2])
            for f in range(5):
                gx[f, SUB * (t + 1) : SUB * (t + 2), :] = g[f]

    def x_change(f, t):
        return (
            gx[f, SUB * (t + 1) - 1 : SUB * (t + 2) - 1, :] - gx[f, SUB * (t + 1) : SUB * (t + 2), :]
        )

    def strip_section(section, side):
        for t in range(tiles):
            cut = slice(SUB * t, SUB * (t + 1))
            state = [strip[section, side, f, cut, :] for f in range(5)]
            ux, uy, uz, pressure, sound = primitives(*state)
            for f, v in enumerate(fluxes(state, ux, pressure, 1)):
                fx[0, f, cut, :] = v
            fx[0, 5, cut, :] = jnp.abs(ux) + sound
            change = along_y(state, uy, pressure, jnp.abs(uy) + sound)
            signal = jnp.abs(uz) + sound
            other = [ahead(v, WINDOW) for v in state]
            g = face(
                fluxes(state, uz, pressure, 3),
                fluxes(other, ahead(uz, WINDOW), ahead(pressure, WINDOW), 3),
                state,
                other,
                signal,
                ahead(signal, WINDOW),
            )
            for f in range(5):
                acc[f, cut, :] = change[f] + (behind(g[f], WINDOW) - g[f])

        def load(cut):
            state = [strip[section, side, f, cut, :] for f in range(5)]
            return state, [fx[0, f, cut, :] for f in range(5)], fx[0, 5, cut, :]

        x_faces(load)
        for t in range(tiles):
            cut = slice(SUB * t, SUB * (t + 1))
            for f in range(5):
                change = half * (acc[f, cut, :] + x_change(f, t))
                here, base = strip[section, side, f, cut, :], strip[0, side, f, cut, :]
                strip[section + 1, side, f, cut, :] = blend(section, base, here, change)

    def plane_values(section, z, slot, t):
        cut = slice(SUB * t, SUB * (t + 1))
        state = [main[section, f, z, cut, :] for f in range(5)]
        ux, uy, uz, pressure, sound = primitives(*state)
        for f, v in enumerate(fluxes(state, ux, pressure, 1)):
            fx[slot, f, cut, :] = v
        fx[slot, 5, cut, :] = jnp.abs(ux) + sound
        fy[slot, 0, cut, :] = uy
        fy[slot, 1, cut, :] = pressure
        fy[slot, 2, cut, :] = jnp.abs(uy) + sound
        flux, signal = fluxes(state, uz, pressure, 3), jnp.abs(uz) + sound
        for f, v in enumerate(flux):
            fz[slot, f, cut, :] = v
        fz[slot, 5, cut, :] = signal
        return state, flux, signal

    def main_section(section, first, last):
        for t in range(tiles):
            plane_values(section, first - 1, (first - 1) % 2, t)

        def plane(z, carry):
            slot = z % 2
            for t in range(tiles):
                cut = slice(SUB * t, SUB * (t + 1))
                state = [main[section, f, z, cut, :] for f in range(5)]
                other, flux_other, signal_other = plane_values(section, z + 1, 1 - slot, t)
                flux = [fz[slot, f, cut, :] for f in range(5)]
                g = face(flux, flux_other, state, other, fz[slot, 5, cut, :], signal_other)
                for f in range(5):
                    acc[f, cut, :] = gz[f, cut, :] - g[f]
                    gz[f, cut, :] = g[f]

            def rest_of_plane():
                def load(cut):
                    state = [main[section, f, z, cut, :] for f in range(5)]
                    return state, [fx[slot, f, cut, :] for f in range(5)], fx[slot, 5, cut, :]

                x_faces(load)
                for t in range(tiles):
                    cut = slice(SUB * t, SUB * (t + 1))
                    state = [main[section, f, z, cut, :] for f in range(5)]
                    sides = along_y(state, *[fy[slot, i, cut, :] for i in range(3)])
                    for f in range(5):
                        change = half * (acc[f, cut, :] + x_change(f, t) + sides[f])
                        base = main[0, f, z, cut, :]
                        main[section + 1, f, z, cut, :] = blend(section, base, state[f], change)

            pl.when(z >= first)(rest_of_plane)
            return carry

        lax.fori_loop(first - 1, last, plane, 0)

    for section in range(3):
        for side in range(2):
            strip_section(section, side)
        main_section(section, 1 + section, planes + 2 * REACH - 1 - section)
    column = lane % WINDOW
    for f in range(5):
        for t in range(rows // SUB):
            cut = slice(SUB * t + REACH, SUB * (t + 1) + REACH)
            edge = jnp.where(
                column < 2 * REACH, strip[3, 1, f, cut, :], behind(strip[3, 0, f, cut, :], REACH)
            )
            for z in range(planes):
                placed = turned(edge, width - REACH - (WINDOW * (z + REACH) + REACH))
                inner = main[3, f, z + REACH, cut, :]
                out_ref[f, z, SUB * t : SUB * (t + 1), :] = jnp.where(
                    (lane < REACH) | (lane >= width - REACH), placed, inner
                )
    for z in range(planes):
        state = [out_ref[f, z] for f in range(5)]
        heat_ref[z] = primitives(*state)[3] / state[0]


def sections(wide, zones, pays, strips, top, rows):
    planes, total, width = wide.shape[1:]
    f32 = jnp.float32
    shared = len(zones) == 1
    tall, deep = total + SUB, planes + 2 * REACH
    args = [wide, *zones, *pays, strips, top]
    return pl.pallas_call(
        functools.partial(section_kernel, shared),
        out_shape=[
            jax.ShapeDtypeStruct((5, planes, rows, width), f32),
            jax.ShapeDtypeStruct((planes, rows, width), f32),
        ],
        in_specs=[VMEM] * len(args),
        out_specs=[VMEM] * 2,
        scratch_shapes=[
            pltpu.VMEM((4, 5, deep, tall, width), f32),
            pltpu.VMEM((4, 2, 5, tall, width), f32),
            pltpu.VMEM((2, 6, tall, width), f32),
            pltpu.VMEM((2, 6, total, width), f32),
            pltpu.VMEM((2, 3, total, width), f32),
            pltpu.VMEM((5, total, width), f32),
            pltpu.VMEM((5, tall, width), f32),
            pltpu.VMEM((5, total, width), f32),
        ],
        name="sections",
    )(*args)


def lanes(values, index):
    return jnp.take_along_axis(values, index, axis=1)

def render_kernel(scale, rho_ref, heat_ref, palette_ref, index_ref, out_ref, table, ke, ko, we, wo):
    planes, rows, width = rho_ref.shape
    count_tf, bins = index_ref.shape
    half = bins // 2
    lane = lax.broadcasted_iota(jnp.int32, (count_tf, half), 1)
    low, high = index_ref[:, :half], index_ref[:, half:]
    for parity in range(2):
        at = lane * 2 + parity
        inside = jnp.where(at < half, at, at - half)
        colour = jnp.where(at < half, lanes(low, inside), lanes(high, inside))
        wrapped = jnp.where(colour < half, colour, colour - half)
        for c in range(4):
            first = jnp.broadcast_to(palette_ref[c:c+1, :half], (count_tf, half))
            second = jnp.broadcast_to(palette_ref[c:c+1, half:], (count_tf, half))
            table[c, parity] = jnp.where(colour < half, lanes(first, wrapped), lanes(second, wrapped))
    def prepare(z, _):
        position = jnp.clip(rho_ref[z] - 0.5, 0.0, 1.0) * (bins - 1)
        cell = jnp.minimum(position.astype(jnp.int32), bins - 2)
        even = (cell + 1) >> 1
        odd = cell >> 1
        ke[z] = even
        ko[z] = odd
        we[z] = 1.0 - jnp.abs(position - (2 * even).astype(jnp.float32))
        wo[z] = 1.0 - jnp.abs(position - (2 * odd + 1).astype(jnp.float32))
        return 0
    lax.fori_loop(0, planes, prepare, 0)
    tables = [[table[c, p] for p in range(2)] for c in range(4)]
    def ray(x, _):
        trans = jnp.ones((count_tf, width), jnp.float32)
        light = [jnp.zeros((count_tf, width), jnp.float32) for _ in range(3)]
        for z in range(planes):
            def wide(ref):
                return jnp.broadcast_to(ref[z, pl.ds(x, 1), :], (count_tf, width))
            ie, io, fe, fo = wide(ke), wide(ko), wide(we), wide(wo)
            looked = [lanes(tables[c][0], ie) * fe + lanes(tables[c][1], io) * fo for c in range(4)]
            passed = jnp.exp(looked[3] * (wide(rho_ref) * -scale))
            weight = trans * (1.0 - passed) * wide(heat_ref)
            light = [light[c] + looked[c] * weight for c in range(3)]
            trans = trans * passed
        for c, values in enumerate(light + [trans]):
            out_ref[pl.ds(c * rows + x, count_tf, stride=4 * rows), :] = values
        return 0
    lax.fori_loop(0, rows, ray, 0)

def render(rho, heat, palette, index, scale):
    planes, rows, width = rho.shape
    count_tf, bins = index.shape
    out = pl.pallas_call(
        lambda *refs: render_kernel(scale, *refs),
        out_shape=jax.ShapeDtypeStruct((count_tf * 4 * rows, width), jnp.float32),
        in_specs=[pl.BlockSpec(memory_space=pltpu.VMEM)] * 4,
        out_specs=pl.BlockSpec(memory_space=pltpu.VMEM),
        scratch_shapes=[pltpu.VMEM((4, 2, count_tf, bins // 2), jnp.float32)]
        + [pltpu.VMEM((planes, rows, width), jnp.int32)] * 2
        + [pltpu.VMEM((planes, rows, width), jnp.float32)] * 2,
        name="render",
    )(rho, heat, palette, index)
    return out.reshape(count_tf, 4, rows, width)


def largest(value, axes):
    for axis in axes:
        size = lax.axis_size(axis)
        step = 1
        while step < size:
            route = [(i, (i + step) % size) for i in range(size)]
            value = jnp.maximum(value, lax.ppermute(value, axis, route))
            step *= 2
    return value


def composed(shares):
    light, passed = None, None
    for d in range(shares.shape[0]):
        slab = shares[d]
        light = slab[:, :3] if d == 0 else light + passed * slab[:, :3]
        passed = slab[:, 3:] if d == 0 else passed * slab[:, 3:]
    return light


def exchanged(shares):
    depth = lax.axis_size("depth")
    count_tf = shares.shape[0]
    per_dev = count_tf // depth
    parts = shares.reshape((depth, per_dev) + shares.shape[1:])
    if depth == 2:
        me = lax.axis_index("depth")
        mine = jnp.where(me == 0, parts[0], parts[1])
        other = lax.ppermute(jnp.where(me == 0, parts[1], parts[0]), "depth", [(0, 1), (1, 0)])
        front = jnp.where(me == 0, mine, other)
        back = jnp.where(me == 0, other, mine)
        return front[:, :3] + front[:, 3:] * back[:, :3]
    return composed(lax.all_to_all(parts, "depth", 0, 0, tiled=True))


def along(axis, distance, wrap):
    size = lax.axis_size(axis)
    if wrap:
        return [(i, (i + distance) % size) for i in range(size)]
    return [(i, i + distance) for i in range(size) if 0 <= i + distance < size]


def shards(density, velocity, pressure, palette, palette_index):
    depth = lax.axis_size("depth")
    planes, rows = density.shape[:2]
    state, zone, low, high, top = opening(density, velocity, pressure)

    def both_ways(block):
        if depth == 2:
            return (lax.ppermute(block, "depth", along("depth", 1, True)),)
        return tuple(lax.ppermute(block, "depth", along("depth", d, True)) for d in (1, -1))

    zones = both_ways(zone)
    from_below = lax.ppermute(high, "group", along("group", 1, False))
    from_above = lax.ppermute(low, "group", along("group", -1, False))
    wide, right, left = windows(state, from_below, from_above)
    from_right = lax.ppermute(right, "image", along("image", -1, True))
    from_left = lax.ppermute(left, "image", along("image", 1, True))
    strips, pay = strips_of(wide, right, left, from_right, from_left)
    pays = both_ways(pay)
    top = largest(top, ("image", "group", "depth"))
    fluid_state, heat = sections(wide, zones, pays, strips, top, rows)
    shares = render(fluid_state[0], heat, palette, palette_index, 2.0 / (planes * depth))
    return (fluid_state, exchanged(shares))


def solution(mesh):
    return jax.shard_map(
        shards,
        mesh=mesh,
        in_specs=(
            P("depth", "group", "image"),
            P(None, "depth", "group", "image"),
            P("depth", "group", "image"),
            P(),
            P(),
        ),
        out_specs=(P(None, "depth", "group", "image"), P("depth", None, "group", "image")),
        check_vma=False,
    )
```

time: 167 us -> 95.3 us (0.57)
  other arithmetic: 40.2 us -> 2.58 us
  Pallas kernels: 12.9 us -> 40.4 us
  local copies, waits for them, and re-layouts: 29.7 us -> 3.83 us
  starting transfers between devices: 40 us -> 14.8 us
  between operations: 5.52 us -> 0.7 us
  waiting for transfers between devices: 37.4 us -> 32.7 us
    pallas_call x0 -> x4, Pallas kernels: none -> 27.5 us  [the longest x1 19.5 us: sections(): pl.pallas_call(functools.partial(section_kernel, shared), out_shape=[jax....]
    slice x15 -> x0, local copies, waits for them, and re-layouts: 18.7 us -> none  [the longest x6 12.3 us: extended(): first = lax.slice_in_dim(array, 0, width, axis=dim)]
    ppermute x18 -> x6, starting transfers between devices: 26.3 us -> 8.78 us  [the longest x2 3.5 us: both_ways(): return (lax.ppermute(block, 'depth', along('depth', 1, True)),)]
    sub x9 -> x0, other arithmetic: 14.3 us -> none  [tendency(): 0.5 * (leading(fluxes, direction) + trailing(fluxes, direction))]
    ppermute x6 -> x0, local copies, waits for them, and re-layouts: 8.52 us -> none  [the longest x3 5.93 us: extended(): after = lax.ppermute(first, axis, down)]
    concatenate x10 -> x0, other arithmetic: 8.22 us -> none  [the longest x6 7.77 us: extended(): array = jnp.concatenate([before, array, after], axis=dim)]
    ppermute x5, starting transfers between devices: 12.2 us -> 4.51 us  [largest(): value = jnp.maximum(value, lax.ppermute(value, axis, route))]
    ppermute x18 -> x6, waiting for transfers between devices: 17.9 us -> 10.7 us  [the longest x1 4.16 us: shards(): from_above = lax.ppermute(low, 'group', along('group', -1, False))]
  transfers between devices with their start and end apart: 24 -> 12, of which waited for: 15 -> 10; matrix products, arithmetic and copies ran while one was open for 12% -> 1% of each run, Pallas kernels for 0% -> 6%
where the time goes in v2:
time: 95.3 us; the launch traced here: 95 us
  Pallas kernels  40.4 us (42%)
  waiting for transfers between devices  32.7 us (34%)
  starting transfers between devices  14.8 us (16%)
  local copies, waits for them, and re-layouts  3.83 us (4%)
  other arithmetic  2.58 us (3%)
    pallas_call x1, Pallas kernels, sections(): pl.pallas_call(functools.partial(section_kernel, shared), out_shape=[jax....  19.5 us
    ppermute x5, waiting for transfers between devices, largest(): value = jnp.maximum(value, lax.ppermute(value, axis, route))  15.6 us
    pallas_call x1, Pallas kernels, render(): pl.pallas_call(lambda *refs: render_kernel(scale, *refs), out_shape=jax.S...  12.9 us
    ppermute x1, waiting for transfers between devices, exchanged(): lax.ppermute(jnp.where(me == 0, parts[1], parts[0]), 'depth', [(0, 1), (1...  6.29 us
    ppermute x5, starting transfers between devices, largest(): value = jnp.maximum(value, lax.ppermute(value, axis, route))  4.51 us
    ppermute x1, waiting for transfers between devices, shards(): from_above = lax.ppermute(low, 'group', along('group', -1, False))  4.16 us
    ppermute x2, starting transfers between devices, both_ways(): return (lax.ppermute(block, 'depth', along('depth', 1, True)),)  3.5 us
    ppermute x1, starting transfers between devices, shards(): from_below = lax.ppermute(high, 'group', along('group', 1, False))  3.47 us
  transfers between devices with their start and end apart: 12, of which 10 were waited for; matrix products, arithmetic and copies ran while one was open for 1% of the time, Pallas kernels for 6%

profile of v2, /device:TPU:0, one launch (start us, length us, event | category | flops | bytes accessed | tf_op | source)
XLA Modules:
  0.0 95.0 jit_solution(7945581167017292003)
XLA Ops:
  0.6 2.5 %opening.1 = (f32[5,8,48,128]{3,2,1,0:T(8,128)}, f32[5,6,48,128]{3,2,1,0:T(8,128)}, f32[120,128]{1,0:T(8,128)}, f32[120,128]{1,0:T(8,128)}, f32[8,128]{1,0:T(8,128)}) custom-call(f32[8,48,128]{2,1,0:T(8,128)} %rho_ref.1, f32[3,8,48,128]{3,2,1,0:T(8,128)} %vel_ref.1, f32[8,48,128]{2,1,0:T(8,128)} %pre_ref.1), custom_call_target="tpu_custom_call" | custom-call | tf_op jit(solution)/shard_map/opening/pallas_call | solution.py:82
  3.2 3.0 %collective-permute-start.2 = (f32[5,6,48,128]{3,2,1,0:T(8,128)}, f32[5,6,48,128]{3,2,1,0:T(8,128)S(1)}, u32[]{:S(2)}, u32[]{:S(2)}) collective-permute-start(f32[5,6,48,128]{3,2,1,0:T(8,128)} %get-tuple-element.18), channel_id=1, source_target_pairs={{0,4},{4,0},{1,5},{5,1},{2,6},{6,2},{3,7},{7,3},{8,12},{12,8},{9,1... | collective-permute-start | bytes 2211848 | tf_op jit(solution)/shard_map/ppermute | solution.py:509
  6.1 3.5 %collective-permute-start = (f32[120,128]{1,0:T(8,128)}, f32[120,128]{1,0:T(8,128)S(1)}, u32[]{:S(2)}, u32[]{:S(2)}) collective-permute-start(f32[120,128]{1,0:T(8,128)} %get-tuple-element.15), channel_id=1, source_target_pairs={{0,8},{8,16},{16,24},{1,9},{9,17},{17,25},{2,10},{10,18},{18,26},{... | collective-permute-start | bytes 184328 | tf_op jit(solution)/shard_map/ppermute | solution.py:513
  9.6 1.3 %collective-permute-start.1 = (f32[120,128]{1,0:T(8,128)}, f32[120,128]{1,0:T(8,128)S(1)}, u32[]{:S(2)}, u32[]{:S(2)}) collective-permute-start(f32[120,128]{1,0:T(8,128)} %get-tuple-element.16), channel_id=1, source_target_pairs={{8,0},{16,8},{24,16},{9,1},{17,9},{25,17},{10,2},{18,10},{26,18},{... | collective-permute-start | bytes 184328 | tf_op jit(solution)/shard_map/ppermute | solution.py:514
  10.9 0.9 collective-permute-done.low_ref
  11.8 0.0 copy-start.4
  11.8 4.2 %collective-permute-done.1.high_ref = f32[120,128]{1,0:T(8,128)S(1)} collective-permute-done((f32[120,128]{1,0:T(8,128)}, f32[120,128]{1,0:T(8,128)S(1)}, u32[]{:S(2)}, u32[]{:S(2)}) %collective-permute-start.1) | collective-permute-done | bytes 61472 | tf_op jit(solution)/shard_map/ppermute | solution.py:514
  15.9 0.0 copy-start.5
  15.9 0.0 copy-done.4
  16.0 0.6 copy-done.5
  16.6 0.0 copy-start.6
  16.6 3.3 %windows.1 = (f32[5,8,56,128]{3,2,1,0:T(8,128)}, f32[5,56,128]{2,1,0:T(8,128)}, f32[5,56,128]{2,1,0:T(8,128)}) custom-call(f32[5,8,48,128]{3,2,1,0:T(8,128)} %get-tuple-element.14.state_ref, f32[120,128]{1,0:T(8,128)} %copy-done.4, f32[120,128]{1,0:T(8,128)} %copy-done.5), custom_call_target="tpu_custom_call" | custom-call | tf_op jit(solution)/shard_map/windows/pallas_call | solution.py:138
  19.8 0.0 collective-permute-start.3
  19.8 0.5 collective-permute-start.4
  20.3 3.0 %collective-permute-done.3.from_right = f32[5,56,128]{2,1,0:T(8,128)S(1)} collective-permute-done((f32[5,56,128]{2,1,0:T(8,128)}, f32[5,56,128]{2,1,0:T(8,128)S(1)}, u32[]{:S(2)}, u32[]{:S(2)}) %collective-permute-start.3) | collective-permute-done | bytes 143392 | tf_op jit(solution)/shard_map/ppermute | solution.py:516
  23.4 0.0 copy-start.2
  23.4 2.7 %collective-permute-done.4.from_left = f32[5,56,128]{2,1,0:T(8,128)S(1)} collective-permute-done((f32[5,56,128]{2,1,0:T(8,128)}, f32[5,56,128]{2,1,0:T(8,128)S(1)}, u32[]{:S(2)}, u32[]{:S(2)}) %collective-permute-start.4) | collective-permute-done | bytes 143392 | tf_op jit(solution)/shard_map/ppermute | solution.py:517
  26.0 0.0 copy-start.3
  26.0 0.0 copy-done.2
  26.0 0.7 copy-done.3
  26.7 2.3 %strips.1 = (f32[2,5,56,128]{3,2,1,0:T(8,128)}, f32[5,72,128]{2,1,0:T(8,128)}) custom-call(f32[5,8,56,128]{3,2,1,0:T(8,128)} %get-tuple-element.17.wide_ref.refs_0_, f32[5,56,128]{2,1,0:T(8,128)} %get-tuple-element.19.right_ref, f32[5,56,128]{2,1,0:T(8,128)} %get-tuple-element.20.left_ref, f32[5,56,128]{2,1,0:T(8,128)} %copy-done.2, f32[5,56,128]{2,1,0:T(8,128)} %copy-done.3), custom_call_target="tpu_custom_call" | custom-call | tf_op jit(solution)/shard_map/strips/pallas_call | solution.py:181
  29.0 0.5 collective-permute-start.5
  29.5 0.0 copy-done.6
  29.5 0.0 collective-permute-start.6
  29.5 3.0 %collective-permute-done.6 = f32[8,128]{1,0:T(8,128)S(1)} collective-permute-done((f32[8,128]{1,0:T(8,128)S(1)}, f32[8,128]{1,0:T(8,128)S(1)}, u32[]{:S(2)}, u32[]{:S(2)}) %collective-permute-start.6) | collective-permute-done | bytes 4128 | tf_op jit(solution)/shard_map/ppermute | solution.py:466
  32.5 0.6 collective-permute-start.7
  33.2 3.0 %collective-permute-done.7 = f32[8,128]{1,0:T(8,128)S(1)} collective-permute-done((f32[8,128]{1,0:T(8,128)S(1)}, f32[8,128]{1,0:T(8,128)S(1)}, u32[]{:S(2)}, u32[]{:S(2)}) %collective-permute-start.7) | collective-permute-done | bytes 4128 | tf_op jit(solution)/shard_map/ppermute | solution.py:466
  36.2 1.6 %collective-permute-start.8 = (f32[8,128]{1,0:T(8,128)S(1)}, f32[8,128]{1,0:T(8,128)S(1)}, u32[]{:S(2)}, u32[]{:S(2)}) collective-permute-start(f32[8,128]{1,0:T(8,128)S(1)} %max.16), channel_id=1, source_target_pairs={{0,8},{8,16},{16,24},{24,0},{1,9},{9,17},{17,25},{25,1},{2,10},{10... | collective-permute-start | bytes 12296 | tf_op jit(solution)/shard_map/ppermute | solution.py:466
  37.7 3.8 %collective-permute-done.8 = f32[8,128]{1,0:T(8,128)S(1)} collective-permute-done((f32[8,128]{1,0:T(8,128)S(1)}, f32[8,128]{1,0:T(8,128)S(1)}, u32[]{:S(2)}, u32[]{:S(2)}) %collective-permute-start.8) | collective-permute-done | bytes 4128 | tf_op jit(solution)/shard_map/ppermute | solution.py:466
  41.6 0.8 collective-permute-start.9
  42.4 3.7 %collective-permute-done.9 = f32[8,128]{1,0:T(8,128)S(1)} collective-permute-done((f32[8,128]{1,0:T(8,128)S(1)}, f32[8,128]{1,0:T(8,128)S(1)}, u32[]{:S(2)}, u32[]{:S(2)}) %collective-permute-start.9) | collective-permute-done | bytes 4128 | tf_op jit(solution)/shard_map/ppermute | solution.py:466
  46.1 1.5 %collective-permute-start.10 = (f32[8,128]{1,0:T(8,128)S(1)}, f32[8,128]{1,0:T(8,128)S(1)}, u32[]{:S(2)}, u32[]{:S(2)}) collective-permute-start(f32[8,128]{1,0:T(8,128)S(1)} %max.18), channel_id=1, source_target_pairs={{0,4},{4,0},{1,5},{5,1},{2,6},{6,2},{3,7},{7,3},{8,12},{12,8},{9,1... | collective-permute-start | bytes 12296 | tf_op jit(solution)/shard_map/ppermute | solution.py:466
  47.6 2.1 %collective-permute-done.10 = f32[8,128]{1,0:T(8,128)S(1)} collective-permute-done((f32[8,128]{1,0:T(8,128)S(1)}, f32[8,128]{1,0:T(8,128)S(1)}, u32[]{:S(2)}, u32[]{:S(2)}) %collective-permute-start.10) | collective-permute-done | bytes 4128 | tf_op jit(solution)/shard_map/ppermute | solution.py:466
  49.7 0.6 max.19.refs_4_
  50.3 0.0 collective-permute-done.5.refs_2_
  50.3 0.0 copy-start.1
  50.3 0.0 collective-permute-done.2.refs_1_
  50.3 0.0 copy-start
  50.3 0.7 copy-done.1
  51.0 0.3 copy-done
  51.2 19.5 %sections.1 = (f32[5,8,48,128]{3,2,1,0:T(8,128)}, f32[8,48,128]{2,1,0:T(8,128)}) custom-call(f32[5,8,56,128]{3,2,1,0:T(8,128)} %get-tuple-element.17.wide_ref.refs_0_, f32[5,6,48,128]{3,2,1,0:T(8,128)} %copy-done, f32[5,72,128]{2,1,0:T(8,128)} %copy-done.1, f32[2,5,56,128]{3,2,1,0:T(8,128)} %get-tuple-element.22.refs_3_, f32[8,128]{1,0:T(8,128)} %max.19.refs_4_), custom_call_target="tpu_custom_call" | custom-call | tf_op jit(solution)/shard_map/sections/pallas_call | solution.py:375
  70.7 1.6 %slice_bitcast_fusion.refs_0_ = f32[8,48,128]{2,1,0:T(8,128)} fusion(f32[5,8,48,128]{3,2,1,0:T(8,128)} %get-tuple-element.12), kind=kLoop, calls=%fused_computation.5 | loop fusion | bytes 393216 | tf_op jit(solution)/shard_map/squeeze | solution.py:522
  72.3 12.9 %render.1 = f32[1536,128]{1,0:T(8,128)} custom-call(f32[8,48,128]{2,1,0:T(8,128)} %slice_bitcast_fusion.refs_0_, f32[8,48,128]{2,1,0:T(8,128)} %get-tuple-element.25.refs_1_, f32[4,256]{1,0:T(4,128)} %refs_2_.1, s32[8,256]{1,0:T(8,128)} %refs_3_.1), custom_call_target="tpu_custom_call" | custom-call | tf_op jit(solution)/shard_map/render/pallas_call | solution.py:447
  85.2 1.2 %slice_select_fusion = (f32[768,128]{1,0:T(8,128)S(1)}, f32[768,128]{1,0:T(8,128)S(1)}) fusion(f32[1536,128]{1,0:T(8,128)} %render.1, pred[]{:T(512)S(6)} %eq.2), kind=kLoop, calls=%fused_computation | loop fusion | flops 196608 | bytes 1572865 | tf_op jit(solution)/shard_map/jit(_where)/select_n | solution.py:488
  86.3 1.6 %collective-permute-start.11 = (f32[4,4,48,128]{3,2,1,0:T(8,128)S(1)}, f32[4,4,48,128]{3,2,1,0:T(8,128)S(1)}, u32[]{:S(2)}, u32[]{:S(2)}) collective-permute-start(f32[4,4,48,128]{3,2,1,0:T(8,128)S(1)} %bitcast.8), channel_id=1, source_target_pairs={{0,4},{4,0},{1,5},{5,1},{2,6},{6,2},{3,7},{7,3},{8,12},{12,8},{9,1... | collective-permute-start | bytes 1179656 | tf_op jit(solution)/shard_map/ppermute | solution.py:488
  87.9 6.3 %collective-permute-done.11 = f32[4,4,48,128]{3,2,1,0:T(8,128)S(1)} collective-permute-done((f32[4,4,48,128]{3,2,1,0:T(8,128)S(1)}, f32[4,4,48,128]{3,2,1,0:T(8,128)S(1)}, u32[]{:S(2)}, u32[]{:S(2)}) %collective-permute-start.11) | collective-permute-done | bytes 393248 | tf_op jit(solution)/shard_map/ppermute | solution.py:488
  94.2 0.8 fusion.1
  (6 shorter events, 0.1 us)
Async XLA Ops:
  3.2 47.1 %collective-permute-start.2 = (f32[5,6,48,128]{3,2,1,0:T(8,128)}, f32[5,6,48,128]{3,2,1,0:T(8,128)S(1)}, u32[]{:S(2)}, u32[]{:S(2)}) collective-permute-start(f32[5,6,48,128]{3,2,1,0:T(8,128)} %get-tuple-element.18), channel_id=1, source_target_pairs={{0,4},{4,0},{1,5},{5,1},{2,6},{6,2},{3,7},{7,3},{8,12},{12,8},{9,1... | collective-permute-start | bytes 2211848 | tf_op jit(solution)/shard_map/ppermute | solution.py:509
  6.1 5.6 %collective-permute-start = (f32[120,128]{1,0:T(8,128)}, f32[120,128]{1,0:T(8,128)S(1)}, u32[]{:S(2)}, u32[]{:S(2)}) collective-permute-start(f32[120,128]{1,0:T(8,128)} %get-tuple-element.15), channel_id=1, source_target_pairs={{0,8},{8,16},{16,24},{1,9},{9,17},{17,25},{2,10},{10,18},{18,26},{... | collective-permute-start | bytes 184328 | tf_op jit(solution)/shard_map/ppermute | solution.py:513
  9.6 6.3 %collective-permute-start.1 = (f32[120,128]{1,0:T(8,128)}, f32[120,128]{1,0:T(8,128)S(1)}, u32[]{:S(2)}, u32[]{:S(2)}) collective-permute-start(f32[120,128]{1,0:T(8,128)} %get-tuple-element.16), channel_id=1, source_target_pairs={{8,0},{16,8},{24,16},{9,1},{17,9},{25,17},{10,2},{18,10},{26,18},{... | collective-permute-start | bytes 184328 | tf_op jit(solution)/shard_map/ppermute | solution.py:514
  11.8 4.2 %copy-start.4 = (f32[120,128]{1,0:T(8,128)}, f32[120,128]{1,0:T(8,128)S(1)}, u32[]{:S(2)}) copy-start(f32[120,128]{1,0:T(8,128)S(1)} %collective-permute-done.low_ref) | copy-start | bytes 184324
  15.9 0.6 copy-start.5
  16.6 12.9 %copy-start.6 = (f32[8,128]{1,0:T(8,128)S(1)}, f32[8,128]{1,0:T(8,128)}, u32[]{:S(2)}) copy-start(f32[8,128]{1,0:T(8,128)} %get-tuple-element.23) | copy-start | bytes 12292
  19.8 3.5 %collective-permute-start.3 = (f32[5,56,128]{2,1,0:T(8,128)}, f32[5,56,128]{2,1,0:T(8,128)S(1)}, u32[]{:S(2)}, u32[]{:S(2)}) collective-permute-start(f32[5,56,128]{2,1,0:T(8,128)} %get-tuple-element.19.right_ref), channel_id=1, source_target_pairs={{0,3},{1,0},{2,1},{3,2},{4,7},{5,4},{6,5},{7,6},{8,11},{9,8},{10,9... | collective-permute-start | bytes 430088 | tf_op jit(solution)/shard_map/ppermute | solution.py:516
  19.8 6.2 %collective-permute-start.4 = (f32[5,56,128]{2,1,0:T(8,128)}, f32[5,56,128]{2,1,0:T(8,128)S(1)}, u32[]{:S(2)}, u32[]{:S(2)}) collective-permute-start(f32[5,56,128]{2,1,0:T(8,128)} %get-tuple-element.20.left_ref), channel_id=1, source_target_pairs={{0,1},{1,2},{2,3},{3,0},{4,5},{5,6},{6,7},{7,4},{8,9},{9,10},{10,1... | collective-permute-start | bytes 430088 | tf_op jit(solution)/shard_map/ppermute | solution.py:517
  23.4 2.7 %copy-start.2 = (f32[5,56,128]{2,1,0:T(8,128)}, f32[5,56,128]{2,1,0:T(8,128)S(1)}, u32[]{:S(2)}) copy-start(f32[5,56,128]{2,1,0:T(8,128)S(1)} %collective-permute-done.3.from_right) | copy-start | bytes 430084
  26.0 0.7 copy-start.3
  29.0 21.3 %collective-permute-start.5 = (f32[5,72,128]{2,1,0:T(8,128)}, f32[5,72,128]{2,1,0:T(8,128)S(1)}, u32[]{:S(2)}, u32[]{:S(2)}) collective-permute-start(f32[5,72,128]{2,1,0:T(8,128)} %get-tuple-element.21), channel_id=1, source_target_pairs={{0,4},{4,0},{1,5},{5,1},{2,6},{6,2},{3,7},{7,3},{8,12},{12,8},{9,1... | collective-permute-start | bytes 552968 | tf_op jit(solution)/shard_map/ppermute | solution.py:509
  29.5 3.0 %collective-permute-start.6 = (f32[8,128]{1,0:T(8,128)S(1)}, f32[8,128]{1,0:T(8,128)S(1)}, u32[]{:S(2)}, u32[]{:S(2)}) collective-permute-start(f32[8,128]{1,0:T(8,128)S(1)} %copy-done.6), channel_id=1, source_target_pairs={{0,1},{1,2},{2,3},{3,0},{4,5},{5,6},{6,7},{7,4},{8,9},{9,10},{10,1... | collective-permute-start | bytes 12296 | tf_op jit(solution)/shard_map/ppermute | solution.py:466
  32.5 3.6 %collective-permute-start.7 = (f32[8,128]{1,0:T(8,128)S(1)}, f32[8,128]{1,0:T(8,128)S(1)}, u32[]{:S(2)}, u32[]{:S(2)}) collective-permute-start(f32[8,128]{1,0:T(8,128)S(1)} %max.15), channel_id=1, source_target_pairs={{0,2},{1,3},{2,0},{3,1},{4,6},{5,7},{6,4},{7,5},{8,10},{9,11},{10,... | collective-permute-start | bytes 12296 | tf_op jit(solution)/shard_map/ppermute | solution.py:466
  36.2 5.4 %collective-permute-start.8 = (f32[8,128]{1,0:T(8,128)S(1)}, f32[8,128]{1,0:T(8,128)S(1)}, u32[]{:S(2)}, u32[]{:S(2)}) collective-permute-start(f32[8,128]{1,0:T(8,128)S(1)} %max.16), channel_id=1, source_target_pairs={{0,8},{8,16},{16,24},{24,0},{1,9},{9,17},{17,25},{25,1},{2,10},{10... | collective-permute-start | bytes 12296 | tf_op jit(solution)/shard_map/ppermute | solution.py:466
  41.6 4.5 %collective-permute-start.9 = (f32[8,128]{1,0:T(8,128)S(1)}, f32[8,128]{1,0:T(8,128)S(1)}, u32[]{:S(2)}, u32[]{:S(2)}) collective-permute-start(f32[8,128]{1,0:T(8,128)S(1)} %max.17), channel_id=1, source_target_pairs={{0,16},{8,24},{16,0},{24,8},{1,17},{9,25},{17,1},{25,9},{2,18},{10... | collective-permute-start | bytes 12296 | tf_op jit(solution)/shard_map/ppermute | solution.py:466
  46.1 3.6 %collective-permute-start.10 = (f32[8,128]{1,0:T(8,128)S(1)}, f32[8,128]{1,0:T(8,128)S(1)}, u32[]{:S(2)}, u32[]{:S(2)}) collective-permute-start(f32[8,128]{1,0:T(8,128)S(1)} %max.18), channel_id=1, source_target_pairs={{0,4},{4,0},{1,5},{5,1},{2,6},{6,2},{3,7},{7,3},{8,12},{12,8},{9,1... | collective-permute-start | bytes 12296 | tf_op jit(solution)/shard_map/ppermute | solution.py:466
  50.3 0.7 copy-start.1
  50.3 0.9 copy-start
  86.3 7.8 %collective-permute-start.11 = (f32[4,4,48,128]{3,2,1,0:T(8,128)S(1)}, f32[4,4,48,128]{3,2,1,0:T(8,128)S(1)}, u32[]{:S(2)}, u32[]{:S(2)}) collective-permute-start(f32[4,4,48,128]{3,2,1,0:T(8,128)S(1)} %bitcast.8), channel_id=1, source_target_pairs={{0,4},{4,0},{1,5},{5,1},{2,6},{6,2},{3,7},{7,3},{8,12},{12,8},{9,1... | collective-permute-start | bytes 1179656 | tf_op jit(solution)/shard_map/ppermute | solution.py:488

commit v3 on v2

v3 whole, which is shorter than its diff:
```python
import functools
import math

import jax
import jax.numpy as jnp
from jax import lax
from jax.experimental import pallas as pl
from jax.experimental.pallas import tpu as pltpu
from jax.sharding import PartitionSpec as P

HEAT_RATIO = 1.4
COURANT = 0.8
REACH = 3
WINDOW = 3 * REACH
SUB = 8
VMEM = pl.BlockSpec(memory_space=pltpu.VMEM)
MIB = 1 << 20


def grant(mib):
    return pltpu.CompilerParams(vmem_limit_bytes=mib * MIB)


def ahead(values, distance=1):
    return pltpu.roll(values, values.shape[-1] - distance, axis=values.ndim - 1)


def behind(values, distance=1):
    return pltpu.roll(values, distance, axis=values.ndim - 1)


def turned(values, shift):
    return pltpu.roll(values, shift % values.shape[-1], axis=values.ndim - 1)


def padded_rows(rows):
    return -(-(rows + 2 * REACH) // SUB) * SUB


def primitives(rho, mx, my, mz, energy):
    inverse = 1.0 / rho
    ux, uy, uz = mx * inverse, my * inverse, mz * inverse
    pressure = (HEAT_RATIO - 1.0) * (energy - 0.5 * (mx * ux + my * uy + mz * uz))
    sound = jnp.sqrt(HEAT_RATIO * pressure * inverse)
    return ux, uy, uz, pressure, sound


def fluxes(state, normal, pressure, component):
    rho, mx, my, mz, energy = state
    rows = [state[component], mx * normal, my * normal, mz * normal, (energy + pressure) * normal]
    rows[component] = rows[component] + pressure
    return rows


def face(flux_a, flux_b, state_a, state_b, signal_a, signal_b):
    fastest = jnp.maximum(signal_a, signal_b)
    return [
        (fa + fb) - fastest * (ub - ua)
        for fa, fb, ua, ub in zip(flux_a, flux_b, state_a, state_b)
    ]


def opening_kernel(rho_ref, vel_ref, pre_ref, state_ref, zpay_ref, low_ref, high_ref, top_ref):
    planes, rows, width = rho_ref.shape
    edge = list(range(REACH)) + list(range(planes - REACH, planes))
    fastest = None
    for z in range(planes):
        rho, p = rho_ref[z], pre_ref[z]
        v = [vel_ref[i, z] for i in range(3)]
        signal = jnp.abs(v[0]) + jnp.abs(v[1]) + jnp.abs(v[2]) + 3.0 * jnp.sqrt(HEAT_RATIO * p / rho)
        signal = jnp.max(signal.reshape(rows // SUB, SUB, width), axis=0)
        fastest = signal if fastest is None else jnp.maximum(fastest, signal)
        kinetic = 0.5 * rho * (v[0] * v[0] + v[1] * v[1] + v[2] * v[2])
        fields = [rho, rho * v[0], rho * v[1], rho * v[2], p / (HEAT_RATIO - 1.0) + kinetic]
        for f in range(5):
            state_ref[f, z] = fields[f]
            if z in edge:
                zpay_ref[f, edge.index(z)] = fields[f]
            at = (f * planes + z) * REACH
            low_ref[at : at + REACH, :] = fields[f][:REACH]
            high_ref[at : at + REACH, :] = fields[f][rows - REACH :]
    top_ref[...] = fastest
    for ref in (low_ref, high_ref):
        ref[5 * planes * REACH :, :] = fastest


def opening(density, velocity, pressure):
    planes, rows, width = density.shape
    f32 = jnp.float32
    return pl.pallas_call(
        opening_kernel,
        out_shape=[
            jax.ShapeDtypeStruct((5, planes, rows, width), f32),
            jax.ShapeDtypeStruct((5, 2 * REACH, rows, width), f32),
            jax.ShapeDtypeStruct((5 * planes * REACH + SUB, width), f32),
            jax.ShapeDtypeStruct((5 * planes * REACH + SUB, width), f32),
            jax.ShapeDtypeStruct((SUB, width), f32),
        ],
        in_specs=[VMEM] * 3,
        out_specs=[VMEM] * 5,
        name="opening",
        compiler_params=grant(8),
    )(density, velocity, pressure)


def window_kernel(
    state_ref, low_ref, high_ref, top_ref, wide_ref, right_ref, left_ref, peak_ref
):
    planes, rows, width = state_ref.shape[1:]
    sent = slice(5 * planes * REACH, 5 * planes * REACH + SUB)
    peak_ref[...] = jnp.maximum(top_ref[...], jnp.maximum(low_ref[sent, :], high_ref[sent, :]))
    total = wide_ref.shape[2]
    group, groups = lax.axis_index("group"), lax.axis_size("group")
    lane = lax.broadcasted_iota(jnp.int32, (SUB, width), 1)
    for f in range(5):
        sign = -1.0 if f == 1 else 1.0
        for z in range(planes):
            at = (f * planes + z) * REACH
            wide_ref[f, z, REACH : REACH + rows, :] = state_ref[f, z]
            mirrored = [state_ref[f, z, r : r + 1, :] * sign for r in range(REACH - 1, -1, -1)]
            below = jnp.where(group == 0, jnp.concatenate(mirrored, axis=0), low_ref[at : at + REACH, :])
            wide_ref[f, z, :REACH, :] = below
            mirrored = [state_ref[f, z, rows - 1 - r : rows - r, :] * sign for r in range(REACH)]
            above = jnp.where(
                group == groups - 1, jnp.concatenate(mirrored, axis=0), high_ref[at : at + REACH, :]
            )
            wide_ref[f, z, REACH + rows : 2 * REACH + rows, :] = above

    def fields(f, carry):
        for t in range(total // SUB):
            cut = slice(SUB * t, SUB * (t + 1))
            right = jnp.zeros((SUB, width), jnp.float32)
            left = right
            for z in range(planes):
                start = WINDOW * (z + REACH)
                inside = (lane >= start) & (lane < start + WINDOW)
                values = wide_ref[f, z, cut, :]
                right = jnp.where(inside, turned(values, start - (width - 2 * REACH)), right)
                left = jnp.where(inside, turned(values, start - (width - REACH)), left)
            right_ref[f, cut, :] = right
            left_ref[f, cut, :] = left
        return carry

    lax.fori_loop(0, 5, fields, 0)


def windows(state, low, high, top):
    planes, rows, width = state.shape[1:]
    total = padded_rows(rows)
    f32 = jnp.float32
    return pl.pallas_call(
        window_kernel,
        out_shape=[
            jax.ShapeDtypeStruct((5, planes, total, width), f32),
            jax.ShapeDtypeStruct((5, total, width), f32),
            jax.ShapeDtypeStruct((5, total, width), f32),
            jax.ShapeDtypeStruct((SUB, width), f32),
        ],
        in_specs=[VMEM] * 4,
        out_specs=[VMEM] * 4,
        name="windows",
        compiler_params=grant(8),
    )(state, low, high, top)


def strip_kernel(wide_ref, right_ref, left_ref, from_right, from_left, strips_ref, pay_ref):
    planes, total, width = wide_ref.shape[1:]
    rows = total - 2 * REACH - (total - 2 * REACH) % SUB
    lane = lax.broadcasted_iota(jnp.int32, (SUB, width), 1)
    column = lane % WINDOW
    span = WINDOW * REACH
    first, last = WINDOW * REACH, WINDOW * planes
    far = WINDOW * (REACH + planes)
    for f in range(5):
        for t in range(total // SUB):
            cut = slice(SUB * t, SUB * (t + 1))
            right = jnp.where(column >= 2 * REACH, from_right[f, cut, :], right_ref[f, cut, :])
            left = jnp.where(column < REACH, from_left[f, cut, :], left_ref[f, cut, :])
            strips_ref[0, f, cut, :] = left
            strips_ref[1, f, cut, :] = right
            sent = jnp.where(lane < span, turned(right, -last), left)
            pay_ref[f, cut, :] = jnp.where(lane >= far, turned(right, far - first), sent)
        low, high = REACH - 1, REACH + rows
        for side, (near, next_one) in enumerate(((0, 1), (planes - 1, planes - 2))):
            at = total + SUB * side
            pay_ref[f, at : at + 2, :] = wide_ref[f, near, low - 1 : low + 1, :]
            pay_ref[f, at + 2 : at + 3, :] = wide_ref[f, next_one, low : low + 1, :]
            pay_ref[f, at + 3 : at + 5, :] = wide_ref[f, near, high : high + 2, :]
            pay_ref[f, at + 5 : at + 6, :] = wide_ref[f, next_one, high : high + 1, :]
            pay_ref[f, at + 6 : at + 8, :] = jnp.zeros((2, width), jnp.float32)


def strips_of(wide, right, left, from_right, from_left):
    planes, total, width = wide.shape[1:]
    f32 = jnp.float32
    return pl.pallas_call(
        strip_kernel,
        out_shape=[
            jax.ShapeDtypeStruct((2, 5, total, width), f32),
            jax.ShapeDtypeStruct((5, total + 2 * SUB, width), f32),
        ],
        in_specs=[VMEM] * 5,
        out_specs=[VMEM] * 2,
        name="strips",
        compiler_params=grant(8),
    )(wide, right, left, from_right, from_left)


def blend(section, base, here, change, half):
    if section == 0:
        return here + half * change
    if section == 1:
        return 0.75 * base + 0.25 * (here + half * change)
    return base * (1.0 / 3.0) + (2.0 / 3.0) * (here + half * change)


def along_y(state, flux, uy, pressure, signal):
    other = [ahead(v) for v in state]
    flux_other = fluxes(other, ahead(uy), ahead(pressure), 2)
    g = face(flux, flux_other, state, other, signal, ahead(signal))
    return [behind(v) - v for v in g]


def section_kernel(shared, *refs):
    if shared:
        wide_ref, zone_ref, pay_ref, strips_ref, top_ref = refs[:5]
        zone_refs, pay_refs = (zone_ref, zone_ref), (pay_ref, pay_ref)
        rest = refs[5:]
    else:
        wide_ref, strips_ref, top_ref = refs[0], refs[5], refs[6]
        zone_refs, pay_refs = refs[1:3], refs[3:5]
        rest = refs[7:]
    out_ref, rho_ref, heat_ref = rest[:3]
    main, strip, (fx, gx, acc, fz, gz) = rest[3:7], rest[7:11], rest[11:]
    planes, total, width = wide_ref.shape[1:]
    rows = out_ref.shape[2]
    tiles = total // SUB
    lane = lax.broadcasted_iota(jnp.int32, (SUB, width), 1)
    far = WINDOW * (REACH + planes)
    for f in range(5):
        for z in range(planes):
            main[0][f, z + REACH, :total, :] = wide_ref[f, z]
        for z in range(REACH):
            main[0][f, z, REACH : REACH + rows, :] = zone_refs[0][f, REACH + z]
            main[0][f, planes + REACH + z, REACH : REACH + rows, :] = zone_refs[1][f, z]
        low, high = REACH - 1, REACH + rows
        for pay, near, next_one, at in (
            (pay_refs[1], planes + REACH, planes + REACH + 1, total),
            (pay_refs[0], REACH - 1, REACH - 2, total + SUB),
        ):
            main[0][f, near, low - 1 : low + 1, :] = pay[f, at : at + 2, :]
            main[0][f, next_one, low : low + 1, :] = pay[f, at + 2 : at + 3, :]
            main[0][f, near, high : high + 2, :] = pay[f, at + 3 : at + 5, :]
            main[0][f, next_one, high : high + 1, :] = pay[f, at + 5 : at + 6, :]
        for t in range(tiles):
            cut = slice(SUB * t, SUB * (t + 1))
            before, after = pay_refs[0][f, cut, :], pay_refs[1][f, cut, :]
            span = WINDOW * REACH
            left = jnp.where(lane < span, turned(before, -WINDOW * planes), strips_ref[0, f, cut, :])
            strip[0][0, f, cut, :] = jnp.where(lane >= far, turned(after, far - span), left)
            right = jnp.where(lane < span, before, strips_ref[1, f, cut, :])
            strip[0][1, f, cut, :] = jnp.where(lane >= far, after, right)
    half = jnp.broadcast_to(0.5 * COURANT / jnp.max(top_ref[...], keepdims=True), (SUB, width))

    def x_pass(which, load, t):
        here, there = slice(SUB * t, SUB * (t + 1)), slice(SUB * t + 1, SUB * (t + 1) + 1)
        a, b = load(here), load(there)
        g = face(
            [fx[which, f, here, :] for f in range(5)],
            [fx[which, f, there, :] for f in range(5)],
            a,
            b,
            fx[which, 5, here, :],
            fx[which, 5, there, :],
        )
        for f in range(5):
            gx[which, f, SUB * (t + 1) : SUB * (t + 2), :] = g[f]
            below = gx[which, f, SUB * (t + 1) - 1 : SUB * (t + 2) - 1, :]
            acc[which, f, here, :] = acc[which, f, here, :] + (below - g[f])

    def keep_x(which, state, ux, pressure, sound, cut):
        for f, v in enumerate(fluxes(state, ux, pressure, 1)):
            fx[which, f, cut, :] = v
        fx[which, 5, cut, :] = jnp.abs(ux) + sound

    def strip_section(section, side):
        source, target = strip[section], strip[section + 1]

        def load(cut):
            return [source[side, f, cut, :] for f in range(5)]

        def finish(t):
            cut = slice(SUB * t, SUB * (t + 1))
            x_pass(side, load, t)
            for f in range(5):
                here, base = source[side, f, cut, :], strip[0][side, f, cut, :]
                target[side, f, cut, :] = blend(section, base, here, acc[side, f, cut, :], half)

        for t in range(tiles):
            cut = slice(SUB * t, SUB * (t + 1))
            state = load(cut)
            ux, uy, uz, pressure, sound = primitives(*state)
            keep_x(side, state, ux, pressure, sound, cut)
            change = along_y(state, fluxes(state, uy, pressure, 2), uy, pressure, jnp.abs(uy) + sound)
            signal = jnp.abs(uz) + sound
            other = [ahead(v, WINDOW) for v in state]
            g = face(
                fluxes(state, uz, pressure, 3),
                fluxes(other, ahead(uz, WINDOW), ahead(pressure, WINDOW), 3),
                state,
                other,
                signal,
                ahead(signal, WINDOW),
            )
            for f in range(5):
                acc[side, f, cut, :] = change[f] + (behind(g[f], WINDOW) - g[f])
            if t:
                finish(t - 1)
        finish(tiles - 1)

    def main_section(section, first, last):
        source, target, base = main[section], main[section + 1], main[0]

        def plane(w, with_face, with_finish, with_sides):
            def load(cut):
                return [source[f, w, cut, :] for f in range(5)]

            for t in range(tiles):
                cut = slice(SUB * t, SUB * (t + 1))
                state = load(cut)
                ux, uy, uz, pressure, sound = primitives(*state)
                flux, signal = fluxes(state, uz, pressure, 3), jnp.abs(uz) + sound
                if with_face:
                    before = [source[f, w - 1, cut, :] for f in range(5)]
                    flux_before = [fz[f, cut, :] for f in range(5)]
                    g = face(flux_before, flux, before, state, fz[5, cut, :], signal)
                    for f in range(5):
                        if with_finish:
                            change = acc[0, f, cut, :] + (gz[f, cut, :] - g[f])
                            started = base[f, w - 1, cut, :] if section else None
                            target[f, w - 1, cut, :] = blend(section, started, before[f], change, half)
                        if with_sides:
                            gz[f, cut, :] = g[f]
                if with_sides or not with_face:
                    for f in range(5):
                        fz[f, cut, :] = flux[f]
                    fz[5, cut, :] = signal
                if with_sides:
                    keep_x(0, state, ux, pressure, sound, cut)
                    flux = fluxes(state, uy, pressure, 2)
                    change = along_y(state, flux, uy, pressure, jnp.abs(uy) + sound)
                    for f in range(5):
                        acc[0, f, cut, :] = change[f]
                    if t:
                        x_pass(0, load, t - 1)
            if with_sides:
                x_pass(0, load, tiles - 1)

        plane(first - 1, False, False, False)
        plane(first, True, False, True)

        def step(w, carry):
            plane(w, True, True, True)
            return carry

        lax.fori_loop(first + 1, last, step, 0)
        plane(last, True, True, False)

    for section in range(3):
        for side in range(2):
            strip_section(section, side)
        main_section(section, 1 + section, planes + 2 * REACH - 1 - section)
    column = lane % WINDOW
    for f in range(5):
        for t in range(rows // SUB):
            cut = slice(SUB * t + REACH, SUB * (t + 1) + REACH)
            edge = jnp.where(
                column < 2 * REACH, strip[3][1, f, cut, :], behind(strip[3][0, f, cut, :], REACH)
            )
            for z in range(planes):
                placed = turned(edge, width - REACH - (WINDOW * (z + REACH) + REACH))
                inner = main[3][f, z + REACH, cut, :]
                out_ref[f, z, SUB * t : SUB * (t + 1), :] = jnp.where(
                    (lane < REACH) | (lane >= width - REACH), placed, inner
                )
    for z in range(planes):
        state = [out_ref[f, z] for f in range(5)]
        rho_ref[z] = state[0]
        heat_ref[z] = primitives(*state)[3] / state[0]


def sections(wide, zones, pays, strips, top, rows):
    planes, total, width = wide.shape[1:]
    f32 = jnp.float32
    shared = len(zones) == 1
    tall, deep = total + SUB, planes + 2 * REACH
    args = [wide, *zones, *pays, strips, top]
    brick = jax.ShapeDtypeStruct((planes, rows, width), f32)
    return pl.pallas_call(
        functools.partial(section_kernel, shared),
        out_shape=[jax.ShapeDtypeStruct((5, planes, rows, width), f32), brick, brick],
        in_specs=[VMEM] * len(args),
        out_specs=[VMEM] * 3,
        scratch_shapes=[pltpu.VMEM((5, deep, tall, width), f32)] * 4
        + [pltpu.VMEM((2, 5, tall, width), f32)] * 4
        + [
            pltpu.VMEM((2, 6, tall, width), f32),
            pltpu.VMEM((2, 5, tall, width), f32),
            pltpu.VMEM((2, 5, total, width), f32),
            pltpu.VMEM((6, total, width), f32),
            pltpu.VMEM((5, total, width), f32),
        ],
        name="sections",
        compiler_params=grant(24),
    )(*args)


def lanes(values, index):
    return lax.gather(
        values,
        index[..., None],
        lax.GatherDimensionNumbers(
            offset_dims=(),
            collapsed_slice_dims=(1,),
            start_index_map=(1,),
            operand_batching_dims=(0,),
            start_indices_batching_dims=(0,),
        ),
        slice_sizes=(1, 1),
        mode=lax.GatherScatterMode.PROMISE_IN_BOUNDS,
    )


LEVELS = 65535


def render_kernel(
    scale, begin, count, halves, rho_ref, heat_ref, palette_ref, index_ref, *refs
):
    outs, (table, ke, ko, we, wo, thick) = refs[: len(refs) - 6], refs[len(refs) - 6 :]
    planes, rows, width = rho_ref.shape
    count_tf, bins = index_ref.shape
    half = bins // 2
    chosen = index_ref[...]
    if halves:
        swapped = pltpu.roll(chosen, count_tf // 2, axis=0)
        chosen = jnp.where(lax.axis_index("depth") == 0, swapped, chosen)
    colours = palette_ref[...]
    least = jnp.min(colours, keepdims=True)
    step = jnp.maximum(jnp.max(colours, keepdims=True) - least, 1e-6) * (1.0 / LEVELS)
    coded = ((colours - least) / step + 0.5).astype(jnp.int32)
    words = [(coded[c : c + 1] - (LEVELS + 1) // 2) * (LEVELS + 1) + coded[c + 1 : c + 2] for c in (0, 2)]
    lane = lax.broadcasted_iota(jnp.int32, (count_tf, half), 1)
    low, high = chosen[:, :half], chosen[:, half:]
    for parity in range(2):
        at = lane * 2 + parity
        inside = jnp.where(at < half, at, at - half)
        colour = jnp.where(at < half, lanes(low, inside), lanes(high, inside))
        wrapped = jnp.where(colour < half, colour, colour - half)
        for pair in range(2):
            first = jnp.broadcast_to(words[pair][:, :half], (count_tf, half))
            second = jnp.broadcast_to(words[pair][:, half:], (count_tf, half))
            table[pair, parity] = jnp.where(
                colour < half, lanes(first, wrapped), lanes(second, wrapped)
            )
    step_wide = jnp.broadcast_to(step, (SUB, width))
    for z in range(planes):
        for t in range(count // SUB):
            cut, from_cut = slice(SUB * t, SUB * (t + 1)), slice(begin + SUB * t, begin + SUB * (t + 1))
            rho = rho_ref[z, from_cut, :]
            position = jnp.clip(rho - 0.5, 0.0, 1.0) * (bins - 1)
            cell = jnp.minimum(position.astype(jnp.int32), bins - 2)
            even = (cell + 1) >> 1
            odd = cell >> 1
            ke[z, cut, :] = even
            ko[z, cut, :] = odd
            we[z, cut, :] = (1.0 - jnp.abs(position - (2 * even).astype(jnp.float32))) * step_wide
            wo[z, cut, :] = (1.0 - jnp.abs(position - (2 * odd + 1).astype(jnp.float32))) * step_wide
            thick[z, cut, :] = rho * (-scale * math.log2(math.e))
    tables = [[table[pair, p] for p in range(2)] for pair in range(2)]
    base_low = jnp.broadcast_to(least, (count_tf, width))
    base_high = base_low + jnp.broadcast_to(step, (count_tf, width)) * ((LEVELS + 1) // 2)

    def ray(x, carry):
        trans = jnp.ones((count_tf, width), jnp.float32)
        light = [jnp.zeros((count_tf, width), jnp.float32) for _ in range(3)]
        for z in range(planes):

            def wide(ref, at=x):
                return jnp.broadcast_to(ref[z, pl.ds(at, 1), :], (count_tf, width))

            ie, io, fe, fo = wide(ke), wide(ko), wide(we), wide(wo)
            looked = []
            for pair in range(2):
                even, odd = lanes(tables[pair][0], ie), lanes(tables[pair][1], io)
                looked.append(
                    base_high
                    + (even >> 16).astype(jnp.float32) * fe
                    + (odd >> 16).astype(jnp.float32) * fo
                )
                looked.append(
                    base_low
                    + (even & LEVELS).astype(jnp.float32) * fe
                    + (odd & LEVELS).astype(jnp.float32) * fo
                )
            passed = trans * jnp.exp2(looked[3] * wide(thick))
            weight = (trans - passed) * wide(heat_ref, x + begin)
            light = [light[c] + looked[c] * weight for c in range(3)]
            trans = passed
        per_out = count_tf // len(outs)
        for c, values in enumerate(light + [trans]):
            for i, out in enumerate(outs):
                out[pl.ds(c * count + x, per_out, stride=4 * count), :] = values[
                    per_out * i : per_out * (i + 1)
                ]
        return carry

    lax.fori_loop(0, count, ray, 0)


def render(rho, heat, palette, index, scale, begin, count, halves):
    planes, rows, width = rho.shape
    count_tf, bins = index.shape
    parts = 2 if halves else 1
    per_out = count_tf // parts
    shape = jax.ShapeDtypeStruct((per_out * 4 * count, width), jnp.float32)
    scratch = [pltpu.VMEM((planes, count, width), t) for t in (jnp.int32,) * 2 + (jnp.float32,) * 3]
    outs = pl.pallas_call(
        functools.partial(render_kernel, scale, begin, count, halves),
        out_shape=[shape] * parts,
        in_specs=[VMEM] * 4,
        out_specs=[VMEM] * parts,
        scratch_shapes=[pltpu.VMEM((2, 2, count_tf, bins // 2), jnp.int32)] + scratch,
        name=f"render_{begin}",
        compiler_params=grant(8),
    )(rho, heat, palette, index)
    return [out.reshape(per_out, 4, count, width) for out in outs]


def exchange_max(value, axis, step):
    size = lax.axis_size(axis)
    if size & (size - 1) == 0:
        route = [(i, i ^ step) for i in range(size)]
    else:
        route = along(axis, step, True)
    return jnp.maximum(value, lax.ppermute(value, axis, route))


def largest(value, axis, step=1):
    while step < lax.axis_size(axis):
        value = exchange_max(value, axis, step)
        step *= 2
    return value


def composed(shares):
    light, passed = None, None
    for d in range(shares.shape[0]):
        slab = shares[d]
        light = slab[:, :3] if d == 0 else light + passed * slab[:, :3]
        passed = slab[:, 3:] if d == 0 else passed * slab[:, 3:]
    return light


def along(axis, distance, wrap):
    size = lax.axis_size(axis)
    if wrap:
        return [(i, (i + distance) % size) for i in range(size)]
    return [(i, i + distance) for i in range(size) if 0 <= i + distance < size]


def pictured(rho, heat, palette, index):
    depth = lax.axis_size("depth")
    planes, rows, _ = rho.shape
    scale = 2.0 / (planes * depth)
    if depth != 2:
        (shares,) = render(rho, heat, palette, index, scale, 0, rows, False)
        parts = shares.reshape((depth, shares.shape[0] // depth) + shares.shape[1:])
        return composed(lax.all_to_all(parts, "depth", 0, 0, tiled=True))
    chunk = rows // 2 if rows % (2 * SUB) == 0 else rows
    kept, sent = [], []
    for begin in range(0, rows, chunk):
        other, own = render(rho, heat, palette, index, scale, begin, chunk, True)
        kept.append(own)
        sent.append(lax.ppermute(other, "depth", along("depth", 1, True)))
    in_front = lax.axis_index("depth") == 0
    pieces = []
    for own, other in zip(kept, sent):
        front, back = jnp.where(in_front, own, other), jnp.where(in_front, other, own)
        pieces.append(front[:, :3] + front[:, 3:] * back[:, :3])
    return jnp.concatenate(pieces, axis=2)


def shards(density, velocity, pressure, palette, palette_index):
    depth, groups = lax.axis_size("depth"), lax.axis_size("group")
    planes, rows = density.shape[:2]
    state, zone, low, high, top = opening(density, velocity, pressure)

    def both_ways(block):
        if depth == 2:
            return (lax.ppermute(block, "depth", along("depth", 1, True)),)
        return tuple(lax.ppermute(block, "depth", along("depth", d, True)) for d in (1, -1))

    zones = both_ways(zone)
    from_below = lax.ppermute(high, "group", along("group", 1, False))
    from_above = lax.ppermute(low, "group", along("group", -1, False))
    wide, right, left, top = windows(state, from_below, from_above, top)
    from_right = lax.ppermute(right, "image", along("image", -1, True))
    from_left = lax.ppermute(left, "image", along("image", 1, True))
    if groups == 4:
        top = exchange_max(top, "group", 2)
    else:
        top = largest(top, "group")
    top = exchange_max(top, "image", 1)
    from_right, from_left, top = lax.optimization_barrier((from_right, from_left, top))
    strips, pay = strips_of(wide, right, left, from_right, from_left)
    pays = both_ways(pay)
    top = largest(largest(top, "image", 2), "depth")
    fluid_state, rho, heat = sections(wide, zones, pays, strips, top, rows)
    return (fluid_state, pictured(rho, heat, palette, palette_index))


def solution(mesh):
    return jax.shard_map(
        shards,
        mesh=mesh,
        in_specs=(
            P("depth", "group", "image"),
            P(None, "depth", "group", "image"),
            P("depth", "group", "image"),
            P(),
            P(),
        ),
        out_specs=(P(None, "depth", "group", "image"), P("depth", None, "group", "image")),
        check_vma=False,
    )
```

time: 95.3 us -> 64.6 us (0.68)
  waiting for transfers between devices: 32.7 us -> 17.1 us
  Pallas kernels: 40.4 us -> 25.8 us
  starting transfers between devices: 14.8 us -> 16.8 us
  other arithmetic: 2.58 us -> 0.87 us
    ppermute x6, waiting for transfers between devices: 21.9 us -> 12.3 us  [the longest x4 7.17 us: exchange_max(): return jnp.maximum(value, lax.ppermute(value, axis, route))]
    pallas_call x1 -> x2, Pallas kernels: 12.9 us -> 8.36 us  [render(): pl.pallas_call(functools.partial(render_kernel, scale, begin, count, halv...]
    pallas_call x1, Pallas kernels: 19.5 us -> 16 us  [sections(): pl.pallas_call(functools.partial(section_kernel, shared), out_shape=[jax....]
    ppermute x1, waiting for transfers between devices: 3.01 us -> 0.01 us  [shards(): from_right = lax.ppermute(right, 'image', along('image', -1, True))]
    ppermute x1, waiting for transfers between devices: 2.68 us -> 0.01 us  [shards(): from_left = lax.ppermute(left, 'image', along('image', 1, True))]
    pallas_call x1, Pallas kernels: 2.54 us -> 0.23 us  [opening(): pl.pallas_call(opening_kernel, out_shape=[jax.ShapeDtypeStruct((5, planes...]
    pallas_call x1, Pallas kernels: 3.26 us -> 1.08 us  [windows(): pl.pallas_call(window_kernel, out_shape=[jax.ShapeDtypeStruct((5, planes,...]
    pallas_call x1, Pallas kernels: 2.26 us -> 0.15 us  [strips_of(): pl.pallas_call(strip_kernel, out_shape=[jax.ShapeDtypeStruct((2, 5, total...]
  transfers between devices with their start and end apart: 12 -> 12, of which waited for: 10 -> 7; matrix products, arithmetic and copies ran while one was open for 1% -> 0% of each run, Pallas kernels for 6% -> 8%
where the time goes in v3:
time: 64.6 us; the launch traced here: 64.4 us
  Pallas kernels  25.8 us (40%)
  waiting for transfers between devices  17.1 us (26%)
  starting transfers between devices  16.8 us (26%)
  local copies, waits for them, and re-layouts  2.93 us (5%)
  other arithmetic  0.87 us (1%)
  between operations  0.75 us (1%)
    pallas_call x1, Pallas kernels, sections(): pl.pallas_call(functools.partial(section_kernel, shared), out_shape=[jax....  16 us
    pallas_call x2, Pallas kernels, render(): pl.pallas_call(functools.partial(render_kernel, scale, begin, count, halv...  8.36 us
    ppermute x4, waiting for transfers between devices, exchange_max(): return jnp.maximum(value, lax.ppermute(value, axis, route))  7.17 us
    ppermute x4, starting transfers between devices, exchange_max(): return jnp.maximum(value, lax.ppermute(value, axis, route))  5.72 us
    ppermute x2, waiting for transfers between devices, pictured(): sent.append(lax.ppermute(other, 'depth', along('depth', 1, True)))  5.09 us
    ppermute x1, waiting for transfers between devices, shards(): from_above = lax.ppermute(low, 'group', along('group', -1, False))  4.27 us
    ppermute x2, starting transfers between devices, both_ways(): return (lax.ppermute(block, 'depth', along('depth', 1, True)),)  3.63 us
    ppermute x1, starting transfers between devices, shards(): from_below = lax.ppermute(high, 'group', along('group', 1, False))  3.47 us
  transfers between devices with their start and end apart: 12, of which 7 were waited for; matrix products, arithmetic and copies ran while one was open for 0% of the time, Pallas kernels for 8%

profile of v3, /device:TPU:0, one launch (start us, length us, event | category | flops | bytes accessed | tf_op | source)
XLA Modules:
  0.0 64.4 jit_solution(13538638688660210184)
XLA Ops:
  0.6 0.0 copy-start
  0.6 1.1 %copy-done = f32[3,8,48,128]{3,2,1,0:T(8,128)S(1)} copy-done((f32[3,8,48,128]{3,2,1,0:T(8,128)S(1)}, f32[3,8,48,128]{3,2,1,0:T(8,128)}, u32[]{:S(2)}) %copy-start) | copy-done | bytes 589848
  1.7 0.0 copy-start.1
  1.7 0.9 %copy-done.1 = f32[8,48,128]{2,1,0:T(8,128)S(1)} copy-done((f32[8,48,128]{2,1,0:T(8,128)S(1)}, f32[8,48,128]{2,1,0:T(8,128)}, u32[]{:S(2)}) %copy-start.1) | copy-done | bytes 196632
  2.6 0.0 copy-start.2
  2.6 0.9 %copy-done.2 = f32[8,48,128]{2,1,0:T(8,128)S(1)} copy-done((f32[8,48,128]{2,1,0:T(8,128)S(1)}, f32[8,48,128]{2,1,0:T(8,128)}, u32[]{:S(2)}) %copy-start.2) | copy-done | bytes 196632
  3.5 0.2 opening.1
  3.8 3.0 %collective-permute-start.2 = (f32[5,6,48,128]{3,2,1,0:T(8,128)S(1)}, f32[5,6,48,128]{3,2,1,0:T(8,128)S(1)}, u32[]{:S(2)}, u32[]{:S(2)}) collective-permute-start(f32[5,6,48,128]{3,2,1,0:T(8,128)S(1)} %get-tuple-element.28), channel_id=1, source_target_pairs={{0,4},{4,0},{1,5},{5,1},{2,6},{6,2},{3,7},{7,3},{8,12},{12,8},{9,1... | collective-permute-start | bytes 2211848 | tf_op jit(solution)/shard_map/ppermute | solution.py:601
  6.8 3.5 %collective-permute-start = (f32[128,128]{1,0:T(8,128)S(1)}, f32[128,128]{1,0:T(8,128)S(1)}, u32[]{:S(2)}, u32[]{:S(2)}) collective-permute-start(f32[128,128]{1,0:T(8,128)S(1)} %get-tuple-element.24), channel_id=1, source_target_pairs={{0,8},{8,16},{16,24},{1,9},{9,17},{17,25},{2,10},{10,18},{18,26},{... | collective-permute-start | bytes 196616 | tf_op jit(solution)/shard_map/ppermute | solution.py:605
  10.3 1.3 %collective-permute-start.1 = (f32[128,128]{1,0:T(8,128)S(1)}, f32[128,128]{1,0:T(8,128)S(1)}, u32[]{:S(2)}, u32[]{:S(2)}) collective-permute-start(f32[128,128]{1,0:T(8,128)S(1)} %get-tuple-element.25), channel_id=1, source_target_pairs={{8,0},{16,8},{24,16},{9,1},{17,9},{25,17},{10,2},{18,10},{26,18},{... | collective-permute-start | bytes 196616 | tf_op jit(solution)/shard_map/ppermute | solution.py:606
  11.6 0.6 collective-permute-done.low_ref
  12.2 4.3 %collective-permute-done.1.high_ref = f32[128,128]{1,0:T(8,128)S(1)} collective-permute-done((f32[128,128]{1,0:T(8,128)S(1)}, f32[128,128]{1,0:T(8,128)S(1)}, u32[]{:S(2)}, u32[]{:S(2)}) %collective-permute-start.1) | collective-permute-done | bytes 65568 | tf_op jit(solution)/shard_map/ppermute | solution.py:606
  16.5 1.1 %windows.1 = (f32[5,8,56,128]{3,2,1,0:T(8,128)S(1)}, f32[5,56,128]{2,1,0:T(8,128)S(1)}, f32[5,56,128]{2,1,0:T(8,128)S(1)}, f32[8,128]{1,0:T(8,128)S(1)}) custom-call(f32[5,8,48,128]{3,2,1,0:T(8,128)S(1)} %get-tuple-element.23.state_ref, f32[128,128]{1,0:T(8,128)S(1)} %collective-permute-done.low_ref, f32[128,128]{1,0:T(8,128)S(1)} %collective-permute-done.1.high_ref, ...), custom_call_target="tpu_custom_call" | custom-call | tf_op jit(solution)/shard_map/windows/pallas_call | solution.py:151
  17.5 0.1 collective-permute-start.3
  17.6 0.5 collective-permute-start.4
  18.1 2.6 %collective-permute-start.5 = (f32[8,128]{1,0:T(8,128)S(1)}, f32[8,128]{1,0:T(8,128)S(1)}, u32[]{:S(2)}, u32[]{:S(2)}) collective-permute-start(f32[8,128]{1,0:T(8,128)S(1)} %get-tuple-element.31), channel_id=1, source_target_pairs={{0,16},{8,24},{16,0},{24,8},{1,17},{9,25},{17,1},{25,9},{2,18},{10... | collective-permute-start | bytes 12296 | tf_op jit(solution)/shard_map/ppermute | solution.py:546
  20.7 1.9 %collective-permute-done.5 = f32[8,128]{1,0:T(8,128)S(1)} collective-permute-done((f32[8,128]{1,0:T(8,128)S(1)}, f32[8,128]{1,0:T(8,128)S(1)}, u32[]{:S(2)}, u32[]{:S(2)}) %collective-permute-start.5) | collective-permute-done | bytes 4128 | tf_op jit(solution)/shard_map/ppermute | solution.py:546
  22.6 0.1 collective-permute-start.6
  22.7 1.1 %collective-permute-done.6 = f32[8,128]{1,0:T(8,128)S(1)} collective-permute-done((f32[8,128]{1,0:T(8,128)S(1)}, f32[8,128]{1,0:T(8,128)S(1)}, u32[]{:S(2)}, u32[]{:S(2)}) %collective-permute-start.6) | collective-permute-done | bytes 4128 | tf_op jit(solution)/shard_map/ppermute | solution.py:546
  23.8 0.0 collective-permute-done.3.from_right
  23.8 0.0 collective-permute-done.4.from_left
  23.8 0.2 strips.1
  24.0 0.6 collective-permute-start.7
  24.6 1.5 %collective-permute-start.8 = (f32[8,128]{1,0:T(8,128)S(1)}, f32[8,128]{1,0:T(8,128)S(1)}, u32[]{:S(2)}, u32[]{:S(2)}) collective-permute-start(f32[8,128]{1,0:T(8,128)S(1)} %max.13), channel_id=1, source_target_pairs={{0,2},{1,3},{2,0},{3,1},{4,6},{5,7},{6,4},{7,5},{8,10},{9,11},{10,... | collective-permute-start | bytes 12296 | tf_op jit(solution)/shard_map/ppermute | solution.py:546
  26.1 2.1 %collective-permute-done.8 = f32[8,128]{1,0:T(8,128)S(1)} collective-permute-done((f32[8,128]{1,0:T(8,128)S(1)}, f32[8,128]{1,0:T(8,128)S(1)}, u32[]{:S(2)}, u32[]{:S(2)}) %collective-permute-start.8) | collective-permute-done | bytes 4128 | tf_op jit(solution)/shard_map/ppermute | solution.py:546
  28.2 1.5 %collective-permute-start.9 = (f32[8,128]{1,0:T(8,128)S(1)}, f32[8,128]{1,0:T(8,128)S(1)}, u32[]{:S(2)}, u32[]{:S(2)}) collective-permute-start(f32[8,128]{1,0:T(8,128)S(1)} %max.14), channel_id=1, source_target_pairs={{0,4},{4,0},{1,5},{5,1},{2,6},{6,2},{3,7},{7,3},{8,12},{12,8},{9,1... | collective-permute-start | bytes 12296 | tf_op jit(solution)/shard_map/ppermute | solution.py:546
  29.7 2.1 %collective-permute-done.9 = f32[8,128]{1,0:T(8,128)S(1)} collective-permute-done((f32[8,128]{1,0:T(8,128)S(1)}, f32[8,128]{1,0:T(8,128)S(1)}, u32[]{:S(2)}, u32[]{:S(2)}) %collective-permute-start.9) | collective-permute-done | bytes 4128 | tf_op jit(solution)/shard_map/ppermute | solution.py:546
  31.8 0.0 collective-permute-done.7.refs_2_
  31.8 0.0 collective-permute-done.2.refs_1_
  31.8 0.0 copy-start.3
  31.8 0.0 copy-start.4
  31.8 16.0 %sections.1 = (f32[5,8,48,128]{3,2,1,0:T(8,128)}, f32[8,48,128]{2,1,0:T(8,128)S(1)}, f32[8,48,128]{2,1,0:T(8,128)S(1)}) custom-call(f32[5,8,56,128]{3,2,1,0:T(8,128)S(1)} %get-tuple-element.27.wide_ref.refs_0_, f32[5,6,48,128]{3,2,1,0:T(8,128)S(1)} %collective-permute-done.2.refs_1_, f32[5,72,128]{2,1,0:T(8,128)S(1)} %collective-permute-done.7.refs_2_, ...), custom_call_target="tpu_custom_call" | custom-call | tf_op jit(solution)/shard_map/sections/pallas_call | solution.py:399
  47.8 0.0 copy-done.3
  47.8 0.0 copy-done.4
  47.8 4.2 %render_0.1 = (f32[384,128]{1,0:T(8,128)S(1)}, f32[384,128]{1,0:T(8,128)S(1)}) custom-call(f32[8,48,128]{2,1,0:T(8,128)S(1)} %get-tuple-element.38.rho_ref, f32[8,48,128]{2,1,0:T(8,128)S(1)} %get-tuple-element.39.heat_ref, f32[4,256]{1,0:T(4,128)S(1)} %copy-done.4, s32[8,256]{1,0:T(8,128)S(1)} %copy-done.3), custom_call_target="tpu_custom_call" | custom-call | tf_op jit(solution)/shard_map/render_0/pallas_call | solution.py:528
  52.0 1.6 %collective-permute-start.10 = (f32[4,4,24,128]{3,2,1,0:T(8,128)S(1)}, f32[4,4,24,128]{3,2,1,0:T(8,128)S(1)}, u32[]{:S(2)}, u32[]{:S(2)}) collective-permute-start(f32[4,4,24,128]{3,2,1,0:T(8,128)S(1)} %bitcast.12), channel_id=1, source_target_pairs={{0,4},{4,0},{1,5},{5,1},{2,6},{6,2},{3,7},{7,3},{8,12},{12,8},{9,1... | collective-permute-start | bytes 589832 | tf_op jit(solution)/shard_map/ppermute | solution.py:585
  53.6 4.2 %render_24.1 = (f32[384,128]{1,0:T(8,128)S(1)}, f32[384,128]{1,0:T(8,128)S(1)}) custom-call(f32[8,48,128]{2,1,0:T(8,128)S(1)} %get-tuple-element.38.rho_ref, f32[8,48,128]{2,1,0:T(8,128)S(1)} %get-tuple-element.39.heat_ref, f32[4,256]{1,0:T(4,128)S(1)} %copy-done.4, s32[8,256]{1,0:T(8,128)S(1)} %copy-done.3), custom_call_target="tpu_custom_call" | custom-call | tf_op jit(solution)/shard_map/render_24/pallas_call | solution.py:528
  57.8 0.6 collective-permute-start.11
  58.4 0.0 collective-permute-done.10
  58.4 5.1 %collective-permute-done.11 = f32[4,4,24,128]{3,2,1,0:T(8,128)S(1)} collective-permute-done((f32[4,4,24,128]{3,2,1,0:T(8,128)S(1)}, f32[4,4,24,128]{3,2,1,0:T(8,128)S(1)}, u32[]{:S(2)}, u32[]{:S(2)}) %collective-permute-start.11) | collective-permute-done | bytes 196640 | tf_op jit(solution)/shard_map/ppermute | solution.py:585
  63.6 0.7 %pad_maximum_fusion = f32[4,3,48,128]{3,2,1,0:T(8,128)} fusion(f32[4,3,24,128]{3,2,1,0:T(8,128)S(1)} %fusion.1, f32[4,3,24,128]{3,2,1,0:T(8,128)S(1)} %fusion.3), kind=kLoop, calls=%fused_computation | loop fusion | flops 73728 | bytes 589824 | tf_op jit(solution)/shard_map/concatenate | solution.py:591
  (10 shorter events, 0.1 us)
Async XLA Ops:
  0.6 1.1 %copy-start = (f32[3,8,48,128]{3,2,1,0:T(8,128)S(1)}, f32[3,8,48,128]{3,2,1,0:T(8,128)}, u32[]{:S(2)}) copy-start(f32[3,8,48,128]{3,2,1,0:T(8,128)} %vel_ref.1) | copy-start | bytes 1769476
  1.7 0.9 %copy-start.1 = (f32[8,48,128]{2,1,0:T(8,128)S(1)}, f32[8,48,128]{2,1,0:T(8,128)}, u32[]{:S(2)}) copy-start(f32[8,48,128]{2,1,0:T(8,128)} %rho_ref.1) | copy-start | bytes 589828
  2.6 0.9 %copy-start.2 = (f32[8,48,128]{2,1,0:T(8,128)S(1)}, f32[8,48,128]{2,1,0:T(8,128)}, u32[]{:S(2)}) copy-start(f32[8,48,128]{2,1,0:T(8,128)} %pre_ref.1) | copy-start | bytes 589828
  3.8 28.0 %collective-permute-start.2 = (f32[5,6,48,128]{3,2,1,0:T(8,128)S(1)}, f32[5,6,48,128]{3,2,1,0:T(8,128)S(1)}, u32[]{:S(2)}, u32[]{:S(2)}) collective-permute-start(f32[5,6,48,128]{3,2,1,0:T(8,128)S(1)} %get-tuple-element.28), channel_id=1, source_target_pairs={{0,4},{4,0},{1,5},{5,1},{2,6},{6,2},{3,7},{7,3},{8,12},{12,8},{9,1... | collective-permute-start | bytes 2211848 | tf_op jit(solution)/shard_map/ppermute | solution.py:601
  6.8 5.4 %collective-permute-start = (f32[128,128]{1,0:T(8,128)S(1)}, f32[128,128]{1,0:T(8,128)S(1)}, u32[]{:S(2)}, u32[]{:S(2)}) collective-permute-start(f32[128,128]{1,0:T(8,128)S(1)} %get-tuple-element.24), channel_id=1, source_target_pairs={{0,8},{8,16},{16,24},{1,9},{9,17},{17,25},{2,10},{10,18},{18,26},{... | collective-permute-start | bytes 196616 | tf_op jit(solution)/shard_map/ppermute | solution.py:605
  10.3 6.2 %collective-permute-start.1 = (f32[128,128]{1,0:T(8,128)S(1)}, f32[128,128]{1,0:T(8,128)S(1)}, u32[]{:S(2)}, u32[]{:S(2)}) collective-permute-start(f32[128,128]{1,0:T(8,128)S(1)} %get-tuple-element.25), channel_id=1, source_target_pairs={{8,0},{16,8},{24,16},{9,1},{17,9},{25,17},{10,2},{18,10},{26,18},{... | collective-permute-start | bytes 196616 | tf_op jit(solution)/shard_map/ppermute | solution.py:606
  17.5 6.2 %collective-permute-start.3 = (f32[5,56,128]{2,1,0:T(8,128)S(1)}, f32[5,56,128]{2,1,0:T(8,128)S(1)}, u32[]{:S(2)}, u32[]{:S(2)}) collective-permute-start(f32[5,56,128]{2,1,0:T(8,128)S(1)} %get-tuple-element.29.right_ref), channel_id=1, source_target_pairs={{0,3},{1,0},{2,1},{3,2},{4,7},{5,4},{6,5},{7,6},{8,11},{9,8},{10,9... | collective-permute-start | bytes 430088 | tf_op jit(solution)/shard_map/ppermute | solution.py:608
  17.6 6.2 %collective-permute-start.4 = (f32[5,56,128]{2,1,0:T(8,128)S(1)}, f32[5,56,128]{2,1,0:T(8,128)S(1)}, u32[]{:S(2)}, u32[]{:S(2)}) collective-permute-start(f32[5,56,128]{2,1,0:T(8,128)S(1)} %get-tuple-element.30.left_ref), channel_id=1, source_target_pairs={{0,1},{1,2},{2,3},{3,0},{4,5},{5,6},{6,7},{7,4},{8,9},{9,10},{10,1... | collective-permute-start | bytes 430088 | tf_op jit(solution)/shard_map/ppermute | solution.py:609
  18.1 4.5 %collective-permute-start.5 = (f32[8,128]{1,0:T(8,128)S(1)}, f32[8,128]{1,0:T(8,128)S(1)}, u32[]{:S(2)}, u32[]{:S(2)}) collective-permute-start(f32[8,128]{1,0:T(8,128)S(1)} %get-tuple-element.31), channel_id=1, source_target_pairs={{0,16},{8,24},{16,0},{24,8},{1,17},{9,25},{17,1},{25,9},{2,18},{10... | collective-permute-start | bytes 12296 | tf_op jit(solution)/shard_map/ppermute | solution.py:546
  22.6 1.2 %collective-permute-start.6 = (f32[8,128]{1,0:T(8,128)S(1)}, f32[8,128]{1,0:T(8,128)S(1)}, u32[]{:S(2)}, u32[]{:S(2)}) collective-permute-start(f32[8,128]{1,0:T(8,128)S(1)} %max.12), channel_id=1, source_target_pairs={{0,1},{1,0},{2,3},{3,2},{4,5},{5,4},{6,7},{7,6},{8,9},{9,8},{10,11... | collective-permute-start | bytes 12296 | tf_op jit(solution)/shard_map/ppermute | solution.py:546
  24.0 7.8 %collective-permute-start.7 = (f32[5,72,128]{2,1,0:T(8,128)S(1)}, f32[5,72,128]{2,1,0:T(8,128)S(1)}, u32[]{:S(2)}, u32[]{:S(2)}) collective-permute-start(f32[5,72,128]{2,1,0:T(8,128)S(1)} %get-tuple-element.34), channel_id=1, source_target_pairs={{0,4},{4,0},{1,5},{5,1},{2,6},{6,2},{3,7},{7,3},{8,12},{12,8},{9,1... | collective-permute-start | bytes 552968 | tf_op jit(solution)/shard_map/ppermute | solution.py:601
  24.6 3.6 %collective-permute-start.8 = (f32[8,128]{1,0:T(8,128)S(1)}, f32[8,128]{1,0:T(8,128)S(1)}, u32[]{:S(2)}, u32[]{:S(2)}) collective-permute-start(f32[8,128]{1,0:T(8,128)S(1)} %max.13), channel_id=1, source_target_pairs={{0,2},{1,3},{2,0},{3,1},{4,6},{5,7},{6,4},{7,5},{8,10},{9,11},{10,... | collective-permute-start | bytes 12296 | tf_op jit(solution)/shard_map/ppermute | solution.py:546
  28.2 3.6 %collective-permute-start.9 = (f32[8,128]{1,0:T(8,128)S(1)}, f32[8,128]{1,0:T(8,128)S(1)}, u32[]{:S(2)}, u32[]{:S(2)}) collective-permute-start(f32[8,128]{1,0:T(8,128)S(1)} %max.14), channel_id=1, source_target_pairs={{0,4},{4,0},{1,5},{5,1},{2,6},{6,2},{3,7},{7,3},{8,12},{12,8},{9,1... | collective-permute-start | bytes 12296 | tf_op jit(solution)/shard_map/ppermute | solution.py:546
  31.8 16.0 %copy-start.3 = (s32[8,256]{1,0:T(8,128)S(1)}, s32[8,256]{1,0:T(8,128)}, u32[]{:S(2)}) copy-start(s32[8,256]{1,0:T(8,128)} %index_ref.3) | copy-start | bytes 24580
  31.8 16.0 %copy-start.4 = (f32[4,256]{1,0:T(4,128)S(1)}, f32[4,256]{1,0:T(4,128)}, u32[]{:S(2)}) copy-start(f32[4,256]{1,0:T(4,128)} %palette_ref.3) | copy-start | bytes 12292
  52.0 6.3 %collective-permute-start.10 = (f32[4,4,24,128]{3,2,1,0:T(8,128)S(1)}, f32[4,4,24,128]{3,2,1,0:T(8,128)S(1)}, u32[]{:S(2)}, u32[]{:S(2)}) collective-permute-start(f32[4,4,24,128]{3,2,1,0:T(8,128)S(1)} %bitcast.12), channel_id=1, source_target_pairs={{0,4},{4,0},{1,5},{5,1},{2,6},{6,2},{3,7},{7,3},{8,12},{12,8},{9,1... | collective-permute-start | bytes 589832 | tf_op jit(solution)/shard_map/ppermute | solution.py:585
  57.8 5.7 %collective-permute-start.11 = (f32[4,4,24,128]{3,2,1,0:T(8,128)S(1)}, f32[4,4,24,128]{3,2,1,0:T(8,128)S(1)}, u32[]{:S(2)}, u32[]{:S(2)}) collective-permute-start(f32[4,4,24,128]{3,2,1,0:T(8,128)S(1)} %bitcast.13), channel_id=1, source_target_pairs={{0,4},{4,0},{1,5},{5,1},{2,6},{6,2},{3,7},{7,3},{8,12},{12,8},{9,1... | collective-permute-start | bytes 589832 | tf_op jit(solution)/shard_map/ppermute | solution.py:585

commit v4 on v3

--- a/solution.py
+++ b/solution.py
@@ -8,11 +8,13 @@
 from jax.experimental.pallas import tpu as pltpu
 from jax.sharding import PartitionSpec as P
 
+
 HEAT_RATIO = 1.4
 COURANT = 0.8
 REACH = 3
 WINDOW = 3 * REACH
 SUB = 8
+PIECES = 3
 VMEM = pl.BlockSpec(memory_space=pltpu.VMEM)
 MIB = 1 << 20
 
@@ -46,7 +48,7 @@
 
 
 def fluxes(state, normal, pressure, component):
-    rho, mx, my, mz, energy = state
+    _, mx, my, mz, energy = state
     rows = [state[component], mx * normal, my * normal, mz * normal, (energy + pressure) * normal]
     rows[component] = rows[component] + pressure
     return rows
@@ -60,8 +62,16 @@
     ]
 
 
-def opening_kernel(rho_ref, vel_ref, pre_ref, state_ref, zpay_ref, low_ref, high_ref, top_ref):
+def opening_kernel(
+    rho_hbm, vel_hbm, pre_hbm, state_ref, zpay_ref, low_ref, high_ref, top_ref, rho_ref, vel_ref, pre_ref, sems
+):
     planes, rows, width = rho_ref.shape
+    pairs = ((rho_hbm, rho_ref), (vel_hbm, vel_ref), (pre_hbm, pre_ref))
+    copies = [pltpu.make_async_copy(src, dst, sems.at[i]) for i, (src, dst) in enumerate(pairs)]
+    for copy in copies:
+        copy.start()
+    for copy in copies:
+        copy.wait()
     edge = list(range(REACH)) + list(range(planes - REACH, planes))
     fastest = None
     for z in range(planes):
@@ -96,11 +106,17 @@
             jax.ShapeDtypeStruct((5 * planes * REACH + SUB, width), f32),
             jax.ShapeDtypeStruct((SUB, width), f32),
         ],
-        in_specs=[VMEM] * 3,
+        in_specs=[pl.BlockSpec(memory_space=pltpu.HBM)] * 3,
         out_specs=[VMEM] * 5,
+        scratch_shapes=[
+            pltpu.VMEM(density.shape, f32),
+            pltpu.VMEM(velocity.shape, f32),
+            pltpu.VMEM(pressure.shape, f32),
+            pltpu.SemaphoreType.DMA((3,)),
+        ],
         name="opening",
         compiler_params=grant(8),
-    )(density, velocity, pressure)
+    )(*[pltpu.with_memory_space_constraint(a, pltpu.HBM) for a in (density, velocity, pressure)])
 
 
 def window_kernel(
@@ -191,7 +207,7 @@
 
 
 def strips_of(wide, right, left, from_right, from_left):
-    planes, total, width = wide.shape[1:]
+    _, total, width = wide.shape[1:]
     f32 = jnp.float32
     return pl.pallas_call(
         strip_kernel,
@@ -231,7 +247,8 @@
         zone_refs, pay_refs = refs[1:3], refs[3:5]
         rest = refs[7:]
     out_ref, rho_ref, heat_ref = rest[:3]
-    main, strip, (fx, gx, acc, fz, gz) = rest[3:7], rest[7:11], rest[11:]
+    main, strip, (fx, gx, acc, fz, gz) = rest[3:7], rest[7:11], rest[11:16]
+    strip_buffers = (rest[16:19], rest[19:22])
     planes, total, width = wide_ref.shape[1:]
     rows = out_ref.shape[2]
     tiles = total // SUB
@@ -262,61 +279,56 @@
             strip[0][1, f, cut, :] = jnp.where(lane >= far, after, right)
     half = jnp.broadcast_to(0.5 * COURANT / jnp.max(top_ref[...], keepdims=True), (SUB, width))
 
-    def x_pass(which, load, t):
+    def x_pass(buffers, load, t):
+        fx, gx, acc = buffers
         here, there = slice(SUB * t, SUB * (t + 1)), slice(SUB * t + 1, SUB * (t + 1) + 1)
         a, b = load(here), load(there)
         g = face(
-            [fx[which, f, here, :] for f in range(5)],
-            [fx[which, f, there, :] for f in range(5)],
+            [fx[f, here, :] for f in range(5)],
+            [fx[f, there, :] for f in range(5)],
             a,
             b,
-            fx[which, 5, here, :],
-            fx[which, 5, there, :],
+            fx[5, here, :],
+            fx[5, there, :],
         )
         for f in range(5):
-            gx[which, f, SUB * (t + 1) : SUB * (t + 2), :] = g[f]
-            below = gx[which, f, SUB * (t + 1) - 1 : SUB * (t + 2) - 1, :]
-            acc[which, f, here, :] = acc[which, f, here, :] + (below - g[f])
-
-    def keep_x(which, state, ux, pressure, sound, cut):
+            gx[f, SUB * (t + 1) : SUB * (t + 2), :] = g[f]
+            below = gx[f, SUB * (t + 1) - 1 : SUB * (t + 2) - 1, :]
+            acc[f, here, :] = acc[f, here, :] + (below - g[f])
+
+    def keep_x(fx, state, ux, pressure, sound, cut):
         for f, v in enumerate(fluxes(state, ux, pressure, 1)):
-            fx[which, f, cut, :] = v
-        fx[which, 5, cut, :] = jnp.abs(ux) + sound
-
-    def strip_section(section, side):
-        source, target = strip[section], strip[section + 1]
-
-        def load(cut):
-            return [source[side, f, cut, :] for f in range(5)]
-
-        def finish(t):
+            fx[f, cut, :] = v
+        fx[5, cut, :] = jnp.abs(ux) + sound
+
+    def strip_start(section, side, t):
+        source, (fx, gx, acc) = strip[section], strip_buffers[side]
+        cut = pl.ds(pl.multiple_of(SUB * t, SUB), SUB)
+        state = [source[side, f, cut, :] for f in range(5)]
+        ux, uy, uz, pressure, sound = primitives(*state)
+        keep_x(fx, state, ux, pressure, sound, cut)
+        change = along_y(state, fluxes(state, uy, pressure, 2), uy, pressure, jnp.abs(uy) + sound)
+        signal = jnp.abs(uz) + sound
+        other = [ahead(v, WINDOW) for v in state]
+        g = face(
+            fluxes(state, uz, pressure, 3),
+            fluxes(other, ahead(uz, WINDOW), ahead(pressure, WINDOW), 3),
+            state,
+            other,
+            signal,
+            ahead(signal, WINDOW),
+        )
+        for f in range(5):
+            acc[f, cut, :] = change[f] + (behind(g[f], WINDOW) - g[f])
+
+    def strip_finish(section, side):
+        source, target, buffers = strip[section], strip[section + 1], strip_buffers[side]
+        for t in range(tiles):
             cut = slice(SUB * t, SUB * (t + 1))
-            x_pass(side, load, t)
+            x_pass(buffers, lambda at: [source[side, f, at, :] for f in range(5)], t)
             for f in range(5):
                 here, base = source[side, f, cut, :], strip[0][side, f, cut, :]
-                target[side, f, cut, :] = blend(section, base, here, acc[side, f, cut, :], half)
-
-        for t in range(tiles):
-            cut = slice(SUB * t, SUB * (t + 1))
-            state = load(cut)
-            ux, uy, uz, pressure, sound = primitives(*state)
-            keep_x(side, state, ux, pressure, sound, cut)
-            change = along_y(state, fluxes(state, uy, pressure, 2), uy, pressure, jnp.abs(uy) + sound)
-            signal = jnp.abs(uz) + sound
-            other = [ahead(v, WINDOW) for v in state]
-            g = face(
-                fluxes(state, uz, pressure, 3),
-                fluxes(other, ahead(uz, WINDOW), ahead(pressure, WINDOW), 3),
-                state,
-                other,
-                signal,
-                ahead(signal, WINDOW),
-            )
-            for f in range(5):
-                acc[side, f, cut, :] = change[f] + (behind(g[f], WINDOW) - g[f])
-            if t:
-                finish(t - 1)
-        finish(tiles - 1)
+                target[side, f, cut, :] = blend(section, base, here, buffers[2][f, cut, :], half)
 
     def main_section(section, first, last):
         source, target, base = main[section], main[section + 1], main[0]
@@ -336,7 +348,7 @@
                     g = face(flux_before, flux, before, state, fz[5, cut, :], signal)
                     for f in range(5):
                         if with_finish:
-                            change = acc[0, f, cut, :] + (gz[f, cut, :] - g[f])
+                            change = acc[f, cut, :] + (gz[f, cut, :] - g[f])
                             started = base[f, w - 1, cut, :] if section else None
                             target[f, w - 1, cut, :] = blend(section, started, before[f], change, half)
                         if with_sides:
@@ -346,30 +358,37 @@
                         fz[f, cut, :] = flux[f]
                     fz[5, cut, :] = signal
                 if with_sides:
-                    keep_x(0, state, ux, pressure, sound, cut)
+                    keep_x(fx, state, ux, pressure, sound, cut)
                     flux = fluxes(state, uy, pressure, 2)
                     change = along_y(state, flux, uy, pressure, jnp.abs(uy) + sound)
                     for f in range(5):
-                        acc[0, f, cut, :] = change[f]
+                        acc[f, cut, :] = change[f]
                     if t:
-                        x_pass(0, load, t - 1)
+                        x_pass((fx, gx, acc), load, t - 1)
             if with_sides:
-                x_pass(0, load, tiles - 1)
+                x_pass((fx, gx, acc), load, tiles - 1)
 
         plane(first - 1, False, False, False)
         plane(first, True, False, True)
 
+        count = last - first - 1
+        for t in range(tiles - count):
+            for side in range(2):
+                strip_start(section, side, count + t)
+
         def step(w, carry):
             plane(w, True, True, True)
+            for side in range(2):
+                strip_start(section, side, jnp.minimum(w - first - 1, tiles - 1))
             return carry
 
         lax.fori_loop(first + 1, last, step, 0)
         plane(last, True, True, False)
 
     for section in range(3):
+        main_section(section, 1 + section, planes + 2 * REACH - 1 - section)
         for side in range(2):
-            strip_section(section, side)
-        main_section(section, 1 + section, planes + 2 * REACH - 1 - section)
+            strip_finish(section, side)
     column = lane % WINDOW
     for f in range(5):
         for t in range(rows // SUB):
@@ -404,12 +423,18 @@
         scratch_shapes=[pltpu.VMEM((5, deep, tall, width), f32)] * 4
         + [pltpu.VMEM((2, 5, tall, width), f32)] * 4
         + [
-            pltpu.VMEM((2, 6, tall, width), f32),
-            pltpu.VMEM((2, 5, tall, width), f32),
-            pltpu.VMEM((2, 5, total, width), f32),
+            pltpu.VMEM((6, tall, width), f32),
+            pltpu.VMEM((5, tall, width), f32),
+            pltpu.VMEM((5, total, width), f32),
             pltpu.VMEM((6, total, width), f32),
             pltpu.VMEM((5, total, width), f32),
-        ],
+        ]
+        + [
+            pltpu.VMEM((6, tall, width), f32),
+            pltpu.VMEM((5, tall, width), f32),
+            pltpu.VMEM((5, total, width), f32),
+        ]
+        * 2,
         name="sections",
         compiler_params=grant(24),
     )(*args)
@@ -432,13 +457,14 @@
 
 
 LEVELS = 65535
+UNROLL = 4
 
 
 def render_kernel(
     scale, begin, count, halves, rho_ref, heat_ref, palette_ref, index_ref, *refs
 ):
     outs, (table, ke, ko, we, wo, thick) = refs[: len(refs) - 6], refs[len(refs) - 6 :]
-    planes, rows, width = rho_ref.shape
+    planes, _, width = rho_ref.shape
     count_tf, bins = index_ref.shape
     half = bins // 2
     chosen = index_ref[...]
@@ -481,7 +507,12 @@
     base_low = jnp.broadcast_to(least, (count_tf, width))
     base_high = base_low + jnp.broadcast_to(step, (count_tf, width)) * ((LEVELS + 1) // 2)
 
-    def ray(x, carry):
+    def rays(group, carry):
+        for i in range(UNROLL):
+            ray(group * UNROLL + i)
+        return carry
+
+    def ray(x):
         trans = jnp.ones((count_tf, width), jnp.float32)
         light = [jnp.zeros((count_tf, width), jnp.float32) for _ in range(3)]
         for z in range(planes):
@@ -513,13 +544,12 @@
                 out[pl.ds(c * count + x, per_out, stride=4 * count), :] = values[
                     per_out * i : per_out * (i + 1)
                 ]
-        return carry
-
-    lax.fori_loop(0, count, ray, 0)
+
+    lax.fori_loop(0, count // UNROLL, rays, 0)
 
 
 def render(rho, heat, palette, index, scale, begin, count, halves):
-    planes, rows, width = rho.shape
+    planes, _, width = rho.shape
     count_tf, bins = index.shape
     parts = 2 if halves else 1
     per_out = count_tf // parts
@@ -531,7 +561,6 @@
         in_specs=[VMEM] * 4,
         out_specs=[VMEM] * parts,
         scratch_shapes=[pltpu.VMEM((2, 2, count_tf, bins // 2), jnp.int32)] + scratch,
-        name=f"render_{begin}",
         compiler_params=grant(8),
     )(rho, heat, palette, index)
     return [out.reshape(per_out, 4, count, width) for out in outs]
@@ -577,23 +606,24 @@
         (shares,) = render(rho, heat, palette, index, scale, 0, rows, False)
         parts = shares.reshape((depth, shares.shape[0] // depth) + shares.shape[1:])
         return composed(lax.all_to_all(parts, "depth", 0, 0, tiled=True))
-    chunk = rows // 2 if rows % (2 * SUB) == 0 else rows
+    pieces = PIECES if rows % (PIECES * SUB) == 0 else 1
+    chunk = rows // pieces
     kept, sent = [], []
-    for begin in range(0, rows, chunk):
-        other, own = render(rho, heat, palette, index, scale, begin, chunk, True)
+    for i in range(pieces):
+        other, own = render(rho, heat, palette, index, scale, i * chunk, chunk, True)
         kept.append(own)
         sent.append(lax.ppermute(other, "depth", along("depth", 1, True)))
     in_front = lax.axis_index("depth") == 0
-    pieces = []
+    shown = []
     for own, other in zip(kept, sent):
         front, back = jnp.where(in_front, own, other), jnp.where(in_front, other, own)
-        pieces.append(front[:, :3] + front[:, 3:] * back[:, :3])
-    return jnp.concatenate(pieces, axis=2)
-
-
-def shards(density, velocity, pressure, palette, palette_index):
-    depth, groups = lax.axis_size("depth"), lax.axis_size("group")
-    planes, rows = density.shape[:2]
+        shown.append(front[:, :3] + front[:, 3:] * back[:, :3])
+    return jnp.concatenate(shown, axis=2)
+
+
+def whole_step(density, velocity, pressure, palette, palette_index):
+    depth = lax.axis_size("depth")
+    _, rows = density.shape[:2]
     state, zone, low, high, top = opening(density, velocity, pressure)
 
     def both_ways(block):
@@ -601,13 +631,13 @@
             return (lax.ppermute(block, "depth", along("depth", 1, True)),)
         return tuple(lax.ppermute(block, "depth", along("depth", d, True)) for d in (1, -1))
 
-    zones = both_ways(zone)
     from_below = lax.ppermute(high, "group", along("group", 1, False))
     from_above = lax.ppermute(low, "group", along("group", -1, False))
+    zones = both_ways(zone)
     wide, right, left, top = windows(state, from_below, from_above, top)
     from_right = lax.ppermute(right, "image", along("image", -1, True))
     from_left = lax.ppermute(left, "image", along("image", 1, True))
-    if groups == 4:
+    if lax.axis_size("group") == 4:
         top = exchange_max(top, "group", 2)
     else:
         top = largest(top, "group")
@@ -622,7 +652,7 @@
 
 def solution(mesh):
     return jax.shard_map(
-        shards,
+        whole_step,
         mesh=mesh,
         in_specs=(
             P("depth", "group", "image"),

time: 64.6 us -> 57.5 us (0.89)
  Pallas kernels: 25.8 us -> 21 us
  local copies, waits for them, and re-layouts: 2.93 us -> 0.03 us
  starting transfers between devices: 16.8 us -> 18.3 us
  waiting for transfers between devices: 17.1 us -> 16.3 us
    pallas_call x1, Pallas kernels: 16 us -> 12.7 us  [sections(): pl.pallas_call(functools.partial(section_kernel, shared), out_shape=[jax....]
    unnamed x10 -> x4, local copies, waits for them, and re-layouts: 2.92 us -> 0.01 us
    pallas_call x2 -> x3, Pallas kernels: 8.36 us -> 5.59 us  [render(): pl.pallas_call(functools.partial(render_kernel, scale, begin, count, halv...]
    ppermute x2 -> x3, starting transfers between devices: 2.16 us -> 3.65 us  [pictured(): sent.append(lax.ppermute(other, 'depth', along('depth', 1, True)))]
    pallas_call x1, Pallas kernels: 0.23 us -> 1.46 us  [opening(): pl.pallas_call(opening_kernel, out_shape=[jax.ShapeDtypeStruct((5, planes...]
    ppermute x2 -> x3, waiting for transfers between devices: 5.09 us -> 4.28 us  [pictured(): sent.append(lax.ppermute(other, 'depth', along('depth', 1, True)))]
  transfers between devices with their start and end apart: 12 -> 13, of which waited for: 7 -> 8; matrix products, arithmetic and copies ran while one was open for 0% -> 0% of each run, Pallas kernels for 8% -> 9%
where the time goes in v4:
time: 57.5 us; the launch traced here: 57.3 us
  Pallas kernels  21 us (37%)
  starting transfers between devices  18.3 us (32%)
  waiting for transfers between devices  16.3 us (28%)
  other arithmetic  0.88 us (2%)
  between operations  0.77 us (1%)
    pallas_call x1, Pallas kernels, sections(): pl.pallas_call(functools.partial(section_kernel, shared), out_shape=[jax....  12.7 us
    ppermute x4, waiting for transfers between devices, exchange_max(): return jnp.maximum(value, lax.ppermute(value, axis, route))  7.17 us
    ppermute x4, starting transfers between devices, exchange_max(): return jnp.maximum(value, lax.ppermute(value, axis, route))  5.72 us
    pallas_call x3, Pallas kernels, render(): pl.pallas_call(functools.partial(render_kernel, scale, begin, count, halv...  5.59 us
    ppermute x3, waiting for transfers between devices, pictured(): sent.append(lax.ppermute(other, 'depth', along('depth', 1, True)))  4.28 us
    ppermute x1, waiting for transfers between devices, whole_step(): from_above = lax.ppermute(low, 'group', along('group', -1, False))  4.27 us
    ppermute x3, starting transfers between devices, pictured(): sent.append(lax.ppermute(other, 'depth', along('depth', 1, True)))  3.65 us
    ppermute x2, starting transfers between devices, both_ways(): return (lax.ppermute(block, 'depth', along('depth', 1, True)),)  3.63 us
  transfers between devices with their start and end apart: 13, of which 8 were waited for; matrix products, arithmetic and copies ran while one was open for 0% of the time, Pallas kernels for 9%

profile of v4, /device:TPU:0, one launch (start us, length us, event | category | flops | bytes accessed | tf_op | source)
XLA Modules:
  0.0 57.3 jit_solution(17314054394018878052)
XLA Ops:
  0.6 1.5 %opening.1 = (f32[5,8,48,128]{3,2,1,0:T(8,128)S(1)}, f32[5,6,48,128]{3,2,1,0:T(8,128)S(1)}, f32[128,128]{1,0:T(8,128)S(1)}, f32[128,128]{1,0:T(8,128)S(1)}, f32[8,128]{1,0:T(8,128)S(1)}) custom-call(f32[8,48,128]{2,1,0:T(8,128)} %rho_hbm.1, f32[3,8,48,128]{3,2,1,0:T(8,128)} %vel_hbm.1, f32[8,48,128]{2,1,0:T(8,128)} %pre_hbm.1), custom_call_target="tpu_custom_call" | custom-call | tf_op jit(solution)/shard_map/opening/pallas_call | solution.py:100
  2.1 3.0 %collective-permute-start.2 = (f32[5,6,48,128]{3,2,1,0:T(8,128)S(1)}, f32[5,6,48,128]{3,2,1,0:T(8,128)S(1)}, u32[]{:S(2)}, u32[]{:S(2)}) collective-permute-start(f32[5,6,48,128]{3,2,1,0:T(8,128)S(1)} %get-tuple-element.30), channel_id=1, source_target_pairs={{0,4},{4,0},{1,5},{5,1},{2,6},{6,2},{3,7},{7,3},{8,12},{12,8},{9,1... | collective-permute-start | bytes 2211848 | tf_op jit(solution)/shard_map/ppermute | solution.py:631
  5.1 3.5 %collective-permute-start = (f32[128,128]{1,0:T(8,128)S(1)}, f32[128,128]{1,0:T(8,128)S(1)}, u32[]{:S(2)}, u32[]{:S(2)}) collective-permute-start(f32[128,128]{1,0:T(8,128)S(1)} %get-tuple-element.26), channel_id=1, source_target_pairs={{0,8},{8,16},{16,24},{1,9},{9,17},{17,25},{2,10},{10,18},{18,26},{... | collective-permute-start | bytes 196616 | tf_op jit(solution)/shard_map/ppermute | solution.py:634
  8.6 1.3 %collective-permute-start.1 = (f32[128,128]{1,0:T(8,128)S(1)}, f32[128,128]{1,0:T(8,128)S(1)}, u32[]{:S(2)}, u32[]{:S(2)}) collective-permute-start(f32[128,128]{1,0:T(8,128)S(1)} %get-tuple-element.27), channel_id=1, source_target_pairs={{8,0},{16,8},{24,16},{9,1},{17,9},{25,17},{10,2},{18,10},{26,18},{... | collective-permute-start | bytes 196616 | tf_op jit(solution)/shard_map/ppermute | solution.py:635
  9.9 0.6 %collective-permute-done.low_ref = f32[128,128]{1,0:T(8,128)S(1)} collective-permute-done((f32[128,128]{1,0:T(8,128)S(1)}, f32[128,128]{1,0:T(8,128)S(1)}, u32[]{:S(2)}, u32[]{:S(2)}) %collective-permute-start) | collective-permute-done | bytes 65568 | tf_op jit(solution)/shard_map/ppermute | solution.py:634
  10.5 4.3 %collective-permute-done.1.high_ref = f32[128,128]{1,0:T(8,128)S(1)} collective-permute-done((f32[128,128]{1,0:T(8,128)S(1)}, f32[128,128]{1,0:T(8,128)S(1)}, u32[]{:S(2)}, u32[]{:S(2)}) %collective-permute-start.1) | collective-permute-done | bytes 65568 | tf_op jit(solution)/shard_map/ppermute | solution.py:635
  14.8 1.1 %windows.1 = (f32[5,8,56,128]{3,2,1,0:T(8,128)S(1)}, f32[5,56,128]{2,1,0:T(8,128)S(1)}, f32[5,56,128]{2,1,0:T(8,128)S(1)}, f32[8,128]{1,0:T(8,128)S(1)}) custom-call(f32[5,8,48,128]{3,2,1,0:T(8,128)S(1)} %get-tuple-element.25.state_ref, f32[128,128]{1,0:T(8,128)S(1)} %collective-permute-done.low_ref, f32[128,128]{1,0:T(8,128)S(1)} %collective-permute-done.1.high_ref, ...), custom_call_target="tpu_custom_call" | custom-call | tf_op jit(solution)/shard_map/windows/pallas_call | solution.py:167
  15.9 0.1 collective-permute-start.3
  15.9 0.5 collective-permute-start.4
  16.4 2.6 %collective-permute-start.5 = (f32[8,128]{1,0:T(8,128)S(1)}, f32[8,128]{1,0:T(8,128)S(1)}, u32[]{:S(2)}, u32[]{:S(2)}) collective-permute-start(f32[8,128]{1,0:T(8,128)S(1)} %get-tuple-element.33), channel_id=1, source_target_pairs={{0,16},{8,24},{16,0},{24,8},{1,17},{9,25},{17,1},{25,9},{2,18},{10... | collective-permute-start | bytes 12296 | tf_op jit(solution)/shard_map/ppermute | solution.py:575
  19.0 1.9 %collective-permute-done.5 = f32[8,128]{1,0:T(8,128)S(1)} collective-permute-done((f32[8,128]{1,0:T(8,128)S(1)}, f32[8,128]{1,0:T(8,128)S(1)}, u32[]{:S(2)}, u32[]{:S(2)}) %collective-permute-start.5) | collective-permute-done | bytes 4128 | tf_op jit(solution)/shard_map/ppermute | solution.py:575
  20.9 0.1 collective-permute-start.6
  21.1 1.1 %collective-permute-done.6 = f32[8,128]{1,0:T(8,128)S(1)} collective-permute-done((f32[8,128]{1,0:T(8,128)S(1)}, f32[8,128]{1,0:T(8,128)S(1)}, u32[]{:S(2)}, u32[]{:S(2)}) %collective-permute-start.6) | collective-permute-done | bytes 4128 | tf_op jit(solution)/shard_map/ppermute | solution.py:575
  22.1 0.0 collective-permute-done.3.from_right
  22.1 0.0 collective-permute-done.4.from_left
  22.1 0.2 strips.1
  22.3 0.6 %collective-permute-start.7 = (f32[5,72,128]{2,1,0:T(8,128)S(1)}, f32[5,72,128]{2,1,0:T(8,128)S(1)}, u32[]{:S(2)}, u32[]{:S(2)}) collective-permute-start(f32[5,72,128]{2,1,0:T(8,128)S(1)} %get-tuple-element.36), channel_id=1, source_target_pairs={{0,4},{4,0},{1,5},{5,1},{2,6},{6,2},{3,7},{7,3},{8,12},{12,8},{9,1... | collective-permute-start | bytes 552968 | tf_op jit(solution)/shard_map/ppermute | solution.py:631
  22.9 1.5 %collective-permute-start.8 = (f32[8,128]{1,0:T(8,128)S(1)}, f32[8,128]{1,0:T(8,128)S(1)}, u32[]{:S(2)}, u32[]{:S(2)}) collective-permute-start(f32[8,128]{1,0:T(8,128)S(1)} %max.13), channel_id=1, source_target_pairs={{0,2},{1,3},{2,0},{3,1},{4,6},{5,7},{6,4},{7,5},{8,10},{9,11},{10,... | collective-permute-start | bytes 12296 | tf_op jit(solution)/shard_map/ppermute | solution.py:575
  24.4 2.1 %collective-permute-done.8 = f32[8,128]{1,0:T(8,128)S(1)} collective-permute-done((f32[8,128]{1,0:T(8,128)S(1)}, f32[8,128]{1,0:T(8,128)S(1)}, u32[]{:S(2)}, u32[]{:S(2)}) %collective-permute-start.8) | collective-permute-done | bytes 4128 | tf_op jit(solution)/shard_map/ppermute | solution.py:575
  26.5 1.5 %collective-permute-start.9 = (f32[8,128]{1,0:T(8,128)S(1)}, f32[8,128]{1,0:T(8,128)S(1)}, u32[]{:S(2)}, u32[]{:S(2)}) collective-permute-start(f32[8,128]{1,0:T(8,128)S(1)} %max.14), channel_id=1, source_target_pairs={{0,4},{4,0},{1,5},{5,1},{2,6},{6,2},{3,7},{7,3},{8,12},{12,8},{9,1... | collective-permute-start | bytes 12296 | tf_op jit(solution)/shard_map/ppermute | solution.py:575
  28.0 2.1 %collective-permute-done.9 = f32[8,128]{1,0:T(8,128)S(1)} collective-permute-done((f32[8,128]{1,0:T(8,128)S(1)}, f32[8,128]{1,0:T(8,128)S(1)}, u32[]{:S(2)}, u32[]{:S(2)}) %collective-permute-start.9) | collective-permute-done | bytes 4128 | tf_op jit(solution)/shard_map/ppermute | solution.py:575
  30.1 0.0 collective-permute-done.7.refs_2_
  30.1 0.0 collective-permute-done.2.refs_1_
  30.1 0.0 copy-start
  30.1 0.0 copy-start.1
  30.1 12.7 %sections.1 = (f32[5,8,48,128]{3,2,1,0:T(8,128)}, f32[8,48,128]{2,1,0:T(8,128)S(1)}, f32[8,48,128]{2,1,0:T(8,128)S(1)}) custom-call(f32[5,8,56,128]{3,2,1,0:T(8,128)S(1)} %get-tuple-element.29.wide_ref.refs_0_, f32[5,6,48,128]{3,2,1,0:T(8,128)S(1)} %collective-permute-done.2.refs_1_, f32[5,72,128]{2,1,0:T(8,128)S(1)} %collective-permute-done.7.refs_2_, ...), custom_call_target="tpu_custom_call" | custom-call | tf_op jit(solution)/shard_map/sections/pallas_call | solution.py:418
  42.9 0.0 copy-done
  42.9 0.0 copy-done.1
  42.9 1.9 %shard_map.68 = (f32[256,128]{1,0:T(8,128)S(1)}, f32[256,128]{1,0:T(8,128)S(1)}) custom-call(f32[8,48,128]{2,1,0:T(8,128)S(1)} %get-tuple-element.40.rho_ref, f32[8,48,128]{2,1,0:T(8,128)S(1)} %get-tuple-element.41.heat_ref, f32[4,256]{1,0:T(4,128)S(1)} %copy-done.1, s32[8,256]{1,0:T(8,128)S(1)} %copy-done), custom_call_target="tpu_custom_call" | custom-call | tf_op jit(solution)/shard_map/pallas_call | solution.py:558
  44.7 1.6 %collective-permute-start.10 = (f32[4,4,16,128]{3,2,1,0:T(8,128)S(1)}, f32[4,4,16,128]{3,2,1,0:T(8,128)S(1)}, u32[]{:S(2)}, u32[]{:S(2)}) collective-permute-start(f32[4,4,16,128]{3,2,1,0:T(8,128)S(1)} %bitcast.18), channel_id=1, source_target_pairs={{0,4},{4,0},{1,5},{5,1},{2,6},{6,2},{3,7},{7,3},{8,12},{12,8},{9,1... | collective-permute-start | bytes 393224 | tf_op jit(solution)/shard_map/ppermute | solution.py:615
  46.3 1.9 %shard_map.69 = (f32[256,128]{1,0:T(8,128)S(1)}, f32[256,128]{1,0:T(8,128)S(1)}) custom-call(f32[8,48,128]{2,1,0:T(8,128)S(1)} %get-tuple-element.40.rho_ref, f32[8,48,128]{2,1,0:T(8,128)S(1)} %get-tuple-element.41.heat_ref, f32[4,256]{1,0:T(4,128)S(1)} %copy-done.1, s32[8,256]{1,0:T(8,128)S(1)} %copy-done), custom_call_target="tpu_custom_call" | custom-call | tf_op jit(solution)/shard_map/pallas_call | solution.py:558
  48.2 1.9 %shard_map.70 = (f32[256,128]{1,0:T(8,128)S(1)}, f32[256,128]{1,0:T(8,128)S(1)}) custom-call(f32[8,48,128]{2,1,0:T(8,128)S(1)} %get-tuple-element.40.rho_ref, f32[8,48,128]{2,1,0:T(8,128)S(1)} %get-tuple-element.41.heat_ref, f32[4,256]{1,0:T(4,128)S(1)} %copy-done.1, s32[8,256]{1,0:T(8,128)S(1)} %copy-done), custom_call_target="tpu_custom_call" | custom-call | tf_op jit(solution)/shard_map/pallas_call | solution.py:558
  50.0 0.6 %collective-permute-start.11 = (f32[4,4,16,128]{3,2,1,0:T(8,128)S(1)}, f32[4,4,16,128]{3,2,1,0:T(8,128)S(1)}, u32[]{:S(2)}, u32[]{:S(2)}) collective-permute-start(f32[4,4,16,128]{3,2,1,0:T(8,128)S(1)} %bitcast.20), channel_id=1, source_target_pairs={{0,4},{4,0},{1,5},{5,1},{2,6},{6,2},{3,7},{7,3},{8,12},{12,8},{9,1... | collective-permute-start | bytes 393224 | tf_op jit(solution)/shard_map/ppermute | solution.py:615
  50.6 1.5 %collective-permute-start.12 = (f32[4,4,16,128]{3,2,1,0:T(8,128)S(1)}, f32[4,4,16,128]{3,2,1,0:T(8,128)S(1)}, u32[]{:S(2)}, u32[]{:S(2)}) collective-permute-start(f32[4,4,16,128]{3,2,1,0:T(8,128)S(1)} %bitcast.19), channel_id=1, source_target_pairs={{0,4},{4,0},{1,5},{5,1},{2,6},{6,2},{3,7},{7,3},{8,12},{12,8},{9,1... | collective-permute-start | bytes 393224 | tf_op jit(solution)/shard_map/ppermute | solution.py:615
  52.1 0.0 collective-permute-done.10
  52.2 2.9 %collective-permute-done.11 = f32[4,4,16,128]{3,2,1,0:T(8,128)S(1)} collective-permute-done((f32[4,4,16,128]{3,2,1,0:T(8,128)S(1)}, f32[4,4,16,128]{3,2,1,0:T(8,128)S(1)}, u32[]{:S(2)}, u32[]{:S(2)}) %collective-permute-start.11) | collective-permute-done | bytes 131104 | tf_op jit(solution)/shard_map/ppermute | solution.py:615
  55.1 1.4 %collective-permute-done.12 = f32[4,4,16,128]{3,2,1,0:T(8,128)S(1)} collective-permute-done((f32[4,4,16,128]{3,2,1,0:T(8,128)S(1)}, f32[4,4,16,128]{3,2,1,0:T(8,128)S(1)}, u32[]{:S(2)}, u32[]{:S(2)}) %collective-permute-start.12) | collective-permute-done | bytes 131104 | tf_op jit(solution)/shard_map/ppermute | solution.py:615
  56.6 0.7 %pad_maximum_fusion = f32[4,3,48,128]{3,2,1,0:T(8,128)} fusion(f32[4,3,16,128]{3,2,1,0:T(8,128)S(1)} %fusion.1, f32[4,3,16,128]{3,2,1,0:T(8,128)S(1)} %fusion.3, f32[4,3,16,128]{3,2,1,0:T(8,128)S(1)} %fusion.5), kind=kLoop, calls=%fused_computation | loop fusion | flops 147456 | bytes 589824 | tf_op jit(solution)/shard_map/concatenate | solution.py:621
  (13 shorter events, 0.2 us)
Async XLA Ops:
  2.1 28.0 %collective-permute-start.2 = (f32[5,6,48,128]{3,2,1,0:T(8,128)S(1)}, f32[5,6,48,128]{3,2,1,0:T(8,128)S(1)}, u32[]{:S(2)}, u32[]{:S(2)}) collective-permute-start(f32[5,6,48,128]{3,2,1,0:T(8,128)S(1)} %get-tuple-element.30), channel_id=1, source_target_pairs={{0,4},{4,0},{1,5},{5,1},{2,6},{6,2},{3,7},{7,3},{8,12},{12,8},{9,1... | collective-permute-start | bytes 2211848 | tf_op jit(solution)/shard_map/ppermute | solution.py:631
  5.1 5.4 %collective-permute-start = (f32[128,128]{1,0:T(8,128)S(1)}, f32[128,128]{1,0:T(8,128)S(1)}, u32[]{:S(2)}, u32[]{:S(2)}) collective-permute-start(f32[128,128]{1,0:T(8,128)S(1)} %get-tuple-element.26), channel_id=1, source_target_pairs={{0,8},{8,16},{16,24},{1,9},{9,17},{17,25},{2,10},{10,18},{18,26},{... | collective-permute-start | bytes 196616 | tf_op jit(solution)/shard_map/ppermute | solution.py:634
  8.6 6.2 %collective-permute-start.1 = (f32[128,128]{1,0:T(8,128)S(1)}, f32[128,128]{1,0:T(8,128)S(1)}, u32[]{:S(2)}, u32[]{:S(2)}) collective-permute-start(f32[128,128]{1,0:T(8,128)S(1)} %get-tuple-element.27), channel_id=1, source_target_pairs={{8,0},{16,8},{24,16},{9,1},{17,9},{25,17},{10,2},{18,10},{26,18},{... | collective-permute-start | bytes 196616 | tf_op jit(solution)/shard_map/ppermute | solution.py:635
  15.9 6.2 %collective-permute-start.3 = (f32[5,56,128]{2,1,0:T(8,128)S(1)}, f32[5,56,128]{2,1,0:T(8,128)S(1)}, u32[]{:S(2)}, u32[]{:S(2)}) collective-permute-start(f32[5,56,128]{2,1,0:T(8,128)S(1)} %get-tuple-element.31.right_ref), channel_id=1, source_target_pairs={{0,3},{1,0},{2,1},{3,2},{4,7},{5,4},{6,5},{7,6},{8,11},{9,8},{10,9... | collective-permute-start | bytes 430088 | tf_op jit(solution)/shard_map/ppermute | solution.py:638
  15.9 6.2 %collective-permute-start.4 = (f32[5,56,128]{2,1,0:T(8,128)S(1)}, f32[5,56,128]{2,1,0:T(8,128)S(1)}, u32[]{:S(2)}, u32[]{:S(2)}) collective-permute-start(f32[5,56,128]{2,1,0:T(8,128)S(1)} %get-tuple-element.32.left_ref), channel_id=1, source_target_pairs={{0,1},{1,2},{2,3},{3,0},{4,5},{5,6},{6,7},{7,4},{8,9},{9,10},{10,1... | collective-permute-start | bytes 430088 | tf_op jit(solution)/shard_map/ppermute | solution.py:639
  16.4 4.5 %collective-permute-start.5 = (f32[8,128]{1,0:T(8,128)S(1)}, f32[8,128]{1,0:T(8,128)S(1)}, u32[]{:S(2)}, u32[]{:S(2)}) collective-permute-start(f32[8,128]{1,0:T(8,128)S(1)} %get-tuple-element.33), channel_id=1, source_target_pairs={{0,16},{8,24},{16,0},{24,8},{1,17},{9,25},{17,1},{25,9},{2,18},{10... | collective-permute-start | bytes 12296 | tf_op jit(solution)/shard_map/ppermute | solution.py:575
  20.9 1.2 %collective-permute-start.6 = (f32[8,128]{1,0:T(8,128)S(1)}, f32[8,128]{1,0:T(8,128)S(1)}, u32[]{:S(2)}, u32[]{:S(2)}) collective-permute-start(f32[8,128]{1,0:T(8,128)S(1)} %max.12), channel_id=1, source_target_pairs={{0,1},{1,0},{2,3},{3,2},{4,5},{5,4},{6,7},{7,6},{8,9},{9,8},{10,11... | collective-permute-start | bytes 12296 | tf_op jit(solution)/shard_map/ppermute | solution.py:575
  22.3 7.8 %collective-permute-start.7 = (f32[5,72,128]{2,1,0:T(8,128)S(1)}, f32[5,72,128]{2,1,0:T(8,128)S(1)}, u32[]{:S(2)}, u32[]{:S(2)}) collective-permute-start(f32[5,72,128]{2,1,0:T(8,128)S(1)} %get-tuple-element.36), channel_id=1, source_target_pairs={{0,4},{4,0},{1,5},{5,1},{2,6},{6,2},{3,7},{7,3},{8,12},{12,8},{9,1... | collective-permute-start | bytes 552968 | tf_op jit(solution)/shard_map/ppermute | solution.py:631
  22.9 3.6 %collective-permute-start.8 = (f32[8,128]{1,0:T(8,128)S(1)}, f32[8,128]{1,0:T(8,128)S(1)}, u32[]{:S(2)}, u32[]{:S(2)}) collective-permute-start(f32[8,128]{1,0:T(8,128)S(1)} %max.13), channel_id=1, source_target_pairs={{0,2},{1,3},{2,0},{3,1},{4,6},{5,7},{6,4},{7,5},{8,10},{9,11},{10,... | collective-permute-start | bytes 12296 | tf_op jit(solution)/shard_map/ppermute | solution.py:575
  26.5 3.6 %collective-permute-start.9 = (f32[8,128]{1,0:T(8,128)S(1)}, f32[8,128]{1,0:T(8,128)S(1)}, u32[]{:S(2)}, u32[]{:S(2)}) collective-permute-start(f32[8,128]{1,0:T(8,128)S(1)} %max.14), channel_id=1, source_target_pairs={{0,4},{4,0},{1,5},{5,1},{2,6},{6,2},{3,7},{7,3},{8,12},{12,8},{9,1... | collective-permute-start | bytes 12296 | tf_op jit(solution)/shard_map/ppermute | solution.py:575
  30.1 12.8 %copy-start = (s32[8,256]{1,0:T(8,128)S(1)}, s32[8,256]{1,0:T(8,128)}, u32[]{:S(2)}) copy-start(s32[8,256]{1,0:T(8,128)} %index_ref.5) | copy-start | bytes 24580
  30.1 12.8 %copy-start.1 = (f32[4,256]{1,0:T(4,128)S(1)}, f32[4,256]{1,0:T(4,128)}, u32[]{:S(2)}) copy-start(f32[4,256]{1,0:T(4,128)} %palette_ref.5) | copy-start | bytes 12292
  44.7 7.4 %collective-permute-start.10 = (f32[4,4,16,128]{3,2,1,0:T(8,128)S(1)}, f32[4,4,16,128]{3,2,1,0:T(8,128)S(1)}, u32[]{:S(2)}, u32[]{:S(2)}) collective-permute-start(f32[4,4,16,128]{3,2,1,0:T(8,128)S(1)} %bitcast.18), channel_id=1, source_target_pairs={{0,4},{4,0},{1,5},{5,1},{2,6},{6,2},{3,7},{7,3},{8,12},{12,8},{9,1... | collective-permute-start | bytes 393224 | tf_op jit(solution)/shard_map/ppermute | solution.py:615
  50.0 5.0 %collective-permute-start.11 = (f32[4,4,16,128]{3,2,1,0:T(8,128)S(1)}, f32[4,4,16,128]{3,2,1,0:T(8,128)S(1)}, u32[]{:S(2)}, u32[]{:S(2)}) collective-permute-start(f32[4,4,16,128]{3,2,1,0:T(8,128)S(1)} %bitcast.20), channel_id=1, source_target_pairs={{0,4},{4,0},{1,5},{5,1},{2,6},{6,2},{3,7},{7,3},{8,12},{12,8},{9,1... | collective-permute-start | bytes 393224 | tf_op jit(solution)/shard_map/ppermute | solution.py:615
  50.6 5.8 %collective-permute-start.12 = (f32[4,4,16,128]{3,2,1,0:T(8,128)S(1)}, f32[4,4,16,128]{3,2,1,0:T(8,128)S(1)}, u32[]{:S(2)}, u32[]{:S(2)}) collective-permute-start(f32[4,4,16,128]{3,2,1,0:T(8,128)S(1)} %bitcast.19), channel_id=1, source_target_pairs={{0,4},{4,0},{1,5},{5,1},{2,6},{6,2},{3,7},{7,3},{8,12},{12,8},{9,1... | collective-permute-start | bytes 393224 | tf_op jit(solution)/shard_map/ppermute | solution.py:615

commit v5 on v4

--- a/solution.py
+++ b/solution.py
@@ -63,7 +63,7 @@
 
 
 def opening_kernel(
-    rho_hbm, vel_hbm, pre_hbm, state_ref, zpay_ref, low_ref, high_ref, top_ref, rho_ref, vel_ref, pre_ref, sems
+    rho_hbm, vel_hbm, pre_hbm, state_ref, zpay_ref, one_ref, two_ref, top_ref, rho_ref, vel_ref, pre_ref, sems
 ):
     planes, rows, width = rho_ref.shape
     pairs = ((rho_hbm, rho_ref), (vel_hbm, vel_ref), (pre_hbm, pre_ref))
@@ -72,6 +72,7 @@
         copy.start()
     for copy in copies:
         copy.wait()
+    even = (lax.axis_index("group") & 1) == 0
     edge = list(range(REACH)) + list(range(planes - REACH, planes))
     fastest = None
     for z in range(planes):
@@ -87,10 +88,11 @@
             if z in edge:
                 zpay_ref[f, edge.index(z)] = fields[f]
             at = (f * planes + z) * REACH
-            low_ref[at : at + REACH, :] = fields[f][:REACH]
-            high_ref[at : at + REACH, :] = fields[f][rows - REACH :]
+            low, high = fields[f][:REACH], fields[f][rows - REACH :]
+            one_ref[at : at + REACH, :] = jnp.where(even, high, low)
+            two_ref[at : at + REACH, :] = jnp.where(even, low, high)
     top_ref[...] = fastest
-    for ref in (low_ref, high_ref):
+    for ref in (one_ref, two_ref):
         ref[5 * planes * REACH :, :] = fastest
 
 
@@ -120,13 +122,14 @@
 
 
 def window_kernel(
-    state_ref, low_ref, high_ref, top_ref, wide_ref, right_ref, left_ref, peak_ref
+    state_ref, one_ref, two_ref, top_ref, wide_ref, first_ref, second_ref, peak_ref
 ):
     planes, rows, width = state_ref.shape[1:]
     sent = slice(5 * planes * REACH, 5 * planes * REACH + SUB)
-    peak_ref[...] = jnp.maximum(top_ref[...], jnp.maximum(low_ref[sent, :], high_ref[sent, :]))
+    peak_ref[...] = jnp.maximum(top_ref[...], jnp.maximum(one_ref[sent, :], two_ref[sent, :]))
     total = wide_ref.shape[2]
     group, groups = lax.axis_index("group"), lax.axis_size("group")
+    even, even_image = (group & 1) == 0, (lax.axis_index("image") & 1) == 0
     lane = lax.broadcasted_iota(jnp.int32, (SUB, width), 1)
     for f in range(5):
         sign = -1.0 if f == 1 else 1.0
@@ -134,11 +137,14 @@
             at = (f * planes + z) * REACH
             wide_ref[f, z, REACH : REACH + rows, :] = state_ref[f, z]
             mirrored = [state_ref[f, z, r : r + 1, :] * sign for r in range(REACH - 1, -1, -1)]
-            below = jnp.where(group == 0, jnp.concatenate(mirrored, axis=0), low_ref[at : at + REACH, :])
+            one, two = one_ref[at : at + REACH, :], two_ref[at : at + REACH, :]
+            below = jnp.where(
+                group == 0, jnp.concatenate(mirrored, axis=0), jnp.where(even, two, one)
+            )
             wide_ref[f, z, :REACH, :] = below
             mirrored = [state_ref[f, z, rows - 1 - r : rows - r, :] * sign for r in range(REACH)]
             above = jnp.where(
-                group == groups - 1, jnp.concatenate(mirrored, axis=0), high_ref[at : at + REACH, :]
+                group == groups - 1, jnp.concatenate(mirrored, axis=0), jnp.where(even, one, two)
             )
             wide_ref[f, z, REACH + rows : 2 * REACH + rows, :] = above
 
@@ -153,14 +159,14 @@
                 values = wide_ref[f, z, cut, :]
                 right = jnp.where(inside, turned(values, start - (width - 2 * REACH)), right)
                 left = jnp.where(inside, turned(values, start - (width - REACH)), left)
-            right_ref[f, cut, :] = right
-            left_ref[f, cut, :] = left
+            first_ref[f, cut, :] = jnp.where(even_image, left, right)
+            second_ref[f, cut, :] = jnp.where(even_image, right, left)
         return carry
 
     lax.fori_loop(0, 5, fields, 0)
 
 
-def windows(state, low, high, top):
+def windows(state, one, two, top):
     planes, rows, width = state.shape[1:]
     total = padded_rows(rows)
     f32 = jnp.float32
@@ -176,26 +182,33 @@
         out_specs=[VMEM] * 4,
         name="windows",
         compiler_params=grant(8),
-    )(state, low, high, top)
-
-
-def strip_kernel(wide_ref, right_ref, left_ref, from_right, from_left, strips_ref, pay_ref):
+    )(state, one, two, top)
+
+
+def strip_kernel(wide_ref, first_ref, second_ref, got_first, got_second, strips_ref, pay_ref):
+    even = (lax.axis_index("image") & 1) == 0
     planes, total, width = wide_ref.shape[1:]
     rows = total - 2 * REACH - (total - 2 * REACH) % SUB
     lane = lax.broadcasted_iota(jnp.int32, (SUB, width), 1)
     column = lane % WINDOW
     span = WINDOW * REACH
-    first, last = WINDOW * REACH, WINDOW * planes
+    start, last = WINDOW * REACH, WINDOW * planes
     far = WINDOW * (REACH + planes)
     for f in range(5):
         for t in range(total // SUB):
             cut = slice(SUB * t, SUB * (t + 1))
-            right = jnp.where(column >= 2 * REACH, from_right[f, cut, :], right_ref[f, cut, :])
-            left = jnp.where(column < REACH, from_left[f, cut, :], left_ref[f, cut, :])
+            first, second = first_ref[f, cut, :], second_ref[f, cut, :]
+            near, after = got_first[f, cut, :], got_second[f, cut, :]
+            right = jnp.where(
+                column >= 2 * REACH, jnp.where(even, near, after), jnp.where(even, second, first)
+            )
+            left = jnp.where(
+                column < REACH, jnp.where(even, after, near), jnp.where(even, first, second)
+            )
             strips_ref[0, f, cut, :] = left
             strips_ref[1, f, cut, :] = right
             sent = jnp.where(lane < span, turned(right, -last), left)
-            pay_ref[f, cut, :] = jnp.where(lane >= far, turned(right, far - first), sent)
+            pay_ref[f, cut, :] = jnp.where(lane >= far, turned(right, far - start), sent)
         low, high = REACH - 1, REACH + rows
         for side, (near, next_one) in enumerate(((0, 1), (planes - 1, planes - 2))):
             at = total + SUB * side
@@ -206,7 +219,7 @@
             pay_ref[f, at + 6 : at + 8, :] = jnp.zeros((2, width), jnp.float32)
 
 
-def strips_of(wide, right, left, from_right, from_left):
+def strips_of(wide, first, second, got_first, got_second):
     _, total, width = wide.shape[1:]
     f32 = jnp.float32
     return pl.pallas_call(
@@ -219,7 +232,7 @@
         out_specs=[VMEM] * 2,
         name="strips",
         compiler_params=grant(8),
-    )(wide, right, left, from_right, from_left)
+    )(wide, first, second, got_first, got_second)
 
 
 def blend(section, base, here, change, half):
@@ -417,7 +430,7 @@
     brick = jax.ShapeDtypeStruct((planes, rows, width), f32)
     return pl.pallas_call(
         functools.partial(section_kernel, shared),
-        out_shape=[jax.ShapeDtypeStruct((5, planes, rows, width), f32), brick, brick],
+        out_shape=[pltpu.VMEM((5, planes, rows, width), f32), brick, brick],
         in_specs=[VMEM] * len(args),
         out_specs=[VMEM] * 3,
         scratch_shapes=[pltpu.VMEM((5, deep, tall, width), f32)] * 4
@@ -575,6 +588,23 @@
     return jnp.maximum(value, lax.ppermute(value, axis, route))
 
 
+def last_rounds(value):
+    images, depth = lax.axis_size("image"), lax.axis_size("depth")
+    if images != 4 or depth != 2:
+        return largest(largest(value, "image", 2), "depth")
+    others = []
+    for flip_depth, flip_image in ((1, 0), (0, 2), (1, 2)):
+        route = [
+            (d * images + i, (d ^ flip_depth) * images + (i ^ flip_image))
+            for d in range(depth)
+            for i in range(images)
+        ]
+        others.append(lax.ppermute(value, ("depth", "image"), route))
+    for other in others:
+        value = jnp.maximum(value, other)
+    return value
+
+
 def largest(value, axis, step=1):
     while step < lax.axis_size(axis):
         value = exchange_max(value, axis, step)
@@ -596,6 +626,13 @@
     if wrap:
         return [(i, (i + distance) % size) for i in range(size)]
     return [(i, i + distance) for i in range(size) if 0 <= i + distance < size]
+
+
+def paired(axis, start, wrap):
+    size = lax.axis_size(axis)
+    assert not wrap or size % 2 == 0, "odd ring"
+    couples = [(i, (i + 1) % size) for i in range(start, size, 2) if wrap or i + 1 < size]
+    return couples + [(j, i) for i, j in couples]
 
 
 def pictured(rho, heat, palette, index):
@@ -624,28 +661,28 @@
 def whole_step(density, velocity, pressure, palette, palette_index):
     depth = lax.axis_size("depth")
     _, rows = density.shape[:2]
-    state, zone, low, high, top = opening(density, velocity, pressure)
+    state, zone, one, two, top = opening(density, velocity, pressure)
 
     def both_ways(block):
         if depth == 2:
             return (lax.ppermute(block, "depth", along("depth", 1, True)),)
         return tuple(lax.ppermute(block, "depth", along("depth", d, True)) for d in (1, -1))
 
-    from_below = lax.ppermute(high, "group", along("group", 1, False))
-    from_above = lax.ppermute(low, "group", along("group", -1, False))
+    got_one = lax.ppermute(one, "group", paired("group", 0, False))
+    got_two = lax.ppermute(two, "group", paired("group", 1, False))
     zones = both_ways(zone)
-    wide, right, left, top = windows(state, from_below, from_above, top)
-    from_right = lax.ppermute(right, "image", along("image", -1, True))
-    from_left = lax.ppermute(left, "image", along("image", 1, True))
+    wide, first, second, top = windows(state, got_one, got_two, top)
+    got_first = lax.ppermute(first, "image", paired("image", 0, True))
+    got_second = lax.ppermute(second, "image", paired("image", 1, True))
     if lax.axis_size("group") == 4:
         top = exchange_max(top, "group", 2)
     else:
         top = largest(top, "group")
     top = exchange_max(top, "image", 1)
-    from_right, from_left, top = lax.optimization_barrier((from_right, from_left, top))
-    strips, pay = strips_of(wide, right, left, from_right, from_left)
+    got_first, got_second, top = lax.optimization_barrier((got_first, got_second, top))
+    strips, pay = strips_of(wide, first, second, got_first, got_second)
     pays = both_ways(pay)
-    top = largest(largest(top, "image", 2), "depth")
+    top = last_rounds(top)
     fluid_state, rho, heat = sections(wide, zones, pays, strips, top, rows)
     return (fluid_state, pictured(rho, heat, palette, palette_index))
 

time: 57.5 us -> 56.3 us (0.979)
  waiting for transfers between devices: 16.3 us -> 13.5 us
  starting transfers between devices: 18.3 us -> 19.8 us
  local copies, waits for them, and re-layouts: 0.03 us -> 0.96 us
  Pallas kernels: 21 us -> 20.1 us
    ppermute x4 -> x2, waiting for transfers between devices: 7.17 us -> 2.76 us  [exchange_max(): return jnp.maximum(value, lax.ppermute(value, axis, route))]
    ppermute x2, waiting for transfers between devices: 0.01 us -> 4.02 us  [both_ways(): return (lax.ppermute(block, 'depth', along('depth', 1, True)),)]
    ppermute x4 -> x7, starting transfers between devices: 5.32 us -> 7.47 us  [the longest x3 3.55 us: last_rounds(): others.append(lax.ppermute(value, ('depth', 'image'), route))]
    ppermute x4 -> x7, waiting for transfers between devices: 4.86 us -> 3.35 us  [the longest x1 2.03 us: whole_step(): got_one = lax.ppermute(one, 'group', paired('group', 0, False))]
    ppermute x3, starting transfers between devices: 3.65 us -> 2.69 us  [pictured(): sent.append(lax.ppermute(other, 'depth', along('depth', 1, True)))]
    pallas_call x1, Pallas kernels: 12.7 us -> 11.8 us  [sections(): pl.pallas_call(functools.partial(section_kernel, shared), out_shape=[pltp...]
    unnamed x4 -> x5, local copies, waits for them, and re-layouts: 0.01 us -> 0.95 us
    ppermute x3, waiting for transfers between devices: 4.28 us -> 3.42 us  [pictured(): sent.append(lax.ppermute(other, 'depth', along('depth', 1, True)))]
  transfers between devices with their start and end apart: 13 -> 14, of which waited for: 8 -> 8; matrix products, arithmetic and copies ran while one was open for 0% -> 2% of each run, Pallas kernels for 9% -> 9%
where the time goes in v5:
time: 56.3 us; the launch traced here: 56.1 us
  Pallas kernels  20.1 us (36%)
  starting transfers between devices  19.8 us (35%)
  waiting for transfers between devices  13.5 us (24%)
  local copies, waits for them, and re-layouts  0.96 us (2%)
  other arithmetic  0.89 us (2%)
  between operations  0.77 us (1%)
    pallas_call x1, Pallas kernels, sections(): pl.pallas_call(functools.partial(section_kernel, shared), out_shape=[pltp...  11.8 us
    ppermute x2, starting transfers between devices, exchange_max(): return jnp.maximum(value, lax.ppermute(value, axis, route))  6.05 us
    pallas_call x3, Pallas kernels, render(): pl.pallas_call(functools.partial(render_kernel, scale, begin, count, halv...  5.59 us
    ppermute x2, waiting for transfers between devices, both_ways(): return (lax.ppermute(block, 'depth', along('depth', 1, True)),)  4.02 us
    ppermute x2, starting transfers between devices, both_ways(): return (lax.ppermute(block, 'depth', along('depth', 1, True)),)  3.63 us
    ppermute x3, starting transfers between devices, last_rounds(): others.append(lax.ppermute(value, ('depth', 'image'), route))  3.55 us
    ppermute x3, waiting for transfers between devices, pictured(): sent.append(lax.ppermute(other, 'depth', along('depth', 1, True)))  3.42 us
    ppermute x2, waiting for transfers between devices, exchange_max(): return jnp.maximum(value, lax.ppermute(value, axis, route))  2.76 us
  transfers between devices with their start and end apart: 14, of which 8 were waited for; matrix products, arithmetic and copies ran while one was open for 2% of the time, Pallas kernels for 9%

profile of v5, /device:TPU:0, one launch (start us, length us, event | category | flops | bytes accessed | tf_op | source)
XLA Modules:
  0.0 56.1 jit_solution(10644915111039603508)
XLA Ops:
  0.6 1.5 %opening.1 = (f32[5,8,48,128]{3,2,1,0:T(8,128)S(1)}, f32[5,6,48,128]{3,2,1,0:T(8,128)S(1)}, f32[128,128]{1,0:T(8,128)S(1)}, f32[128,128]{1,0:T(8,128)S(1)}, f32[8,128]{1,0:T(8,128)S(1)}) custom-call(f32[8,48,128]{2,1,0:T(8,128)} %rho_hbm.1, f32[3,8,48,128]{3,2,1,0:T(8,128)} %vel_hbm.1, f32[8,48,128]{2,1,0:T(8,128)} %pre_hbm.1), custom_call_target="tpu_custom_call" | custom-call | tf_op jit(solution)/shard_map/opening/pallas_call | solution.py:102
  2.1 3.0 %collective-permute-start.2 = (f32[5,6,48,128]{3,2,1,0:T(8,128)S(1)}, f32[5,6,48,128]{3,2,1,0:T(8,128)S(1)}, u32[]{:S(2)}, u32[]{:S(2)}) collective-permute-start(f32[5,6,48,128]{3,2,1,0:T(8,128)S(1)} %get-tuple-element.30), channel_id=1, source_target_pairs={{0,4},{4,0},{1,5},{5,1},{2,6},{6,2},{3,7},{7,3},{8,12},{12,8},{9,1... | collective-permute-start | bytes 2211848 | tf_op jit(solution)/shard_map/ppermute | solution.py:668
  5.1 1.6 %collective-permute-start = (f32[128,128]{1,0:T(8,128)S(1)}, f32[128,128]{1,0:T(8,128)S(1)}, u32[]{:S(2)}, u32[]{:S(2)}) collective-permute-start(f32[128,128]{1,0:T(8,128)S(1)} %get-tuple-element.26), channel_id=1, source_target_pairs={{0,8},{16,24},{8,0},{24,16},{1,9},{17,25},{9,1},{25,17},{2,10},{18... | collective-permute-start | bytes 196616 | tf_op jit(solution)/shard_map/ppermute | solution.py:671
  6.7 0.7 %collective-permute-start.1 = (f32[128,128]{1,0:T(8,128)S(1)}, f32[128,128]{1,0:T(8,128)S(1)}, u32[]{:S(2)}, u32[]{:S(2)}) collective-permute-start(f32[128,128]{1,0:T(8,128)S(1)} %get-tuple-element.27), channel_id=1, source_target_pairs={{8,16},{16,8},{9,17},{17,9},{10,18},{18,10},{11,19},{19,11},{12,20... | collective-permute-start | bytes 196616 | tf_op jit(solution)/shard_map/ppermute | solution.py:672
  7.4 2.0 %collective-permute-done.one_ref = f32[128,128]{1,0:T(8,128)S(1)} collective-permute-done((f32[128,128]{1,0:T(8,128)S(1)}, f32[128,128]{1,0:T(8,128)S(1)}, u32[]{:S(2)}, u32[]{:S(2)}) %collective-permute-start) | collective-permute-done | bytes 65568 | tf_op jit(solution)/shard_map/ppermute | solution.py:671
  9.4 0.0 collective-permute-done.1.two_ref
  9.4 1.1 %windows.1 = (f32[5,8,56,128]{3,2,1,0:T(8,128)S(1)}, f32[5,56,128]{2,1,0:T(8,128)S(1)}, f32[5,56,128]{2,1,0:T(8,128)S(1)}, f32[8,128]{1,0:T(8,128)S(1)}) custom-call(f32[5,8,48,128]{3,2,1,0:T(8,128)S(1)} %get-tuple-element.25.state_ref, f32[128,128]{1,0:T(8,128)S(1)} %collective-permute-done.one_ref, f32[128,128]{1,0:T(8,128)S(1)} %collective-permute-done.1.two_ref, ...), custom_call_target="tpu_custom_call" | custom-call | tf_op jit(solution)/shard_map/windows/pallas_call | solution.py:173
  10.5 0.1 collective-permute-start.3
  10.6 1.6 %collective-permute-start.4 = (f32[5,56,128]{2,1,0:T(8,128)S(1)}, f32[5,56,128]{2,1,0:T(8,128)S(1)}, u32[]{:S(2)}, u32[]{:S(2)}) collective-permute-start(f32[5,56,128]{2,1,0:T(8,128)S(1)} %get-tuple-element.32.second_ref), channel_id=1, source_target_pairs={{1,2},{3,0},{2,1},{0,3},{5,6},{7,4},{6,5},{4,7},{9,10},{11,8},{10,... | collective-permute-start | bytes 430088 | tf_op jit(solution)/shard_map/ppermute | solution.py:676
  12.2 6.0 %collective-permute-start.5 = (f32[8,128]{1,0:T(8,128)S(1)}, f32[8,128]{1,0:T(8,128)S(1)}, u32[]{:S(2)}, u32[]{:S(2)}) collective-permute-start(f32[8,128]{1,0:T(8,128)S(1)} %get-tuple-element.33), channel_id=1, source_target_pairs={{0,16},{8,24},{16,0},{24,8},{1,17},{9,25},{17,1},{25,9},{2,18},{10... | collective-permute-start | bytes 12296 | tf_op jit(solution)/shard_map/ppermute | solution.py:588
  18.3 1.6 %collective-permute-done.5 = f32[8,128]{1,0:T(8,128)S(1)} collective-permute-done((f32[8,128]{1,0:T(8,128)S(1)}, f32[8,128]{1,0:T(8,128)S(1)}, u32[]{:S(2)}, u32[]{:S(2)}) %collective-permute-start.5) | collective-permute-done | bytes 4128 | tf_op jit(solution)/shard_map/ppermute | solution.py:588
  19.9 0.0 collective-permute-start.6
  19.9 1.2 %collective-permute-done.6 = f32[8,128]{1,0:T(8,128)S(1)} collective-permute-done((f32[8,128]{1,0:T(8,128)S(1)}, f32[8,128]{1,0:T(8,128)S(1)}, u32[]{:S(2)}, u32[]{:S(2)}) %collective-permute-start.6) | collective-permute-done | bytes 4128 | tf_op jit(solution)/shard_map/ppermute | solution.py:588
  21.0 0.0 collective-permute-done.3.got_first
  21.0 0.0 collective-permute-done.4.got_second
  21.0 0.5 collective-permute-start.10
  21.6 1.5 %collective-permute-start.8 = (f32[8,128]{1,0:T(8,128)S(1)}, f32[8,128]{1,0:T(8,128)S(1)}, u32[]{:S(2)}, u32[]{:S(2)}) collective-permute-start(f32[8,128]{1,0:T(8,128)S(1)} %max.16), channel_id=1, source_target_pairs={{0,4},{1,5},{2,6},{3,7},{4,0},{5,1},{6,2},{7,3},{8,12},{9,13},{10,... | collective-permute-start | bytes 12296 | tf_op jit(solution)/shard_map/ppermute | solution.py:602
  23.1 1.5 %collective-permute-start.9 = (f32[8,128]{1,0:T(8,128)S(1)}, f32[8,128]{1,0:T(8,128)S(1)}, u32[]{:S(2)}, u32[]{:S(2)}) collective-permute-start(f32[8,128]{1,0:T(8,128)S(1)} %max.16), channel_id=1, source_target_pairs={{0,2},{1,3},{2,0},{3,1},{4,6},{5,7},{6,4},{7,5},{8,10},{9,11},{10,... | collective-permute-start | bytes 12296 | tf_op jit(solution)/shard_map/ppermute | solution.py:602
  24.6 0.2 strips.1
  24.8 0.6 %collective-permute-start.7 = (f32[5,72,128]{2,1,0:T(8,128)S(1)}, f32[5,72,128]{2,1,0:T(8,128)S(1)}, u32[]{:S(2)}, u32[]{:S(2)}) collective-permute-start(f32[5,72,128]{2,1,0:T(8,128)S(1)} %get-tuple-element.36), channel_id=1, source_target_pairs={{0,4},{4,0},{1,5},{5,1},{2,6},{6,2},{3,7},{7,3},{8,12},{12,8},{9,1... | collective-permute-start | bytes 552968 | tf_op jit(solution)/shard_map/ppermute | solution.py:668
  25.4 0.2 collective-permute-done.10
  25.6 0.0 collective-permute-done.8
  25.6 1.1 %collective-permute-done.9 = f32[8,128]{1,0:T(8,128)S(1)} collective-permute-done((f32[8,128]{1,0:T(8,128)S(1)}, f32[8,128]{1,0:T(8,128)S(1)}, u32[]{:S(2)}, u32[]{:S(2)}) %collective-permute-start.9) | collective-permute-done | bytes 4128 | tf_op jit(solution)/shard_map/ppermute | solution.py:602
  26.7 4.0 %collective-permute-done.7.refs_2_ = f32[5,72,128]{2,1,0:T(8,128)S(1)} collective-permute-done((f32[5,72,128]{2,1,0:T(8,128)S(1)}, f32[5,72,128]{2,1,0:T(8,128)S(1)}, u32[]{:S(2)}, u32[]{:S(2)}) %collective-permute-start.7) | collective-permute-done | bytes 184352 | tf_op jit(solution)/shard_map/ppermute | solution.py:668
  30.7 0.0 collective-permute-done.2.refs_1_
  30.7 0.0 copy-start
  30.7 0.0 copy-start.1
  30.7 11.8 %sections.1 = (f32[5,8,48,128]{3,2,1,0:T(8,128)S(1)}, f32[8,48,128]{2,1,0:T(8,128)S(1)}, f32[8,48,128]{2,1,0:T(8,128)S(1)}) custom-call(f32[5,8,56,128]{3,2,1,0:T(8,128)S(1)} %get-tuple-element.29.wide_ref.refs_0_, f32[5,6,48,128]{3,2,1,0:T(8,128)S(1)} %collective-permute-done.2.refs_1_, f32[5,72,128]{2,1,0:T(8,128)S(1)} %collective-permute-done.7.refs_2_, ...), custom_call_target="tpu_custom_call" | custom-call | tf_op jit(solution)/shard_map/sections/pallas_call | solution.py:431
  42.5 0.0 copy-done
  42.5 0.0 copy-done.1
  42.5 1.9 %shard_map.68 = (f32[256,128]{1,0:T(8,128)S(1)}, f32[256,128]{1,0:T(8,128)S(1)}) custom-call(f32[8,48,128]{2,1,0:T(8,128)S(1)} %get-tuple-element.40.rho_ref, f32[8,48,128]{2,1,0:T(8,128)S(1)} %get-tuple-element.41.heat_ref, f32[4,256]{1,0:T(4,128)S(1)} %copy-done.1, s32[8,256]{1,0:T(8,128)S(1)} %copy-done), custom_call_target="tpu_custom_call" | custom-call | tf_op jit(solution)/shard_map/pallas_call | solution.py:571
  44.4 0.6 %collective-permute-start.11 = (f32[4,4,16,128]{3,2,1,0:T(8,128)S(1)}, f32[4,4,16,128]{3,2,1,0:T(8,128)S(1)}, u32[]{:S(2)}, u32[]{:S(2)}) collective-permute-start(f32[4,4,16,128]{3,2,1,0:T(8,128)S(1)} %bitcast.18), channel_id=1, source_target_pairs={{0,4},{4,0},{1,5},{5,1},{2,6},{6,2},{3,7},{7,3},{8,12},{12,8},{9,1... | collective-permute-start | bytes 393224 | tf_op jit(solution)/shard_map/ppermute | solution.py:652
  45.0 1.9 %shard_map.69 = (f32[256,128]{1,0:T(8,128)S(1)}, f32[256,128]{1,0:T(8,128)S(1)}) custom-call(f32[8,48,128]{2,1,0:T(8,128)S(1)} %get-tuple-element.40.rho_ref, f32[8,48,128]{2,1,0:T(8,128)S(1)} %get-tuple-element.41.heat_ref, f32[4,256]{1,0:T(4,128)S(1)} %copy-done.1, s32[8,256]{1,0:T(8,128)S(1)} %copy-done), custom_call_target="tpu_custom_call" | custom-call | tf_op jit(solution)/shard_map/pallas_call | solution.py:571
  46.9 1.9 %shard_map.70 = (f32[256,128]{1,0:T(8,128)S(1)}, f32[256,128]{1,0:T(8,128)S(1)}) custom-call(f32[8,48,128]{2,1,0:T(8,128)S(1)} %get-tuple-element.40.rho_ref, f32[8,48,128]{2,1,0:T(8,128)S(1)} %get-tuple-element.41.heat_ref, f32[4,256]{1,0:T(4,128)S(1)} %copy-done.1, s32[8,256]{1,0:T(8,128)S(1)} %copy-done), custom_call_target="tpu_custom_call" | custom-call | tf_op jit(solution)/shard_map/pallas_call | solution.py:571
  48.7 1.6 %collective-permute-start.12 = (f32[4,4,16,128]{3,2,1,0:T(8,128)S(1)}, f32[4,4,16,128]{3,2,1,0:T(8,128)S(1)}, u32[]{:S(2)}, u32[]{:S(2)}) collective-permute-start(f32[4,4,16,128]{3,2,1,0:T(8,128)S(1)} %bitcast.20), channel_id=1, source_target_pairs={{0,4},{4,0},{1,5},{5,1},{2,6},{6,2},{3,7},{7,3},{8,12},{12,8},{9,1... | collective-permute-start | bytes 393224 | tf_op jit(solution)/shard_map/ppermute | solution.py:652
  50.3 0.5 collective-permute-start.13
  50.8 0.9 %copy.7 = f32[5,8,48,128]{3,2,1,0:T(8,128)} copy(f32[5,8,48,128]{3,2,1,0:T(8,128)S(1)} %get-tuple-element.48) | data formatting | bytes 1966080
  51.8 0.0 collective-permute-done.11
  51.8 2.0 %collective-permute-done.12 = f32[4,4,16,128]{3,2,1,0:T(8,128)S(1)} collective-permute-done((f32[4,4,16,128]{3,2,1,0:T(8,128)S(1)}, f32[4,4,16,128]{3,2,1,0:T(8,128)S(1)}, u32[]{:S(2)}, u32[]{:S(2)}) %collective-permute-start.12) | collective-permute-done | bytes 131104 | tf_op jit(solution)/shard_map/ppermute | solution.py:652
  53.8 1.4 %collective-permute-done.13 = f32[4,4,16,128]{3,2,1,0:T(8,128)S(1)} collective-permute-done((f32[4,4,16,128]{3,2,1,0:T(8,128)S(1)}, f32[4,4,16,128]{3,2,1,0:T(8,128)S(1)}, u32[]{:S(2)}, u32[]{:S(2)}) %collective-permute-start.13) | collective-permute-done | bytes 131104 | tf_op jit(solution)/shard_map/ppermute | solution.py:652
  55.4 0.7 %pad_maximum_fusion = f32[4,3,48,128]{3,2,1,0:T(8,128)} fusion(f32[4,3,16,128]{3,2,1,0:T(8,128)S(1)} %fusion.1, f32[4,3,16,128]{3,2,1,0:T(8,128)S(1)} %fusion.3, f32[4,3,16,128]{3,2,1,0:T(8,128)S(1)} %fusion.5), kind=kLoop, calls=%fused_computation | loop fusion | flops 147456 | bytes 589824 | tf_op jit(solution)/shard_map/concatenate | solution.py:658
  (12 shorter events, 0.2 us)
Async XLA Ops:
  2.1 28.6 %collective-permute-start.2 = (f32[5,6,48,128]{3,2,1,0:T(8,128)S(1)}, f32[5,6,48,128]{3,2,1,0:T(8,128)S(1)}, u32[]{:S(2)}, u32[]{:S(2)}) collective-permute-start(f32[5,6,48,128]{3,2,1,0:T(8,128)S(1)} %get-tuple-element.30), channel_id=1, source_target_pairs={{0,4},{4,0},{1,5},{5,1},{2,6},{6,2},{3,7},{7,3},{8,12},{12,8},{9,1... | collective-permute-start | bytes 2211848 | tf_op jit(solution)/shard_map/ppermute | solution.py:668
  5.1 4.3 %collective-permute-start = (f32[128,128]{1,0:T(8,128)S(1)}, f32[128,128]{1,0:T(8,128)S(1)}, u32[]{:S(2)}, u32[]{:S(2)}) collective-permute-start(f32[128,128]{1,0:T(8,128)S(1)} %get-tuple-element.26), channel_id=1, source_target_pairs={{0,8},{16,24},{8,0},{24,16},{1,9},{17,25},{9,1},{25,17},{2,10},{18... | collective-permute-start | bytes 196616 | tf_op jit(solution)/shard_map/ppermute | solution.py:671
  6.7 2.7 %collective-permute-start.1 = (f32[128,128]{1,0:T(8,128)S(1)}, f32[128,128]{1,0:T(8,128)S(1)}, u32[]{:S(2)}, u32[]{:S(2)}) collective-permute-start(f32[128,128]{1,0:T(8,128)S(1)} %get-tuple-element.27), channel_id=1, source_target_pairs={{8,16},{16,8},{9,17},{17,9},{10,18},{18,10},{11,19},{19,11},{12,20... | collective-permute-start | bytes 196616 | tf_op jit(solution)/shard_map/ppermute | solution.py:672
  10.5 10.5 %collective-permute-start.3 = (f32[5,56,128]{2,1,0:T(8,128)S(1)}, f32[5,56,128]{2,1,0:T(8,128)S(1)}, u32[]{:S(2)}, u32[]{:S(2)}) collective-permute-start(f32[5,56,128]{2,1,0:T(8,128)S(1)} %get-tuple-element.31.first_ref), channel_id=1, source_target_pairs={{0,1},{2,3},{1,0},{3,2},{4,5},{6,7},{5,4},{7,6},{8,9},{10,11},{9,8... | collective-permute-start | bytes 430088 | tf_op jit(solution)/shard_map/ppermute | solution.py:675
  10.6 10.4 %collective-permute-start.4 = (f32[5,56,128]{2,1,0:T(8,128)S(1)}, f32[5,56,128]{2,1,0:T(8,128)S(1)}, u32[]{:S(2)}, u32[]{:S(2)}) collective-permute-start(f32[5,56,128]{2,1,0:T(8,128)S(1)} %get-tuple-element.32.second_ref), channel_id=1, source_target_pairs={{1,2},{3,0},{2,1},{0,3},{5,6},{7,4},{6,5},{4,7},{9,10},{11,8},{10,... | collective-permute-start | bytes 430088 | tf_op jit(solution)/shard_map/ppermute | solution.py:676
  12.2 7.6 %collective-permute-start.5 = (f32[8,128]{1,0:T(8,128)S(1)}, f32[8,128]{1,0:T(8,128)S(1)}, u32[]{:S(2)}, u32[]{:S(2)}) collective-permute-start(f32[8,128]{1,0:T(8,128)S(1)} %get-tuple-element.33), channel_id=1, source_target_pairs={{0,16},{8,24},{16,0},{24,8},{1,17},{9,25},{17,1},{25,9},{2,18},{10... | collective-permute-start | bytes 12296 | tf_op jit(solution)/shard_map/ppermute | solution.py:588
  19.9 1.2 %collective-permute-start.6 = (f32[8,128]{1,0:T(8,128)S(1)}, f32[8,128]{1,0:T(8,128)S(1)}, u32[]{:S(2)}, u32[]{:S(2)}) collective-permute-start(f32[8,128]{1,0:T(8,128)S(1)} %max.15), channel_id=1, source_target_pairs={{0,1},{1,0},{2,3},{3,2},{4,5},{5,4},{6,7},{7,6},{8,9},{9,8},{10,11... | collective-permute-start | bytes 12296 | tf_op jit(solution)/shard_map/ppermute | solution.py:588
  21.0 4.6 %collective-permute-start.10 = (f32[8,128]{1,0:T(8,128)S(1)}, f32[8,128]{1,0:T(8,128)S(1)}, u32[]{:S(2)}, u32[]{:S(2)}) collective-permute-start(f32[8,128]{1,0:T(8,128)S(1)} %max.16), channel_id=1, source_target_pairs={{0,6},{1,7},{2,4},{3,5},{4,2},{5,3},{6,0},{7,1},{8,14},{9,15},{10,... | collective-permute-start | bytes 12296 | tf_op jit(solution)/shard_map/ppermute | solution.py:602
  21.6 4.0 %collective-permute-start.8 = (f32[8,128]{1,0:T(8,128)S(1)}, f32[8,128]{1,0:T(8,128)S(1)}, u32[]{:S(2)}, u32[]{:S(2)}) collective-permute-start(f32[8,128]{1,0:T(8,128)S(1)} %max.16), channel_id=1, source_target_pairs={{0,4},{1,5},{2,6},{3,7},{4,0},{5,1},{6,2},{7,3},{8,12},{9,13},{10,... | collective-permute-start | bytes 12296 | tf_op jit(solution)/shard_map/ppermute | solution.py:602
  23.1 3.6 %collective-permute-start.9 = (f32[8,128]{1,0:T(8,128)S(1)}, f32[8,128]{1,0:T(8,128)S(1)}, u32[]{:S(2)}, u32[]{:S(2)}) collective-permute-start(f32[8,128]{1,0:T(8,128)S(1)} %max.16), channel_id=1, source_target_pairs={{0,2},{1,3},{2,0},{3,1},{4,6},{5,7},{6,4},{7,5},{8,10},{9,11},{10,... | collective-permute-start | bytes 12296 | tf_op jit(solution)/shard_map/ppermute | solution.py:602
  24.8 5.9 %collective-permute-start.7 = (f32[5,72,128]{2,1,0:T(8,128)S(1)}, f32[5,72,128]{2,1,0:T(8,128)S(1)}, u32[]{:S(2)}, u32[]{:S(2)}) collective-permute-start(f32[5,72,128]{2,1,0:T(8,128)S(1)} %get-tuple-element.36), channel_id=1, source_target_pairs={{0,4},{4,0},{1,5},{5,1},{2,6},{6,2},{3,7},{7,3},{8,12},{12,8},{9,1... | collective-permute-start | bytes 552968 | tf_op jit(solution)/shard_map/ppermute | solution.py:668
  30.7 11.8 %copy-start = (s32[8,256]{1,0:T(8,128)S(1)}, s32[8,256]{1,0:T(8,128)}, u32[]{:S(2)}) copy-start(s32[8,256]{1,0:T(8,128)} %index_ref.5) | copy-start | bytes 24580
  30.7 11.8 %copy-start.1 = (f32[4,256]{1,0:T(4,128)S(1)}, f32[4,256]{1,0:T(4,128)}, u32[]{:S(2)}) copy-start(f32[4,256]{1,0:T(4,128)} %palette_ref.5) | copy-start | bytes 12292
  44.4 7.4 %collective-permute-start.11 = (f32[4,4,16,128]{3,2,1,0:T(8,128)S(1)}, f32[4,4,16,128]{3,2,1,0:T(8,128)S(1)}, u32[]{:S(2)}, u32[]{:S(2)}) collective-permute-start(f32[4,4,16,128]{3,2,1,0:T(8,128)S(1)} %bitcast.18), channel_id=1, source_target_pairs={{0,4},{4,0},{1,5},{5,1},{2,6},{6,2},{3,7},{7,3},{8,12},{12,8},{9,1... | collective-permute-start | bytes 393224 | tf_op jit(solution)/shard_map/ppermute | solution.py:652
  48.7 5.1 %collective-permute-start.12 = (f32[4,4,16,128]{3,2,1,0:T(8,128)S(1)}, f32[4,4,16,128]{3,2,1,0:T(8,128)S(1)}, u32[]{:S(2)}, u32[]{:S(2)}) collective-permute-start(f32[4,4,16,128]{3,2,1,0:T(8,128)S(1)} %bitcast.20), channel_id=1, source_target_pairs={{0,4},{4,0},{1,5},{5,1},{2,6},{6,2},{3,7},{7,3},{8,12},{12,8},{9,1... | collective-permute-start | bytes 393224 | tf_op jit(solution)/shard_map/ppermute | solution.py:652
  50.3 5.0 %collective-permute-start.13 = (f32[4,4,16,128]{3,2,1,0:T(8,128)S(1)}, f32[4,4,16,128]{3,2,1,0:T(8,128)S(1)}, u32[]{:S(2)}, u32[]{:S(2)}) collective-permute-start(f32[4,4,16,128]{3,2,1,0:T(8,128)S(1)} %bitcast.19), channel_id=1, source_target_pairs={{0,4},{4,0},{1,5},{5,1},{2,6},{6,2},{3,7},{7,3},{8,12},{12,8},{9,1... | collective-permute-start | bytes 393224 | tf_op jit(solution)/shard_map/ppermute | solution.py:652

commit v6 on v5

--- a/solution.py
+++ b/solution.py
@@ -243,9 +243,9 @@
     return base * (1.0 / 3.0) + (2.0 / 3.0) * (here + half * change)
 
 
-def along_y(state, flux, uy, pressure, signal):
+def along_y(state, flux, pressure, signal):
     other = [ahead(v) for v in state]
-    flux_other = fluxes(other, ahead(uy), ahead(pressure), 2)
+    flux_other = fluxes(other, other[2] * (1.0 / other[0]), ahead(pressure), 2)
     g = face(flux, flux_other, state, other, signal, ahead(signal))
     return [behind(v) - v for v in g]
 
@@ -320,16 +320,17 @@
         state = [source[side, f, cut, :] for f in range(5)]
         ux, uy, uz, pressure, sound = primitives(*state)
         keep_x(fx, state, ux, pressure, sound, cut)
-        change = along_y(state, fluxes(state, uy, pressure, 2), uy, pressure, jnp.abs(uy) + sound)
+        change = along_y(state, fluxes(state, uy, pressure, 2), pressure, jnp.abs(uy) + sound)
         signal = jnp.abs(uz) + sound
         other = [ahead(v, WINDOW) for v in state]
+        _, _, normal, pressure_other, sound_other = primitives(*other)
         g = face(
             fluxes(state, uz, pressure, 3),
-            fluxes(other, ahead(uz, WINDOW), ahead(pressure, WINDOW), 3),
+            fluxes(other, normal, pressure_other, 3),
             state,
             other,
             signal,
-            ahead(signal, WINDOW),
+            jnp.abs(normal) + sound_other,
         )
         for f in range(5):
             acc[f, cut, :] = change[f] + (behind(g[f], WINDOW) - g[f])
@@ -373,7 +374,7 @@
                 if with_sides:
                     keep_x(fx, state, ux, pressure, sound, cut)
                     flux = fluxes(state, uy, pressure, 2)
-                    change = along_y(state, flux, uy, pressure, jnp.abs(uy) + sound)
+                    change = along_y(state, flux, pressure, jnp.abs(uy) + sound)
                     for f in range(5):
                         acc[f, cut, :] = change[f]
                     if t:
@@ -389,13 +390,19 @@
             for side in range(2):
                 strip_start(section, side, count + t)
 
-        def step(w, carry):
-            plane(w, True, True, True)
-            for side in range(2):
-                strip_start(section, side, jnp.minimum(w - first - 1, tiles - 1))
-            return carry
-
-        lax.fori_loop(first + 1, last, step, 0)
+        def step(with_strips):
+            def one_plane(w, carry):
+                plane(w, True, True, True)
+                for side in range(2 if with_strips else 0):
+                    strip_start(section, side, w - first - 1)
+                return carry
+
+            return one_plane
+
+        middle = first + 1 + min(count, tiles)
+        lax.fori_loop(first + 1, middle, step(True), 0)
+        if middle < last:
+            lax.fori_loop(middle, last, step(False), 0)
         plane(last, True, True, False)
 
     for section in range(3):
@@ -470,7 +477,7 @@
 
 
 LEVELS = 65535
-UNROLL = 4
+UNROLL = 8
 
 
 def render_kernel(

time: 56.3 us -> 54.8 us (0.973)
  Pallas kernels: 20.1 us -> 18.5 us
    pallas_call x1, Pallas kernels: 11.8 us -> 10.7 us  [sections(): pl.pallas_call(functools.partial(section_kernel, shared), out_shape=[pltp...]
where the time goes in v6:
time: 54.8 us; the launch traced here: 54.6 us
  starting transfers between devices  19.8 us (36%)
  Pallas kernels  18.5 us (34%)
  waiting for transfers between devices  13.6 us (25%)
  local copies, waits for them, and re-layouts  0.96 us (2%)
  other arithmetic  0.89 us (2%)
  between operations  0.77 us (1%)
    pallas_call x1, Pallas kernels, sections(): pl.pallas_call(functools.partial(section_kernel, shared), out_shape=[pltp...  10.7 us
    ppermute x2, starting transfers between devices, exchange_max(): return jnp.maximum(value, lax.ppermute(value, axis, route))  6.05 us
    pallas_call x3, Pallas kernels, render(): pl.pallas_call(functools.partial(render_kernel, scale, begin, count, halv...  5.1 us
    ppermute x2, waiting for transfers between devices, both_ways(): return (lax.ppermute(block, 'depth', along('depth', 1, True)),)  4.02 us
    ppermute x2, starting transfers between devices, both_ways(): return (lax.ppermute(block, 'depth', along('depth', 1, True)),)  3.63 us
    ppermute x3, starting transfers between devices, last_rounds(): others.append(lax.ppermute(value, ('depth', 'image'), route))  3.55 us
    ppermute x3, waiting for transfers between devices, pictured(): sent.append(lax.ppermute(other, 'depth', along('depth', 1, True)))  3.52 us
    ppermute x2, waiting for transfers between devices, exchange_max(): return jnp.maximum(value, lax.ppermute(value, axis, route))  2.76 us
  transfers between devices with their start and end apart: 14, of which 8 were waited for; matrix products, arithmetic and copies ran while one was open for 2% of the time, Pallas kernels for 9%

profile of v6, /device:TPU:0, one launch (start us, length us, event | category | flops | bytes accessed | tf_op | source)
XLA Modules:
  0.0 54.6 jit_solution(4578547957743376357)
XLA Ops:
  0.6 1.5 %opening.1 = (f32[5,8,48,128]{3,2,1,0:T(8,128)S(1)}, f32[5,6,48,128]{3,2,1,0:T(8,128)S(1)}, f32[128,128]{1,0:T(8,128)S(1)}, f32[128,128]{1,0:T(8,128)S(1)}, f32[8,128]{1,0:T(8,128)S(1)}) custom-call(f32[8,48,128]{2,1,0:T(8,128)} %rho_hbm.1, f32[3,8,48,128]{3,2,1,0:T(8,128)} %vel_hbm.1, f32[8,48,128]{2,1,0:T(8,128)} %pre_hbm.1), custom_call_target="tpu_custom_call" | custom-call | tf_op jit(solution)/shard_map/opening/pallas_call | solution.py:102
  2.1 3.0 %collective-permute-start.2 = (f32[5,6,48,128]{3,2,1,0:T(8,128)S(1)}, f32[5,6,48,128]{3,2,1,0:T(8,128)S(1)}, u32[]{:S(2)}, u32[]{:S(2)}) collective-permute-start(f32[5,6,48,128]{3,2,1,0:T(8,128)S(1)} %get-tuple-element.30), channel_id=1, source_target_pairs={{0,4},{4,0},{1,5},{5,1},{2,6},{6,2},{3,7},{7,3},{8,12},{12,8},{9,1... | collective-permute-start | bytes 2211848 | tf_op jit(solution)/shard_map/ppermute | solution.py:675
  5.1 1.6 %collective-permute-start = (f32[128,128]{1,0:T(8,128)S(1)}, f32[128,128]{1,0:T(8,128)S(1)}, u32[]{:S(2)}, u32[]{:S(2)}) collective-permute-start(f32[128,128]{1,0:T(8,128)S(1)} %get-tuple-element.26), channel_id=1, source_target_pairs={{0,8},{16,24},{8,0},{24,16},{1,9},{17,25},{9,1},{25,17},{2,10},{18... | collective-permute-start | bytes 196616 | tf_op jit(solution)/shard_map/ppermute | solution.py:678
  6.7 0.7 %collective-permute-start.1 = (f32[128,128]{1,0:T(8,128)S(1)}, f32[128,128]{1,0:T(8,128)S(1)}, u32[]{:S(2)}, u32[]{:S(2)}) collective-permute-start(f32[128,128]{1,0:T(8,128)S(1)} %get-tuple-element.27), channel_id=1, source_target_pairs={{8,16},{16,8},{9,17},{17,9},{10,18},{18,10},{11,19},{19,11},{12,20... | collective-permute-start | bytes 196616 | tf_op jit(solution)/shard_map/ppermute | solution.py:679
  7.4 2.0 %collective-permute-done.one_ref = f32[128,128]{1,0:T(8,128)S(1)} collective-permute-done((f32[128,128]{1,0:T(8,128)S(1)}, f32[128,128]{1,0:T(8,128)S(1)}, u32[]{:S(2)}, u32[]{:S(2)}) %collective-permute-start) | collective-permute-done | bytes 65568 | tf_op jit(solution)/shard_map/ppermute | solution.py:678
  9.4 0.0 collective-permute-done.1.two_ref
  9.4 1.1 %windows.1 = (f32[5,8,56,128]{3,2,1,0:T(8,128)S(1)}, f32[5,56,128]{2,1,0:T(8,128)S(1)}, f32[5,56,128]{2,1,0:T(8,128)S(1)}, f32[8,128]{1,0:T(8,128)S(1)}) custom-call(f32[5,8,48,128]{3,2,1,0:T(8,128)S(1)} %get-tuple-element.25.state_ref, f32[128,128]{1,0:T(8,128)S(1)} %collective-permute-done.one_ref, f32[128,128]{1,0:T(8,128)S(1)} %collective-permute-done.1.two_ref, ...), custom_call_target="tpu_custom_call" | custom-call | tf_op jit(solution)/shard_map/windows/pallas_call | solution.py:173
  10.5 0.1 collective-permute-start.3
  10.6 1.6 %collective-permute-start.4 = (f32[5,56,128]{2,1,0:T(8,128)S(1)}, f32[5,56,128]{2,1,0:T(8,128)S(1)}, u32[]{:S(2)}, u32[]{:S(2)}) collective-permute-start(f32[5,56,128]{2,1,0:T(8,128)S(1)} %get-tuple-element.32.second_ref), channel_id=1, source_target_pairs={{1,2},{3,0},{2,1},{0,3},{5,6},{7,4},{6,5},{4,7},{9,10},{11,8},{10,... | collective-permute-start | bytes 430088 | tf_op jit(solution)/shard_map/ppermute | solution.py:683
  12.2 6.0 %collective-permute-start.5 = (f32[8,128]{1,0:T(8,128)S(1)}, f32[8,128]{1,0:T(8,128)S(1)}, u32[]{:S(2)}, u32[]{:S(2)}) collective-permute-start(f32[8,128]{1,0:T(8,128)S(1)} %get-tuple-element.33), channel_id=1, source_target_pairs={{0,16},{8,24},{16,0},{24,8},{1,17},{9,25},{17,1},{25,9},{2,18},{10... | collective-permute-start | bytes 12296 | tf_op jit(solution)/shard_map/ppermute | solution.py:595
  18.3 1.6 %collective-permute-done.5 = f32[8,128]{1,0:T(8,128)S(1)} collective-permute-done((f32[8,128]{1,0:T(8,128)S(1)}, f32[8,128]{1,0:T(8,128)S(1)}, u32[]{:S(2)}, u32[]{:S(2)}) %collective-permute-start.5) | collective-permute-done | bytes 4128 | tf_op jit(solution)/shard_map/ppermute | solution.py:595
  19.9 0.0 collective-permute-start.6
  19.9 1.2 %collective-permute-done.6 = f32[8,128]{1,0:T(8,128)S(1)} collective-permute-done((f32[8,128]{1,0:T(8,128)S(1)}, f32[8,128]{1,0:T(8,128)S(1)}, u32[]{:S(2)}, u32[]{:S(2)}) %collective-permute-start.6) | collective-permute-done | bytes 4128 | tf_op jit(solution)/shard_map/ppermute | solution.py:595
  21.0 0.0 collective-permute-done.3.got_first
  21.0 0.0 collective-permute-done.4.got_second
  21.0 0.5 collective-permute-start.10
  21.6 1.5 %collective-permute-start.8 = (f32[8,128]{1,0:T(8,128)S(1)}, f32[8,128]{1,0:T(8,128)S(1)}, u32[]{:S(2)}, u32[]{:S(2)}) collective-permute-start(f32[8,128]{1,0:T(8,128)S(1)} %max.16), channel_id=1, source_target_pairs={{0,4},{1,5},{2,6},{3,7},{4,0},{5,1},{6,2},{7,3},{8,12},{9,13},{10,... | collective-permute-start | bytes 12296 | tf_op jit(solution)/shard_map/ppermute | solution.py:609
  23.1 1.5 %collective-permute-start.9 = (f32[8,128]{1,0:T(8,128)S(1)}, f32[8,128]{1,0:T(8,128)S(1)}, u32[]{:S(2)}, u32[]{:S(2)}) collective-permute-start(f32[8,128]{1,0:T(8,128)S(1)} %max.16), channel_id=1, source_target_pairs={{0,2},{1,3},{2,0},{3,1},{4,6},{5,7},{6,4},{7,5},{8,10},{9,11},{10,... | collective-permute-start | bytes 12296 | tf_op jit(solution)/shard_map/ppermute | solution.py:609
  24.6 0.2 strips.1
  24.8 0.6 %collective-permute-start.7 = (f32[5,72,128]{2,1,0:T(8,128)S(1)}, f32[5,72,128]{2,1,0:T(8,128)S(1)}, u32[]{:S(2)}, u32[]{:S(2)}) collective-permute-start(f32[5,72,128]{2,1,0:T(8,128)S(1)} %get-tuple-element.36), channel_id=1, source_target_pairs={{0,4},{4,0},{1,5},{5,1},{2,6},{6,2},{3,7},{7,3},{8,12},{12,8},{9,1... | collective-permute-start | bytes 552968 | tf_op jit(solution)/shard_map/ppermute | solution.py:675
  25.4 0.2 collective-permute-done.10
  25.6 0.0 collective-permute-done.8
  25.6 1.1 %collective-permute-done.9 = f32[8,128]{1,0:T(8,128)S(1)} collective-permute-done((f32[8,128]{1,0:T(8,128)S(1)}, f32[8,128]{1,0:T(8,128)S(1)}, u32[]{:S(2)}, u32[]{:S(2)}) %collective-permute-start.9) | collective-permute-done | bytes 4128 | tf_op jit(solution)/shard_map/ppermute | solution.py:609
  26.7 4.0 %collective-permute-done.7.refs_2_ = f32[5,72,128]{2,1,0:T(8,128)S(1)} collective-permute-done((f32[5,72,128]{2,1,0:T(8,128)S(1)}, f32[5,72,128]{2,1,0:T(8,128)S(1)}, u32[]{:S(2)}, u32[]{:S(2)}) %collective-permute-start.7) | collective-permute-done | bytes 184352 | tf_op jit(solution)/shard_map/ppermute | solution.py:675
  30.7 0.0 collective-permute-done.2.refs_1_
  30.7 0.0 copy-start
  30.7 0.0 copy-start.1
  30.7 10.7 %sections.1 = (f32[5,8,48,128]{3,2,1,0:T(8,128)S(1)}, f32[8,48,128]{2,1,0:T(8,128)S(1)}, f32[8,48,128]{2,1,0:T(8,128)S(1)}) custom-call(f32[5,8,56,128]{3,2,1,0:T(8,128)S(1)} %get-tuple-element.29.wide_ref.refs_0_, f32[5,6,48,128]{3,2,1,0:T(8,128)S(1)} %collective-permute-done.2.refs_1_, f32[5,72,128]{2,1,0:T(8,128)S(1)} %collective-permute-done.7.refs_2_, ...), custom_call_target="tpu_custom_call" | custom-call | tf_op jit(solution)/shard_map/sections/pallas_call | solution.py:438
  41.4 0.0 copy-done
  41.4 0.0 copy-done.1
  41.4 1.7 %shard_map.68 = (f32[256,128]{1,0:T(8,128)S(1)}, f32[256,128]{1,0:T(8,128)S(1)}) custom-call(f32[8,48,128]{2,1,0:T(8,128)S(1)} %get-tuple-element.40.rho_ref, f32[8,48,128]{2,1,0:T(8,128)S(1)} %get-tuple-element.41.heat_ref, f32[4,256]{1,0:T(4,128)S(1)} %copy-done.1, s32[8,256]{1,0:T(8,128)S(1)} %copy-done), custom_call_target="tpu_custom_call" | custom-call | tf_op jit(solution)/shard_map/pallas_call | solution.py:578
  43.1 0.6 %collective-permute-start.11 = (f32[4,4,16,128]{3,2,1,0:T(8,128)S(1)}, f32[4,4,16,128]{3,2,1,0:T(8,128)S(1)}, u32[]{:S(2)}, u32[]{:S(2)}) collective-permute-start(f32[4,4,16,128]{3,2,1,0:T(8,128)S(1)} %bitcast.18), channel_id=1, source_target_pairs={{0,4},{4,0},{1,5},{5,1},{2,6},{6,2},{3,7},{7,3},{8,12},{12,8},{9,1... | collective-permute-start | bytes 393224 | tf_op jit(solution)/shard_map/ppermute | solution.py:659
  43.7 1.7 %shard_map.69 = (f32[256,128]{1,0:T(8,128)S(1)}, f32[256,128]{1,0:T(8,128)S(1)}) custom-call(f32[8,48,128]{2,1,0:T(8,128)S(1)} %get-tuple-element.40.rho_ref, f32[8,48,128]{2,1,0:T(8,128)S(1)} %get-tuple-element.41.heat_ref, f32[4,256]{1,0:T(4,128)S(1)} %copy-done.1, s32[8,256]{1,0:T(8,128)S(1)} %copy-done), custom_call_target="tpu_custom_call" | custom-call | tf_op jit(solution)/shard_map/pallas_call | solution.py:578
  45.4 1.7 %shard_map.70 = (f32[256,128]{1,0:T(8,128)S(1)}, f32[256,128]{1,0:T(8,128)S(1)}) custom-call(f32[8,48,128]{2,1,0:T(8,128)S(1)} %get-tuple-element.40.rho_ref, f32[8,48,128]{2,1,0:T(8,128)S(1)} %get-tuple-element.41.heat_ref, f32[4,256]{1,0:T(4,128)S(1)} %copy-done.1, s32[8,256]{1,0:T(8,128)S(1)} %copy-done), custom_call_target="tpu_custom_call" | custom-call | tf_op jit(solution)/shard_map/pallas_call | solution.py:578
  47.1 1.6 %collective-permute-start.12 = (f32[4,4,16,128]{3,2,1,0:T(8,128)S(1)}, f32[4,4,16,128]{3,2,1,0:T(8,128)S(1)}, u32[]{:S(2)}, u32[]{:S(2)}) collective-permute-start(f32[4,4,16,128]{3,2,1,0:T(8,128)S(1)} %bitcast.20), channel_id=1, source_target_pairs={{0,4},{4,0},{1,5},{5,1},{2,6},{6,2},{3,7},{7,3},{8,12},{12,8},{9,1... | collective-permute-start | bytes 393224 | tf_op jit(solution)/shard_map/ppermute | solution.py:659
  48.7 0.5 collective-permute-start.13
  49.2 0.9 %copy.7 = f32[5,8,48,128]{3,2,1,0:T(8,128)} copy(f32[5,8,48,128]{3,2,1,0:T(8,128)S(1)} %get-tuple-element.48) | data formatting | bytes 1966080
  50.1 0.0 collective-permute-done.11
  50.2 2.2 %collective-permute-done.12 = f32[4,4,16,128]{3,2,1,0:T(8,128)S(1)} collective-permute-done((f32[4,4,16,128]{3,2,1,0:T(8,128)S(1)}, f32[4,4,16,128]{3,2,1,0:T(8,128)S(1)}, u32[]{:S(2)}, u32[]{:S(2)}) %collective-permute-start.12) | collective-permute-done | bytes 131104 | tf_op jit(solution)/shard_map/ppermute | solution.py:659
  52.4 1.4 %collective-permute-done.13 = f32[4,4,16,128]{3,2,1,0:T(8,128)S(1)} collective-permute-done((f32[4,4,16,128]{3,2,1,0:T(8,128)S(1)}, f32[4,4,16,128]{3,2,1,0:T(8,128)S(1)}, u32[]{:S(2)}, u32[]{:S(2)}) %collective-permute-start.13) | collective-permute-done | bytes 131104 | tf_op jit(solution)/shard_map/ppermute | solution.py:659
  53.9 0.7 %pad_maximum_fusion = f32[4,3,48,128]{3,2,1,0:T(8,128)} fusion(f32[4,3,16,128]{3,2,1,0:T(8,128)S(1)} %fusion.1, f32[4,3,16,128]{3,2,1,0:T(8,128)S(1)} %fusion.3, f32[4,3,16,128]{3,2,1,0:T(8,128)S(1)} %fusion.5), kind=kLoop, calls=%fused_computation | loop fusion | flops 147456 | bytes 589824 | tf_op jit(solution)/shard_map/concatenate | solution.py:665
  (12 shorter events, 0.2 us)
Async XLA Ops:
  2.1 28.6 %collective-permute-start.2 = (f32[5,6,48,128]{3,2,1,0:T(8,128)S(1)}, f32[5,6,48,128]{3,2,1,0:T(8,128)S(1)}, u32[]{:S(2)}, u32[]{:S(2)}) collective-permute-start(f32[5,6,48,128]{3,2,1,0:T(8,128)S(1)} %get-tuple-element.30), channel_id=1, source_target_pairs={{0,4},{4,0},{1,5},{5,1},{2,6},{6,2},{3,7},{7,3},{8,12},{12,8},{9,1... | collective-permute-start | bytes 2211848 | tf_op jit(solution)/shard_map/ppermute | solution.py:675
  5.1 4.3 %collective-permute-start = (f32[128,128]{1,0:T(8,128)S(1)}, f32[128,128]{1,0:T(8,128)S(1)}, u32[]{:S(2)}, u32[]{:S(2)}) collective-permute-start(f32[128,128]{1,0:T(8,128)S(1)} %get-tuple-element.26), channel_id=1, source_target_pairs={{0,8},{16,24},{8,0},{24,16},{1,9},{17,25},{9,1},{25,17},{2,10},{18... | collective-permute-start | bytes 196616 | tf_op jit(solution)/shard_map/ppermute | solution.py:678
  6.7 2.7 %collective-permute-start.1 = (f32[128,128]{1,0:T(8,128)S(1)}, f32[128,128]{1,0:T(8,128)S(1)}, u32[]{:S(2)}, u32[]{:S(2)}) collective-permute-start(f32[128,128]{1,0:T(8,128)S(1)} %get-tuple-element.27), channel_id=1, source_target_pairs={{8,16},{16,8},{9,17},{17,9},{10,18},{18,10},{11,19},{19,11},{12,20... | collective-permute-start | bytes 196616 | tf_op jit(solution)/shard_map/ppermute | solution.py:679
  10.5 10.5 %collective-permute-start.3 = (f32[5,56,128]{2,1,0:T(8,128)S(1)}, f32[5,56,128]{2,1,0:T(8,128)S(1)}, u32[]{:S(2)}, u32[]{:S(2)}) collective-permute-start(f32[5,56,128]{2,1,0:T(8,128)S(1)} %get-tuple-element.31.first_ref), channel_id=1, source_target_pairs={{0,1},{2,3},{1,0},{3,2},{4,5},{6,7},{5,4},{7,6},{8,9},{10,11},{9,8... | collective-permute-start | bytes 430088 | tf_op jit(solution)/shard_map/ppermute | solution.py:682
  10.6 10.4 %collective-permute-start.4 = (f32[5,56,128]{2,1,0:T(8,128)S(1)}, f32[5,56,128]{2,1,0:T(8,128)S(1)}, u32[]{:S(2)}, u32[]{:S(2)}) collective-permute-start(f32[5,56,128]{2,1,0:T(8,128)S(1)} %get-tuple-element.32.second_ref), channel_id=1, source_target_pairs={{1,2},{3,0},{2,1},{0,3},{5,6},{7,4},{6,5},{4,7},{9,10},{11,8},{10,... | collective-permute-start | bytes 430088 | tf_op jit(solution)/shard_map/ppermute | solution.py:683
  12.2 7.6 %collective-permute-start.5 = (f32[8,128]{1,0:T(8,128)S(1)}, f32[8,128]{1,0:T(8,128)S(1)}, u32[]{:S(2)}, u32[]{:S(2)}) collective-permute-start(f32[8,128]{1,0:T(8,128)S(1)} %get-tuple-element.33), channel_id=1, source_target_pairs={{0,16},{8,24},{16,0},{24,8},{1,17},{9,25},{17,1},{25,9},{2,18},{10... | collective-permute-start | bytes 12296 | tf_op jit(solution)/shard_map/ppermute | solution.py:595
  19.9 1.2 %collective-permute-start.6 = (f32[8,128]{1,0:T(8,128)S(1)}, f32[8,128]{1,0:T(8,128)S(1)}, u32[]{:S(2)}, u32[]{:S(2)}) collective-permute-start(f32[8,128]{1,0:T(8,128)S(1)} %max.15), channel_id=1, source_target_pairs={{0,1},{1,0},{2,3},{3,2},{4,5},{5,4},{6,7},{7,6},{8,9},{9,8},{10,11... | collective-permute-start | bytes 12296 | tf_op jit(solution)/shard_map/ppermute | solution.py:595
  21.0 4.6 %collective-permute-start.10 = (f32[8,128]{1,0:T(8,128)S(1)}, f32[8,128]{1,0:T(8,128)S(1)}, u32[]{:S(2)}, u32[]{:S(2)}) collective-permute-start(f32[8,128]{1,0:T(8,128)S(1)} %max.16), channel_id=1, source_target_pairs={{0,6},{1,7},{2,4},{3,5},{4,2},{5,3},{6,0},{7,1},{8,14},{9,15},{10,... | collective-permute-start | bytes 12296 | tf_op jit(solution)/shard_map/ppermute | solution.py:609
  21.6 4.0 %collective-permute-start.8 = (f32[8,128]{1,0:T(8,128)S(1)}, f32[8,128]{1,0:T(8,128)S(1)}, u32[]{:S(2)}, u32[]{:S(2)}) collective-permute-start(f32[8,128]{1,0:T(8,128)S(1)} %max.16), channel_id=1, source_target_pairs={{0,4},{1,5},{2,6},{3,7},{4,0},{5,1},{6,2},{7,3},{8,12},{9,13},{10,... | collective-permute-start | bytes 12296 | tf_op jit(solution)/shard_map/ppermute | solution.py:609
  23.1 3.6 %collective-permute-start.9 = (f32[8,128]{1,0:T(8,128)S(1)}, f32[8,128]{1,0:T(8,128)S(1)}, u32[]{:S(2)}, u32[]{:S(2)}) collective-permute-start(f32[8,128]{1,0:T(8,128)S(1)} %max.16), channel_id=1, source_target_pairs={{0,2},{1,3},{2,0},{3,1},{4,6},{5,7},{6,4},{7,5},{8,10},{9,11},{10,... | collective-permute-start | bytes 12296 | tf_op jit(solution)/shard_map/ppermute | solution.py:609
  24.8 5.9 %collective-permute-start.7 = (f32[5,72,128]{2,1,0:T(8,128)S(1)}, f32[5,72,128]{2,1,0:T(8,128)S(1)}, u32[]{:S(2)}, u32[]{:S(2)}) collective-permute-start(f32[5,72,128]{2,1,0:T(8,128)S(1)} %get-tuple-element.36), channel_id=1, source_target_pairs={{0,4},{4,0},{1,5},{5,1},{2,6},{6,2},{3,7},{7,3},{8,12},{12,8},{9,1... | collective-permute-start | bytes 552968 | tf_op jit(solution)/shard_map/ppermute | solution.py:675
  30.7 10.7 %copy-start = (s32[8,256]{1,0:T(8,128)S(1)}, s32[8,256]{1,0:T(8,128)}, u32[]{:S(2)}) copy-start(s32[8,256]{1,0:T(8,128)} %index_ref.5) | copy-start | bytes 24580
  30.7 10.7 %copy-start.1 = (f32[4,256]{1,0:T(4,128)S(1)}, f32[4,256]{1,0:T(4,128)}, u32[]{:S(2)}) copy-start(f32[4,256]{1,0:T(4,128)} %palette_ref.5) | copy-start | bytes 12292
  43.1 7.1 %collective-permute-start.11 = (f32[4,4,16,128]{3,2,1,0:T(8,128)S(1)}, f32[4,4,16,128]{3,2,1,0:T(8,128)S(1)}, u32[]{:S(2)}, u32[]{:S(2)}) collective-permute-start(f32[4,4,16,128]{3,2,1,0:T(8,128)S(1)} %bitcast.18), channel_id=1, source_target_pairs={{0,4},{4,0},{1,5},{5,1},{2,6},{6,2},{3,7},{7,3},{8,12},{12,8},{9,1... | collective-permute-start | bytes 393224 | tf_op jit(solution)/shard_map/ppermute | solution.py:659
  47.1 5.2 %collective-permute-start.12 = (f32[4,4,16,128]{3,2,1,0:T(8,128)S(1)}, f32[4,4,16,128]{3,2,1,0:T(8,128)S(1)}, u32[]{:S(2)}, u32[]{:S(2)}) collective-permute-start(f32[4,4,16,128]{3,2,1,0:T(8,128)S(1)} %bitcast.20), channel_id=1, source_target_pairs={{0,4},{4,0},{1,5},{5,1},{2,6},{6,2},{3,7},{7,3},{8,12},{12,8},{9,1... | collective-permute-start | bytes 393224 | tf_op jit(solution)/shard_map/ppermute | solution.py:659
  48.7 5.1 %collective-permute-start.13 = (f32[4,4,16,128]{3,2,1,0:T(8,128)S(1)}, f32[4,4,16,128]{3,2,1,0:T(8,128)S(1)}, u32[]{:S(2)}, u32[]{:S(2)}) collective-permute-start(f32[4,4,16,128]{3,2,1,0:T(8,128)S(1)} %bitcast.19), channel_id=1, source_target_pairs={{0,4},{4,0},{1,5},{5,1},{2,6},{6,2},{3,7},{7,3},{8,12},{12,8},{9,1... | collective-permute-start | bytes 393224 | tf_op jit(solution)/shard_map/ppermute | solution.py:659

commit v7 on v6

--- a/solution.py
+++ b/solution.py
@@ -243,8 +243,14 @@
     return base * (1.0 / 3.0) + (2.0 / 3.0) * (here + half * change)
 
 
-def along_y(state, flux, pressure, signal):
+def along_y(state, flux, pressure, signal, anew=False):
     other = [ahead(v) for v in state]
+    if anew:
+        _, normal, _, pressure, sound = primitives(*other)
+        g = face(
+            flux, fluxes(other, normal, pressure, 2), state, other, signal, jnp.abs(normal) + sound
+        )
+        return [behind(v) - v for v in g]
     flux_other = fluxes(other, other[2] * (1.0 / other[0]), ahead(pressure), 2)
     g = face(flux, flux_other, state, other, signal, ahead(signal))
     return [behind(v) - v for v in g]
@@ -320,7 +326,8 @@
         state = [source[side, f, cut, :] for f in range(5)]
         ux, uy, uz, pressure, sound = primitives(*state)
         keep_x(fx, state, ux, pressure, sound, cut)
-        change = along_y(state, fluxes(state, uy, pressure, 2), pressure, jnp.abs(uy) + sound)
+        flux_y, signal_y = fluxes(state, uy, pressure, 2), jnp.abs(uy) + sound
+        change = along_y(state, flux_y, pressure, signal_y, True)
         signal = jnp.abs(uz) + sound
         other = [ahead(v, WINDOW) for v in state]
         _, _, normal, pressure_other, sound_other = primitives(*other)

time: 54.8 us -> 54.8 us (level)
  no operation moved by 1% of the time
where the time goes in v7:
time: 54.8 us; the launch traced here: 54.6 us
  starting transfers between devices  19.8 us (36%)
  Pallas kernels  18.5 us (34%)
  waiting for transfers between devices  13.6 us (25%)
  local copies, waits for them, and re-layouts  0.96 us (2%)
  other arithmetic  0.89 us (2%)
  between operations  0.77 us (1%)
    pallas_call x1, Pallas kernels, sections(): pl.pallas_call(functools.partial(section_kernel, shared), out_shape=[pltp...  10.7 us
    ppermute x2, starting transfers between devices, exchange_max(): return jnp.maximum(value, lax.ppermute(value, axis, route))  6.05 us
    pallas_call x3, Pallas kernels, render(): pl.pallas_call(functools.partial(render_kernel, scale, begin, count, halv...  5.1 us
    ppermute x2, waiting for transfers between devices, both_ways(): return (lax.ppermute(block, 'depth', along('depth', 1, True)),)  4.02 us
    ppermute x2, starting transfers between devices, both_ways(): return (lax.ppermute(block, 'depth', along('depth', 1, True)),)  3.63 us
    ppermute x3, starting transfers between devices, last_rounds(): others.append(lax.ppermute(value, ('depth', 'image'), route))  3.55 us
    ppermute x3, waiting for transfers between devices, pictured(): sent.append(lax.ppermute(other, 'depth', along('depth', 1, True)))  3.52 us
    ppermute x2, waiting for transfers between devices, exchange_max(): return jnp.maximum(value, lax.ppermute(value, axis, route))  2.76 us
  transfers between devices with their start and end apart: 14, of which 8 were waited for; matrix products, arithmetic and copies ran while one was open for 2% of the time, Pallas kernels for 9%

profile of v7, /device:TPU:0, one launch (start us, length us, event | category | flops | bytes accessed | tf_op | source)
XLA Modules:
  0.0 54.6 jit_solution(6132900071046524875)
XLA Ops:
  0.6 1.5 %opening.1 = (f32[5,8,48,128]{3,2,1,0:T(8,128)S(1)}, f32[5,6,48,128]{3,2,1,0:T(8,128)S(1)}, f32[128,128]{1,0:T(8,128)S(1)}, f32[128,128]{1,0:T(8,128)S(1)}, f32[8,128]{1,0:T(8,128)S(1)}) custom-call(f32[8,48,128]{2,1,0:T(8,128)} %rho_hbm.1, f32[3,8,48,128]{3,2,1,0:T(8,128)} %vel_hbm.1, f32[8,48,128]{2,1,0:T(8,128)} %pre_hbm.1), custom_call_target="tpu_custom_call" | custom-call | tf_op jit(solution)/shard_map/opening/pallas_call | solution.py:102
  2.1 3.0 %collective-permute-start.2 = (f32[5,6,48,128]{3,2,1,0:T(8,128)S(1)}, f32[5,6,48,128]{3,2,1,0:T(8,128)S(1)}, u32[]{:S(2)}, u32[]{:S(2)}) collective-permute-start(f32[5,6,48,128]{3,2,1,0:T(8,128)S(1)} %get-tuple-element.30), channel_id=1, source_target_pairs={{0,4},{4,0},{1,5},{5,1},{2,6},{6,2},{3,7},{7,3},{8,12},{12,8},{9,1... | collective-permute-start | bytes 2211848 | tf_op jit(solution)/shard_map/ppermute | solution.py:682
  5.1 1.6 %collective-permute-start = (f32[128,128]{1,0:T(8,128)S(1)}, f32[128,128]{1,0:T(8,128)S(1)}, u32[]{:S(2)}, u32[]{:S(2)}) collective-permute-start(f32[128,128]{1,0:T(8,128)S(1)} %get-tuple-element.26), channel_id=1, source_target_pairs={{0,8},{16,24},{8,0},{24,16},{1,9},{17,25},{9,1},{25,17},{2,10},{18... | collective-permute-start | bytes 196616 | tf_op jit(solution)/shard_map/ppermute | solution.py:685
  6.7 0.7 %collective-permute-start.1 = (f32[128,128]{1,0:T(8,128)S(1)}, f32[128,128]{1,0:T(8,128)S(1)}, u32[]{:S(2)}, u32[]{:S(2)}) collective-permute-start(f32[128,128]{1,0:T(8,128)S(1)} %get-tuple-element.27), channel_id=1, source_target_pairs={{8,16},{16,8},{9,17},{17,9},{10,18},{18,10},{11,19},{19,11},{12,20... | collective-permute-start | bytes 196616 | tf_op jit(solution)/shard_map/ppermute | solution.py:686
  7.4 2.0 %collective-permute-done.one_ref = f32[128,128]{1,0:T(8,128)S(1)} collective-permute-done((f32[128,128]{1,0:T(8,128)S(1)}, f32[128,128]{1,0:T(8,128)S(1)}, u32[]{:S(2)}, u32[]{:S(2)}) %collective-permute-start) | collective-permute-done | bytes 65568 | tf_op jit(solution)/shard_map/ppermute | solution.py:685
  9.4 0.0 collective-permute-done.1.two_ref
  9.4 1.1 %windows.1 = (f32[5,8,56,128]{3,2,1,0:T(8,128)S(1)}, f32[5,56,128]{2,1,0:T(8,128)S(1)}, f32[5,56,128]{2,1,0:T(8,128)S(1)}, f32[8,128]{1,0:T(8,128)S(1)}) custom-call(f32[5,8,48,128]{3,2,1,0:T(8,128)S(1)} %get-tuple-element.25.state_ref, f32[128,128]{1,0:T(8,128)S(1)} %collective-permute-done.one_ref, f32[128,128]{1,0:T(8,128)S(1)} %collective-permute-done.1.two_ref, ...), custom_call_target="tpu_custom_call" | custom-call | tf_op jit(solution)/shard_map/windows/pallas_call | solution.py:173
  10.5 0.1 collective-permute-start.3
  10.6 1.6 %collective-permute-start.4 = (f32[5,56,128]{2,1,0:T(8,128)S(1)}, f32[5,56,128]{2,1,0:T(8,128)S(1)}, u32[]{:S(2)}, u32[]{:S(2)}) collective-permute-start(f32[5,56,128]{2,1,0:T(8,128)S(1)} %get-tuple-element.32.second_ref), channel_id=1, source_target_pairs={{1,2},{3,0},{2,1},{0,3},{5,6},{7,4},{6,5},{4,7},{9,10},{11,8},{10,... | collective-permute-start | bytes 430088 | tf_op jit(solution)/shard_map/ppermute | solution.py:690
  12.2 6.0 %collective-permute-start.5 = (f32[8,128]{1,0:T(8,128)S(1)}, f32[8,128]{1,0:T(8,128)S(1)}, u32[]{:S(2)}, u32[]{:S(2)}) collective-permute-start(f32[8,128]{1,0:T(8,128)S(1)} %get-tuple-element.33), channel_id=1, source_target_pairs={{0,16},{8,24},{16,0},{24,8},{1,17},{9,25},{17,1},{25,9},{2,18},{10... | collective-permute-start | bytes 12296 | tf_op jit(solution)/shard_map/ppermute | solution.py:602
  18.3 1.6 %collective-permute-done.5 = f32[8,128]{1,0:T(8,128)S(1)} collective-permute-done((f32[8,128]{1,0:T(8,128)S(1)}, f32[8,128]{1,0:T(8,128)S(1)}, u32[]{:S(2)}, u32[]{:S(2)}) %collective-permute-start.5) | collective-permute-done | bytes 4128 | tf_op jit(solution)/shard_map/ppermute | solution.py:602
  19.9 0.0 collective-permute-start.6
  19.9 1.2 %collective-permute-done.6 = f32[8,128]{1,0:T(8,128)S(1)} collective-permute-done((f32[8,128]{1,0:T(8,128)S(1)}, f32[8,128]{1,0:T(8,128)S(1)}, u32[]{:S(2)}, u32[]{:S(2)}) %collective-permute-start.6) | collective-permute-done | bytes 4128 | tf_op jit(solution)/shard_map/ppermute | solution.py:602
  21.0 0.0 collective-permute-done.3.got_first
  21.0 0.0 collective-permute-done.4.got_second
  21.0 0.5 collective-permute-start.10
  21.6 1.5 %collective-permute-start.8 = (f32[8,128]{1,0:T(8,128)S(1)}, f32[8,128]{1,0:T(8,128)S(1)}, u32[]{:S(2)}, u32[]{:S(2)}) collective-permute-start(f32[8,128]{1,0:T(8,128)S(1)} %max.16), channel_id=1, source_target_pairs={{0,4},{1,5},{2,6},{3,7},{4,0},{5,1},{6,2},{7,3},{8,12},{9,13},{10,... | collective-permute-start | bytes 12296 | tf_op jit(solution)/shard_map/ppermute | solution.py:616
  23.1 1.5 %collective-permute-start.9 = (f32[8,128]{1,0:T(8,128)S(1)}, f32[8,128]{1,0:T(8,128)S(1)}, u32[]{:S(2)}, u32[]{:S(2)}) collective-permute-start(f32[8,128]{1,0:T(8,128)S(1)} %max.16), channel_id=1, source_target_pairs={{0,2},{1,3},{2,0},{3,1},{4,6},{5,7},{6,4},{7,5},{8,10},{9,11},{10,... | collective-permute-start | bytes 12296 | tf_op jit(solution)/shard_map/ppermute | solution.py:616
  24.6 0.2 strips.1
  24.8 0.6 %collective-permute-start.7 = (f32[5,72,128]{2,1,0:T(8,128)S(1)}, f32[5,72,128]{2,1,0:T(8,128)S(1)}, u32[]{:S(2)}, u32[]{:S(2)}) collective-permute-start(f32[5,72,128]{2,1,0:T(8,128)S(1)} %get-tuple-element.36), channel_id=1, source_target_pairs={{0,4},{4,0},{1,5},{5,1},{2,6},{6,2},{3,7},{7,3},{8,12},{12,8},{9,1... | collective-permute-start | bytes 552968 | tf_op jit(solution)/shard_map/ppermute | solution.py:682
  25.4 0.2 collective-permute-done.10
  25.6 0.0 collective-permute-done.8
  25.6 1.1 %collective-permute-done.9 = f32[8,128]{1,0:T(8,128)S(1)} collective-permute-done((f32[8,128]{1,0:T(8,128)S(1)}, f32[8,128]{1,0:T(8,128)S(1)}, u32[]{:S(2)}, u32[]{:S(2)}) %collective-permute-start.9) | collective-permute-done | bytes 4128 | tf_op jit(solution)/shard_map/ppermute | solution.py:616
  26.7 4.0 %collective-permute-done.7.refs_2_ = f32[5,72,128]{2,1,0:T(8,128)S(1)} collective-permute-done((f32[5,72,128]{2,1,0:T(8,128)S(1)}, f32[5,72,128]{2,1,0:T(8,128)S(1)}, u32[]{:S(2)}, u32[]{:S(2)}) %collective-permute-start.7) | collective-permute-done | bytes 184352 | tf_op jit(solution)/shard_map/ppermute | solution.py:682
  30.7 0.0 collective-permute-done.2.refs_1_
  30.7 0.0 copy-start
  30.7 0.0 copy-start.1
  30.7 10.7 %sections.1 = (f32[5,8,48,128]{3,2,1,0:T(8,128)S(1)}, f32[8,48,128]{2,1,0:T(8,128)S(1)}, f32[8,48,128]{2,1,0:T(8,128)S(1)}) custom-call(f32[5,8,56,128]{3,2,1,0:T(8,128)S(1)} %get-tuple-element.29.wide_ref.refs_0_, f32[5,6,48,128]{3,2,1,0:T(8,128)S(1)} %collective-permute-done.2.refs_1_, f32[5,72,128]{2,1,0:T(8,128)S(1)} %collective-permute-done.7.refs_2_, ...), custom_call_target="tpu_custom_call" | custom-call | tf_op jit(solution)/shard_map/sections/pallas_call | solution.py:445
  41.4 0.0 copy-done
  41.4 0.0 copy-done.1
  41.4 1.7 %shard_map.68 = (f32[256,128]{1,0:T(8,128)S(1)}, f32[256,128]{1,0:T(8,128)S(1)}) custom-call(f32[8,48,128]{2,1,0:T(8,128)S(1)} %get-tuple-element.40.rho_ref, f32[8,48,128]{2,1,0:T(8,128)S(1)} %get-tuple-element.41.heat_ref, f32[4,256]{1,0:T(4,128)S(1)} %copy-done.1, s32[8,256]{1,0:T(8,128)S(1)} %copy-done), custom_call_target="tpu_custom_call" | custom-call | tf_op jit(solution)/shard_map/pallas_call | solution.py:585
  43.1 0.6 %collective-permute-start.11 = (f32[4,4,16,128]{3,2,1,0:T(8,128)S(1)}, f32[4,4,16,128]{3,2,1,0:T(8,128)S(1)}, u32[]{:S(2)}, u32[]{:S(2)}) collective-permute-start(f32[4,4,16,128]{3,2,1,0:T(8,128)S(1)} %bitcast.18), channel_id=1, source_target_pairs={{0,4},{4,0},{1,5},{5,1},{2,6},{6,2},{3,7},{7,3},{8,12},{12,8},{9,1... | collective-permute-start | bytes 393224 | tf_op jit(solution)/shard_map/ppermute | solution.py:666
  43.7 1.7 %shard_map.69 = (f32[256,128]{1,0:T(8,128)S(1)}, f32[256,128]{1,0:T(8,128)S(1)}) custom-call(f32[8,48,128]{2,1,0:T(8,128)S(1)} %get-tuple-element.40.rho_ref, f32[8,48,128]{2,1,0:T(8,128)S(1)} %get-tuple-element.41.heat_ref, f32[4,256]{1,0:T(4,128)S(1)} %copy-done.1, s32[8,256]{1,0:T(8,128)S(1)} %copy-done), custom_call_target="tpu_custom_call" | custom-call | tf_op jit(solution)/shard_map/pallas_call | solution.py:585
  45.4 1.7 %shard_map.70 = (f32[256,128]{1,0:T(8,128)S(1)}, f32[256,128]{1,0:T(8,128)S(1)}) custom-call(f32[8,48,128]{2,1,0:T(8,128)S(1)} %get-tuple-element.40.rho_ref, f32[8,48,128]{2,1,0:T(8,128)S(1)} %get-tuple-element.41.heat_ref, f32[4,256]{1,0:T(4,128)S(1)} %copy-done.1, s32[8,256]{1,0:T(8,128)S(1)} %copy-done), custom_call_target="tpu_custom_call" | custom-call | tf_op jit(solution)/shard_map/pallas_call | solution.py:585
  47.2 1.6 %collective-permute-start.12 = (f32[4,4,16,128]{3,2,1,0:T(8,128)S(1)}, f32[4,4,16,128]{3,2,1,0:T(8,128)S(1)}, u32[]{:S(2)}, u32[]{:S(2)}) collective-permute-start(f32[4,4,16,128]{3,2,1,0:T(8,128)S(1)} %bitcast.20), channel_id=1, source_target_pairs={{0,4},{4,0},{1,5},{5,1},{2,6},{6,2},{3,7},{7,3},{8,12},{12,8},{9,1... | collective-permute-start | bytes 393224 | tf_op jit(solution)/shard_map/ppermute | solution.py:666
  48.7 0.5 collective-permute-start.13
  49.2 0.9 %copy.7 = f32[5,8,48,128]{3,2,1,0:T(8,128)} copy(f32[5,8,48,128]{3,2,1,0:T(8,128)S(1)} %get-tuple-element.48) | data formatting | bytes 1966080
  50.2 0.0 collective-permute-done.11
  50.2 2.2 %collective-permute-done.12 = f32[4,4,16,128]{3,2,1,0:T(8,128)S(1)} collective-permute-done((f32[4,4,16,128]{3,2,1,0:T(8,128)S(1)}, f32[4,4,16,128]{3,2,1,0:T(8,128)S(1)}, u32[]{:S(2)}, u32[]{:S(2)}) %collective-permute-start.12) | collective-permute-done | bytes 131104 | tf_op jit(solution)/shard_map/ppermute | solution.py:666
  52.4 1.4 %collective-permute-done.13 = f32[4,4,16,128]{3,2,1,0:T(8,128)S(1)} collective-permute-done((f32[4,4,16,128]{3,2,1,0:T(8,128)S(1)}, f32[4,4,16,128]{3,2,1,0:T(8,128)S(1)}, u32[]{:S(2)}, u32[]{:S(2)}) %collective-permute-start.13) | collective-permute-done | bytes 131104 | tf_op jit(solution)/shard_map/ppermute | solution.py:666
  53.9 0.7 %pad_maximum_fusion = f32[4,3,48,128]{3,2,1,0:T(8,128)} fusion(f32[4,3,16,128]{3,2,1,0:T(8,128)S(1)} %fusion.1, f32[4,3,16,128]{3,2,1,0:T(8,128)S(1)} %fusion.3, f32[4,3,16,128]{3,2,1,0:T(8,128)S(1)} %fusion.5), kind=kLoop, calls=%fused_computation | loop fusion | flops 147456 | bytes 589824 | tf_op jit(solution)/shard_map/concatenate | solution.py:672
  (12 shorter events, 0.2 us)
Async XLA Ops:
  2.1 28.6 %collective-permute-start.2 = (f32[5,6,48,128]{3,2,1,0:T(8,128)S(1)}, f32[5,6,48,128]{3,2,1,0:T(8,128)S(1)}, u32[]{:S(2)}, u32[]{:S(2)}) collective-permute-start(f32[5,6,48,128]{3,2,1,0:T(8,128)S(1)} %get-tuple-element.30), channel_id=1, source_target_pairs={{0,4},{4,0},{1,5},{5,1},{2,6},{6,2},{3,7},{7,3},{8,12},{12,8},{9,1... | collective-permute-start | bytes 2211848 | tf_op jit(solution)/shard_map/ppermute | solution.py:682
  5.1 4.3 %collective-permute-start = (f32[128,128]{1,0:T(8,128)S(1)}, f32[128,128]{1,0:T(8,128)S(1)}, u32[]{:S(2)}, u32[]{:S(2)}) collective-permute-start(f32[128,128]{1,0:T(8,128)S(1)} %get-tuple-element.26), channel_id=1, source_target_pairs={{0,8},{16,24},{8,0},{24,16},{1,9},{17,25},{9,1},{25,17},{2,10},{18... | collective-permute-start | bytes 196616 | tf_op jit(solution)/shard_map/ppermute | solution.py:685
  6.7 2.7 %collective-permute-start.1 = (f32[128,128]{1,0:T(8,128)S(1)}, f32[128,128]{1,0:T(8,128)S(1)}, u32[]{:S(2)}, u32[]{:S(2)}) collective-permute-start(f32[128,128]{1,0:T(8,128)S(1)} %get-tuple-element.27), channel_id=1, source_target_pairs={{8,16},{16,8},{9,17},{17,9},{10,18},{18,10},{11,19},{19,11},{12,20... | collective-permute-start | bytes 196616 | tf_op jit(solution)/shard_map/ppermute | solution.py:686
  10.5 10.5 %collective-permute-start.3 = (f32[5,56,128]{2,1,0:T(8,128)S(1)}, f32[5,56,128]{2,1,0:T(8,128)S(1)}, u32[]{:S(2)}, u32[]{:S(2)}) collective-permute-start(f32[5,56,128]{2,1,0:T(8,128)S(1)} %get-tuple-element.31.first_ref), channel_id=1, source_target_pairs={{0,1},{2,3},{1,0},{3,2},{4,5},{6,7},{5,4},{7,6},{8,9},{10,11},{9,8... | collective-permute-start | bytes 430088 | tf_op jit(solution)/shard_map/ppermute | solution.py:689
  10.6 10.4 %collective-permute-start.4 = (f32[5,56,128]{2,1,0:T(8,128)S(1)}, f32[5,56,128]{2,1,0:T(8,128)S(1)}, u32[]{:S(2)}, u32[]{:S(2)}) collective-permute-start(f32[5,56,128]{2,1,0:T(8,128)S(1)} %get-tuple-element.32.second_ref), channel_id=1, source_target_pairs={{1,2},{3,0},{2,1},{0,3},{5,6},{7,4},{6,5},{4,7},{9,10},{11,8},{10,... | collective-permute-start | bytes 430088 | tf_op jit(solution)/shard_map/ppermute | solution.py:690
  12.2 7.6 %collective-permute-start.5 = (f32[8,128]{1,0:T(8,128)S(1)}, f32[8,128]{1,0:T(8,128)S(1)}, u32[]{:S(2)}, u32[]{:S(2)}) collective-permute-start(f32[8,128]{1,0:T(8,128)S(1)} %get-tuple-element.33), channel_id=1, source_target_pairs={{0,16},{8,24},{16,0},{24,8},{1,17},{9,25},{17,1},{25,9},{2,18},{10... | collective-permute-start | bytes 12296 | tf_op jit(solution)/shard_map/ppermute | solution.py:602
  19.9 1.2 %collective-permute-start.6 = (f32[8,128]{1,0:T(8,128)S(1)}, f32[8,128]{1,0:T(8,128)S(1)}, u32[]{:S(2)}, u32[]{:S(2)}) collective-permute-start(f32[8,128]{1,0:T(8,128)S(1)} %max.15), channel_id=1, source_target_pairs={{0,1},{1,0},{2,3},{3,2},{4,5},{5,4},{6,7},{7,6},{8,9},{9,8},{10,11... | collective-permute-start | bytes 12296 | tf_op jit(solution)/shard_map/ppermute | solution.py:602
  21.0 4.6 %collective-permute-start.10 = (f32[8,128]{1,0:T(8,128)S(1)}, f32[8,128]{1,0:T(8,128)S(1)}, u32[]{:S(2)}, u32[]{:S(2)}) collective-permute-start(f32[8,128]{1,0:T(8,128)S(1)} %max.16), channel_id=1, source_target_pairs={{0,6},{1,7},{2,4},{3,5},{4,2},{5,3},{6,0},{7,1},{8,14},{9,15},{10,... | collective-permute-start | bytes 12296 | tf_op jit(solution)/shard_map/ppermute | solution.py:616
  21.6 4.0 %collective-permute-start.8 = (f32[8,128]{1,0:T(8,128)S(1)}, f32[8,128]{1,0:T(8,128)S(1)}, u32[]{:S(2)}, u32[]{:S(2)}) collective-permute-start(f32[8,128]{1,0:T(8,128)S(1)} %max.16), channel_id=1, source_target_pairs={{0,4},{1,5},{2,6},{3,7},{4,0},{5,1},{6,2},{7,3},{8,12},{9,13},{10,... | collective-permute-start | bytes 12296 | tf_op jit(solution)/shard_map/ppermute | solution.py:616
  23.1 3.6 %collective-permute-start.9 = (f32[8,128]{1,0:T(8,128)S(1)}, f32[8,128]{1,0:T(8,128)S(1)}, u32[]{:S(2)}, u32[]{:S(2)}) collective-permute-start(f32[8,128]{1,0:T(8,128)S(1)} %max.16), channel_id=1, source_target_pairs={{0,2},{1,3},{2,0},{3,1},{4,6},{5,7},{6,4},{7,5},{8,10},{9,11},{10,... | collective-permute-start | bytes 12296 | tf_op jit(solution)/shard_map/ppermute | solution.py:616
  24.8 5.9 %collective-permute-start.7 = (f32[5,72,128]{2,1,0:T(8,128)S(1)}, f32[5,72,128]{2,1,0:T(8,128)S(1)}, u32[]{:S(2)}, u32[]{:S(2)}) collective-permute-start(f32[5,72,128]{2,1,0:T(8,128)S(1)} %get-tuple-element.36), channel_id=1, source_target_pairs={{0,4},{4,0},{1,5},{5,1},{2,6},{6,2},{3,7},{7,3},{8,12},{12,8},{9,1... | collective-permute-start | bytes 552968 | tf_op jit(solution)/shard_map/ppermute | solution.py:682
  30.7 10.7 %copy-start = (s32[8,256]{1,0:T(8,128)S(1)}, s32[8,256]{1,0:T(8,128)}, u32[]{:S(2)}) copy-start(s32[8,256]{1,0:T(8,128)} %index_ref.5) | copy-start | bytes 24580
  30.7 10.7 %copy-start.1 = (f32[4,256]{1,0:T(4,128)S(1)}, f32[4,256]{1,0:T(4,128)}, u32[]{:S(2)}) copy-start(f32[4,256]{1,0:T(4,128)} %palette_ref.5) | copy-start | bytes 12292
  43.1 7.1 %collective-permute-start.11 = (f32[4,4,16,128]{3,2,1,0:T(8,128)S(1)}, f32[4,4,16,128]{3,2,1,0:T(8,128)S(1)}, u32[]{:S(2)}, u32[]{:S(2)}) collective-permute-start(f32[4,4,16,128]{3,2,1,0:T(8,128)S(1)} %bitcast.18), channel_id=1, source_target_pairs={{0,4},{4,0},{1,5},{5,1},{2,6},{6,2},{3,7},{7,3},{8,12},{12,8},{9,1... | collective-permute-start | bytes 393224 | tf_op jit(solution)/shard_map/ppermute | solution.py:666
  47.2 5.2 %collective-permute-start.12 = (f32[4,4,16,128]{3,2,1,0:T(8,128)S(1)}, f32[4,4,16,128]{3,2,1,0:T(8,128)S(1)}, u32[]{:S(2)}, u32[]{:S(2)}) collective-permute-start(f32[4,4,16,128]{3,2,1,0:T(8,128)S(1)} %bitcast.20), channel_id=1, source_target_pairs={{0,4},{4,0},{1,5},{5,1},{2,6},{6,2},{3,7},{7,3},{8,12},{12,8},{9,1... | collective-permute-start | bytes 393224 | tf_op jit(solution)/shard_map/ppermute | solution.py:666
  48.7 5.1 %collective-permute-start.13 = (f32[4,4,16,128]{3,2,1,0:T(8,128)S(1)}, f32[4,4,16,128]{3,2,1,0:T(8,128)S(1)}, u32[]{:S(2)}, u32[]{:S(2)}) collective-permute-start(f32[4,4,16,128]{3,2,1,0:T(8,128)S(1)} %bitcast.19), channel_id=1, source_target_pairs={{0,4},{4,0},{1,5},{5,1},{2,6},{6,2},{3,7},{7,3},{8,12},{12,8},{9,1... | collective-permute-start | bytes 393224 | tf_op jit(solution)/shard_map/ppermute | solution.py:666
